TPU v7x, 256 devices: a whole 4x4x8 slice. The times are simulated.
256 devices in a mesh: seq: 32 (over z, x), hg: 8 (over y, core).
Axes of the slice: x: 4, y: 4, z: 8, core: 2. Of those that a mesh axis runs over, the one named last changes fastest.
Arguments:
- conv_input: bfloat16 [65536, 4096], P('seq', 'hg'), may hold values from -6 to 6
- grad_output: bfloat16 [65536, 4096], P('seq', 'hg'), may hold values from -0.015625 to 0.015625
- inject: bfloat16 [65536, 128], P('seq'), may hold values from -6 to 6
- readout: bfloat16 [65536, 128], P('seq'), may hold values from -6 to 6
- conv_weight: bfloat16 [4, 4096], P(None, 'hg'), may hold values from -3 to 3
- decay_codes: int32 [64, 256], P('hg', 'seq'), may hold values from 0 to 1000, as said below
Outputs:
- grad_input: float32 [65536, 4096], P('seq', 'hg')
- grad_inject: float32 [65536, 128], P('seq')
- grad_readout: float32 [65536, 128], P('seq')
Inputs may be any that keep to these rules, and one draw needn't show every extreme that they name: The decay of every step of span c in head h is 1 - 1e-6 decay_codes[h, c].
All inputs are finite; a program needn't handle non-finite values.
Results may differ from a plain program's by a relative error of at most 0.0029.
Values may be sent and summed in bfloat16 or wider, within the bound.
No kernel may reach another device: no remote copies, remote signals or barrier semaphores. Data moves between devices by JAX's collectives and lax.ppermute only.
A program may use at most 128 MiB of HBM per device.

v0:
```python
import jax
import jax.numpy as jnp
from jax import lax
from jax.sharding import PartitionSpec as P

precise = lax.Precision.HIGHEST


def passed_along(array, axis, by):
    length = lax.axis_size(axis)
    pairs = [(i, i + by) for i in range(length) if 0 <= i + by < length]
    return lax.ppermute(array, axis, pairs)


def causal_conv(padded, weights, length):
    summed = weights[0] * padded[0:length].astype(jnp.float32)
    for offset in range(1, 4):
        summed = summed + weights[offset] * padded[offset : offset + length].astype(jnp.float32)
    return summed


def silu_slope(preact):
    squashed = jax.nn.sigmoid(preact)
    return squashed * (1.0 + preact * (1.0 - squashed))


def span_terms(
    block_act, block_grad, block_inject, block_readout, block_rates, state_before, grad_after
):
    span_len = block_act.shape[0]
    places = jnp.arange(span_len).astype(jnp.float32)
    spread = places[:, None] - places[None, :]
    decay_mask = jnp.where(
        spread[None] >= 0.0,
        jnp.exp(jnp.maximum(spread, 0.0)[None] * block_rates[:, None, None]),
        0.0,
    )
    products = jnp.einsum(
        "jn,in->ji", block_readout, block_inject, preferred_element_type=jnp.float32
    )
    mixing = (products[None] * decay_mask).astype(jnp.bfloat16)
    grad_act = jnp.einsum("hji,jhp->ihp", mixing, block_grad, preferred_element_type=jnp.float32)
    pair_weights = (
        jnp.einsum("ihp,jhp->hij", block_grad, block_act, preferred_element_type=jnp.float32)
        * decay_mask
    ).astype(jnp.bfloat16)
    grad_readout = jnp.einsum(
        "hij,jn->in", pair_weights, block_inject, preferred_element_type=jnp.float32
    )
    grad_inject = jnp.einsum(
        "hij,in->jn", pair_weights, block_readout, preferred_element_type=jnp.float32
    )
    tail_decay = jnp.exp((span_len - 1.0 - places)[:, None] * block_rates[None, :])
    lead_decay = jnp.exp((places + 1.0)[:, None] * block_rates[None, :])
    grad_act = (
        grad_act
        + jnp.einsum("qn,hpn->qhp", block_inject.astype(jnp.float32), grad_after, precision=precise)
        * tail_decay[:, :, None]
    )
    grad_inject = grad_inject + jnp.einsum(
        "qhp,hpn->qn",
        block_act.astype(jnp.float32) * tail_decay[:, :, None],
        grad_after,
        precision=precise,
    )
    grad_readout = grad_readout + jnp.einsum(
        "qhp,hpn->qn",
        block_grad.astype(jnp.float32) * lead_decay[:, :, None],
        state_before,
        precision=precise,
    )
    return (grad_act, grad_inject, grad_readout)


def span_apply(block_items):
    return span_terms(*block_items)


def body(conv_input, grad_output, inject, readout, conv_weight, decay_codes):
    tokens, channels = conv_input.shape
    head_count, spans = decay_codes.shape
    span_len = tokens // spans
    head_dim = channels // head_count
    states = inject.shape[1]
    weights = conv_weight.astype(jnp.float32)
    earlier_rows = passed_along(conv_input[tokens - 3 :], "seq", 1)
    padded = jnp.concatenate([earlier_rows, conv_input], axis=0)
    preact = causal_conv(padded, weights, tokens)
    activated = jax.nn.silu(preact).astype(jnp.bfloat16)
    log_rates = jnp.log1p(-decay_codes.astype(jnp.float32) * 1e-06)
    rate_blocks = log_rates.T
    act_blocks = activated.reshape(spans, span_len, head_count, head_dim)
    grad_blocks = grad_output.reshape(spans, span_len, head_count, head_dim)
    inject_blocks = inject.reshape(spans, span_len, states)
    readout_blocks = readout.reshape(spans, span_len, states)
    places = jnp.arange(span_len).astype(jnp.float32)
    tail_decay = jnp.exp((span_len - 1.0 - places)[None, :, None] * rate_blocks[:, None, :])
    lead_decay = jnp.exp((places + 1.0)[None, :, None] * rate_blocks[:, None, :])
    fresh_states = jnp.einsum(
        "kqhp,kqn->khpn",
        act_blocks.astype(jnp.float32) * tail_decay[..., None],
        inject_blocks.astype(jnp.float32),
        precision=precise,
    )
    fresh_grads = jnp.einsum(
        "kqhp,kqn->khpn",
        grad_blocks.astype(jnp.float32) * lead_decay[..., None],
        readout_blocks.astype(jnp.float32),
        precision=precise,
    )
    span_gain = jnp.exp(span_len * rate_blocks)

    def local_fold(carried, members):
        gain_now, fresh_now = members
        return (gain_now[:, None, None] * carried + fresh_now, carried)

    empty_state = jnp.zeros((head_count, head_dim, states), jnp.float32)
    own_state, local_before = lax.scan(local_fold, empty_state, (span_gain, fresh_states))
    own_grad, local_after = lax.scan(
        local_fold, empty_state, (span_gain, fresh_grads), reverse=True
    )
    own_decay = span_len * jnp.sum(log_rates, axis=1)
    device_gain = jnp.exp(own_decay)

    def push_state(step_index, incoming):
        return passed_along(device_gain[:, None, None] * incoming + own_state, "seq", 1)

    def push_grad(step_index, incoming):
        return passed_along(device_gain[:, None, None] * incoming + own_grad, "seq", -1)

    entering = lax.fori_loop(0, lax.axis_size("seq") - 1, push_state, empty_state)
    arriving = lax.fori_loop(0, lax.axis_size("seq") - 1, push_grad, empty_state)
    running_logs = jnp.cumsum(rate_blocks, axis=0)
    prior_logs = span_len * (running_logs - rate_blocks)
    later_logs = span_len * (running_logs[-1][None] - running_logs)
    state_before = local_before + jnp.exp(prior_logs)[:, :, None, None] * entering[None]
    grad_after = local_after + jnp.exp(later_logs)[:, :, None, None] * arriving[None]
    grad_act, grad_inject, grad_readout = lax.map(
        span_apply,
        (
            act_blocks,
            grad_blocks,
            inject_blocks,
            readout_blocks,
            rate_blocks,
            state_before,
            grad_after,
        ),
    )
    grad_pre = grad_act.reshape(tokens, channels) * silu_slope(preact)
    later_rows = passed_along(grad_pre[:3], "seq", -1)
    padded_grad = jnp.concatenate([grad_pre, later_rows], axis=0)
    grad_input = weights[0] * padded_grad[3 : 3 + tokens]
    for offset in range(1, 4):
        grad_input = grad_input + weights[offset] * padded_grad[3 - offset : 3 - offset + tokens]
    grad_inject, grad_readout = lax.psum(
        (grad_inject.reshape(tokens, states), grad_readout.reshape(tokens, states)), "hg"
    )
    return (grad_input, grad_inject, grad_readout)


def solution(mesh):
    return jax.shard_map(
        body,
        mesh=mesh,
        in_specs=(
            P("seq", "hg"),
            P("seq", "hg"),
            P("seq", None),
            P("seq", None),
            P(None, "hg"),
            P("hg", "seq"),
        ),
        out_specs=(P("seq", "hg"), P("seq", None), P("seq", None)),
        check_vma=False,
    )
```

profile of v0, /device:TPU:7, one launch (start us, length us, event | category | flops | bytes accessed | tf_op | source)
XLA Modules:
  0.0 1116.1 jit_solution(9426463784251113668)
XLA Ops:
  26.5 14.4 %while.67 = (s32[]{:T(128)}, f32[8,64,128]{2,1,0:T(8,128)S(1)}, f32[8,8,64,128]{3,2,1,0:T(8,128)}, f32[8,8]{1,0:T(8,128)S(1)}, f32[8,8,64,128]{3,2,1,0:T(8,128)}, /*index=5*/s32[]{:T(128)}, s32[]{:T(128)}, s32[]{:T(128)}) while((s32[]{:T(128)}, f32[8,64,128]{2,1,0:T(8,128)S(1)}, f32[8,8,64,128]{3,2,1,0:T(8,128)}, ...), condition=%wide.region_7.8_spmd.clone, body=%wide.region_6.7_spmd.clone.sunk | while | flops 262148 | bytes 1310944 | solution.py:119
  59.0 8.9 while.68
  69.3 316.3 %while.64 = (s32[]{:T(128)}, f32[8,64,128]{2,1,0:T(8,128)S(1)}, f32[8]{0:T(128)S(1)}, f32[8,64,128]{2,1,0:T(8,128)S(1)}, s32[]{:T(128)}) while((s32[]{:T(128)}, f32[8,64,128]{2,1,0:T(8,128)S(1)}, f32[8]{0:T(128)S(1)}, f32[8,64,128]{2,1,0:T(8,128)S(1)}, s32[]{:T(128)}) %tuple.125), condition=%wide.region_9.10_spmd, body=%wide.region_8.9_spmd.sunk | while | flops 131074 | bytes 1835141 | solution.py:132
  71.3 8.9 collective-permute-done
  139.1 8.6 collective-permute-done
  149.7 9.6 collective-permute-done
  161.3 9.7 collective-permute-done
  173.0 8.8 collective-permute-done
  240.6 8.7 collective-permute-done
  251.4 9.9 collective-permute-done
  263.3 9.6 collective-permute-done
  274.9 8.6 collective-permute-done
  342.4 8.8 collective-permute-done
  353.2 10.1 collective-permute-done
  365.4 9.6 collective-permute-done
  376.9 8.6 collective-permute-done
  385.6 323.2 %while.65 = (s32[]{:T(128)}, f32[8,64,128]{2,1,0:T(8,128)S(1)}, f32[8]{0:T(128)S(1)}, f32[8,64,128]{2,1,0:T(8,128)S(1)}, s32[]{:T(128)}) while((s32[]{:T(128)}, f32[8,64,128]{2,1,0:T(8,128)S(1)}, f32[8]{0:T(128)S(1)}, f32[8,64,128]{2,1,0:T(8,128)S(1)}, s32[]{:T(128)}) %tuple.137), condition=%wide.region_5.6_spmd, body=%wide.region_4.5_spmd.sunk | while | flops 131074 | bytes 1835141 | solution.py:131
  511.5 9.0 collective-permute-start.1
  627.7 8.0 collective-permute-start.1
  639.1 9.1 collective-permute-start.1
  653.0 8.3 collective-permute-start.1
  712.7 199.3 %while.66 = (s32[]{:T(128)}, f32[8,256,8,64]{1,0,3,2:T(8,128)}, f32[8,256,128]{2,1,0:T(8,128)}, f32[8,256,128]{2,1,0:T(8,128)}, bf16[8,256,8,64]{1,3,2,0:T(8,128...) while((s32[]{:T(128)}, f32[8,256,8,64]{1,0,3,2:T(8,128)}, ...), condition=%wide.region_12.13_spmd, body=%wide.region_10.12_spmd.sunk | while | flops 794825728 | bytes 8837425 | solution.py:138
  724.9 12.7 %dynamic_update_slice.37 = f32[8,256,8,64]{1,0,3,2:T(8,128)} dynamic-update-slice(f32[8,256,8,64]{1,0,3,2:T(8,128)} %get-tuple-element.663, f32[1,256,8,64]{1,0,3,2:T(1,128)S(1)} %copy.39, s32[]{:T(128)S(6)} %copy.79, s32[]{:T(128)} %constant.99.clone.1..sunk, s32[]{:T(128)} %constant.99.clone.1..sunk, s32[]{:T(128)} %constant.99.clone.1..sunk) | dynamic-update-slice | bytes 1048580 | tf_op jit(solution)/shard_map/while/body/jit(dynamic_update_index_in_dim)/dynamic_update_slice | solution.py:138
  749.9 12.7 %dynamic_update_slice.37 = f32[8,256,8,64]{1,0,3,2:T(8,128)} dynamic-update-slice(f32[8,256,8,64]{1,0,3,2:T(8,128)} %get-tuple-element.663, f32[1,256,8,64]{1,0,3,2:T(1,128)S(1)} %copy.39, s32[]{:T(128)S(6)} %copy.79, s32[]{:T(128)} %constant.99.clone.1..sunk, s32[]{:T(128)} %constant.99.clone.1..sunk, s32[]{:T(128)} %constant.99.clone.1..sunk) | dynamic-update-slice | bytes 1048580 | tf_op jit(solution)/shard_map/while/body/jit(dynamic_update_index_in_dim)/dynamic_update_slice | solution.py:138
  774.8 12.7 %dynamic_update_slice.37 = f32[8,256,8,64]{1,0,3,2:T(8,128)} dynamic-update-slice(f32[8,256,8,64]{1,0,3,2:T(8,128)} %get-tuple-element.663, f32[1,256,8,64]{1,0,3,2:T(1,128)S(1)} %copy.39, s32[]{:T(128)S(6)} %copy.79, s32[]{:T(128)} %constant.99.clone.1..sunk, s32[]{:T(128)} %constant.99.clone.1..sunk, s32[]{:T(128)} %constant.99.clone.1..sunk) | dynamic-update-slice | bytes 1048580 | tf_op jit(solution)/shard_map/while/body/jit(dynamic_update_index_in_dim)/dynamic_update_slice | solution.py:138
  799.7 12.7 %dynamic_update_slice.37 = f32[8,256,8,64]{1,0,3,2:T(8,128)} dynamic-update-slice(f32[8,256,8,64]{1,0,3,2:T(8,128)} %get-tuple-element.663, f32[1,256,8,64]{1,0,3,2:T(1,128)S(1)} %copy.39, s32[]{:T(128)S(6)} %copy.79, s32[]{:T(128)} %constant.99.clone.1..sunk, s32[]{:T(128)} %constant.99.clone.1..sunk, s32[]{:T(128)} %constant.99.clone.1..sunk) | dynamic-update-slice | bytes 1048580 | tf_op jit(solution)/shard_map/while/body/jit(dynamic_update_index_in_dim)/dynamic_update_slice | solution.py:138
  824.6 12.7 %dynamic_update_slice.37 = f32[8,256,8,64]{1,0,3,2:T(8,128)} dynamic-update-slice(f32[8,256,8,64]{1,0,3,2:T(8,128)} %get-tuple-element.663, f32[1,256,8,64]{1,0,3,2:T(1,128)S(1)} %copy.39, s32[]{:T(128)S(6)} %copy.79, s32[]{:T(128)} %constant.99.clone.1..sunk, s32[]{:T(128)} %constant.99.clone.1..sunk, s32[]{:T(128)} %constant.99.clone.1..sunk) | dynamic-update-slice | bytes 1048580 | tf_op jit(solution)/shard_map/while/body/jit(dynamic_update_index_in_dim)/dynamic_update_slice | solution.py:138
  849.5 12.7 %dynamic_update_slice.37 = f32[8,256,8,64]{1,0,3,2:T(8,128)} dynamic-update-slice(f32[8,256,8,64]{1,0,3,2:T(8,128)} %get-tuple-element.663, f32[1,256,8,64]{1,0,3,2:T(1,128)S(1)} %copy.39, s32[]{:T(128)S(6)} %copy.79, s32[]{:T(128)} %constant.99.clone.1..sunk, s32[]{:T(128)} %constant.99.clone.1..sunk, s32[]{:T(128)} %constant.99.clone.1..sunk) | dynamic-update-slice | bytes 1048580 | tf_op jit(solution)/shard_map/while/body/jit(dynamic_update_index_in_dim)/dynamic_update_slice | solution.py:138
  874.4 12.7 %dynamic_update_slice.37 = f32[8,256,8,64]{1,0,3,2:T(8,128)} dynamic-update-slice(f32[8,256,8,64]{1,0,3,2:T(8,128)} %get-tuple-element.663, f32[1,256,8,64]{1,0,3,2:T(1,128)S(1)} %copy.39, s32[]{:T(128)S(6)} %copy.79, s32[]{:T(128)} %constant.99.clone.1..sunk, s32[]{:T(128)} %constant.99.clone.1..sunk, s32[]{:T(128)} %constant.99.clone.1..sunk) | dynamic-update-slice | bytes 1048580 | tf_op jit(solution)/shard_map/while/body/jit(dynamic_update_index_in_dim)/dynamic_update_slice | solution.py:138
  899.4 12.7 %dynamic_update_slice.37 = f32[8,256,8,64]{1,0,3,2:T(8,128)} dynamic-update-slice(f32[8,256,8,64]{1,0,3,2:T(8,128)} %get-tuple-element.663, f32[1,256,8,64]{1,0,3,2:T(1,128)S(1)} %copy.39, s32[]{:T(128)S(6)} %copy.79, s32[]{:T(128)} %constant.99.clone.1..sunk, s32[]{:T(128)} %constant.99.clone.1..sunk, s32[]{:T(128)} %constant.99.clone.1..sunk) | dynamic-update-slice | bytes 1048580 | tf_op jit(solution)/shard_map/while/body/jit(dynamic_update_index_in_dim)/dynamic_update_slice | solution.py:138
  925.1 8.7 collective-permute-done.3
  946.0 158.7 %all-reduce.3.cloned.1.call-done = (f32[2048,128]{1,0:T(8,128)}, f32[2048,128]{1,0:T(8,128)}) async-done(((f32[2048,128]{1,0:T(8,128)}, f32[2048,128]{1,0:T(8,128)}), (f32[2048,128]{1,0:T(8,128)}, f32[2048,128]{1,0:T(8,128)})) %all-reduce.3.cloned.1.call-update) | async-done | bytes 2097168 | tf_op jit(solution)/shard_map/psum | solution.py:156
  (389 shorter events, 676.9 us)
Async XLA Ops:
  7.2 1097.5 %all-reduce.3.cloned.1.call-start = ((), (), s32[]{:S(2)}) async-start(), calls=%async_computation | async-start | bytes 4194304 | tf_op jit(solution)/shard_map/psum | solution.py:156
  8.1 37.7 %collective-permute-start.2 = (bf16[3,512]{0,1:T(8,128)(2,1)S(1)}, bf16[3,512]{0,1:T(8,128)(2,1)S(1)}, u32[]{:S(2)}, u32[]{:S(2)}) collective-permute-start(bf16[3,512]{0,1:T(8,128)(2,1)S(1)} %copy.17), channel_id=1, source_target_pairs={{0,8},{8,16},{16,24},{24,32},{32,40},{40,48},{48,56},{56,64},{64,7... | collective-permute-start | bytes 9224 | tf_op jit(solution)/shard_map/ppermute | solution.py:12
  69.4 10.9 collective-permute-start
  137.1 10.5 collective-permute-start
  147.7 11.6 %collective-permute-start = (f32[8,64,128]{2,1,0:T(8,128)S(1)}, f32[8,64,128]{2,1,0:T(8,128)S(1)}, u32[]{:S(2)}, u32[]{:S(2)}) collective-permute-start(f32[8,64,128]{2,1,0:T(8,128)S(1)} %multiply_add_fusion.8), channel_id=1, source_target_pairs={{8,0},{16,8},{24,16},{32,24},{40,32},{48,40},{56,48},{64,56},{72,6... | collective-permute-start | bytes 786440 | tf_op jit(solution)/shard_map/while/body/eval_jaxpr/ppermute | solution.py:12
  159.4 11.6 %collective-permute-start = (f32[8,64,128]{2,1,0:T(8,128)S(1)}, f32[8,64,128]{2,1,0:T(8,128)S(1)}, u32[]{:S(2)}, u32[]{:S(2)}) collective-permute-start(f32[8,64,128]{2,1,0:T(8,128)S(1)} %multiply_add_fusion.8), channel_id=1, source_target_pairs={{8,0},{16,8},{24,16},{32,24},{40,32},{48,40},{56,48},{64,56},{72,6... | collective-permute-start | bytes 786440 | tf_op jit(solution)/shard_map/while/body/eval_jaxpr/ppermute | solution.py:12
  171.1 10.7 collective-permute-start
  238.7 10.7 collective-permute-start
  249.5 11.8 %collective-permute-start = (f32[8,64,128]{2,1,0:T(8,128)S(1)}, f32[8,64,128]{2,1,0:T(8,128)S(1)}, u32[]{:S(2)}, u32[]{:S(2)}) collective-permute-start(f32[8,64,128]{2,1,0:T(8,128)S(1)} %multiply_add_fusion.8), channel_id=1, source_target_pairs={{8,0},{16,8},{24,16},{32,24},{40,32},{48,40},{56,48},{64,56},{72,6... | collective-permute-start | bytes 786440 | tf_op jit(solution)/shard_map/while/body/eval_jaxpr/ppermute | solution.py:12
  261.3 11.5 %collective-permute-start = (f32[8,64,128]{2,1,0:T(8,128)S(1)}, f32[8,64,128]{2,1,0:T(8,128)S(1)}, u32[]{:S(2)}, u32[]{:S(2)}) collective-permute-start(f32[8,64,128]{2,1,0:T(8,128)S(1)} %multiply_add_fusion.8), channel_id=1, source_target_pairs={{8,0},{16,8},{24,16},{32,24},{40,32},{48,40},{56,48},{64,56},{72,6... | collective-permute-start | bytes 786440 | tf_op jit(solution)/shard_map/while/body/eval_jaxpr/ppermute | solution.py:12
  272.9 10.6 collective-permute-start
  340.4 10.8 collective-permute-start
  351.3 12.0 %collective-permute-start = (f32[8,64,128]{2,1,0:T(8,128)S(1)}, f32[8,64,128]{2,1,0:T(8,128)S(1)}, u32[]{:S(2)}, u32[]{:S(2)}) collective-permute-start(f32[8,64,128]{2,1,0:T(8,128)S(1)} %multiply_add_fusion.8), channel_id=1, source_target_pairs={{8,0},{16,8},{24,16},{32,24},{40,32},{48,40},{56,48},{64,56},{72,6... | collective-permute-start | bytes 786440 | tf_op jit(solution)/shard_map/while/body/eval_jaxpr/ppermute | solution.py:12
  363.4 11.5 %collective-permute-start = (f32[8,64,128]{2,1,0:T(8,128)S(1)}, f32[8,64,128]{2,1,0:T(8,128)S(1)}, u32[]{:S(2)}, u32[]{:S(2)}) collective-permute-start(f32[8,64,128]{2,1,0:T(8,128)S(1)} %multiply_add_fusion.8), channel_id=1, source_target_pairs={{8,0},{16,8},{24,16},{32,24},{40,32},{48,40},{56,48},{64,56},{72,6... | collective-permute-start | bytes 786440 | tf_op jit(solution)/shard_map/while/body/eval_jaxpr/ppermute | solution.py:12
  375.0 10.6 collective-permute-start
  438.1 10.7 collective-permute-start.1
  448.9 11.8 %collective-permute-start.1 = (f32[8,64,128]{2,1,0:T(8,128)S(1)}, f32[8,64,128]{2,1,0:T(8,128)S(1)}, u32[]{:S(2)}, u32[]{:S(2)}) collective-permute-start(f32[8,64,128]{2,1,0:T(8,128)S(1)} %multiply_add_fusion.9), channel_id=1, source_target_pairs={{0,8},{8,16},{16,24},{24,32},{32,40},{40,48},{48,56},{56,64},{64,7... | collective-permute-start | bytes 786440 | tf_op jit(solution)/shard_map/while/body/eval_jaxpr/ppermute | solution.py:12
  460.8 11.3 %collective-permute-start.1 = (f32[8,64,128]{2,1,0:T(8,128)S(1)}, f32[8,64,128]{2,1,0:T(8,128)S(1)}, u32[]{:S(2)}, u32[]{:S(2)}) collective-permute-start(f32[8,64,128]{2,1,0:T(8,128)S(1)} %multiply_add_fusion.9), channel_id=1, source_target_pairs={{0,8},{8,16},{16,24},{24,32},{32,40},{40,48},{48,56},{56,64},{64,7... | collective-permute-start | bytes 786440 | tf_op jit(solution)/shard_map/while/body/eval_jaxpr/ppermute | solution.py:12
  472.2 10.6 collective-permute-start.1
  511.5 12.3 %collective-permute-start.1 = (f32[8,64,128]{2,1,0:T(8,128)S(1)}, f32[8,64,128]{2,1,0:T(8,128)S(1)}, u32[]{:S(2)}, u32[]{:S(2)}) collective-permute-start(f32[8,64,128]{2,1,0:T(8,128)S(1)} %multiply_add_fusion.9), channel_id=1, source_target_pairs={{0,8},{8,16},{16,24},{24,32},{32,40},{40,48},{48,56},{56,64},{64,7... | collective-permute-start | bytes 786440 | tf_op jit(solution)/shard_map/while/body/eval_jaxpr/ppermute | solution.py:12
  552.1 10.7 collective-permute-start.1
  562.9 11.5 %collective-permute-start.1 = (f32[8,64,128]{2,1,0:T(8,128)S(1)}, f32[8,64,128]{2,1,0:T(8,128)S(1)}, u32[]{:S(2)}, u32[]{:S(2)}) collective-permute-start(f32[8,64,128]{2,1,0:T(8,128)S(1)} %multiply_add_fusion.9), channel_id=1, source_target_pairs={{0,8},{8,16},{16,24},{24,32},{32,40},{40,48},{48,56},{56,64},{64,7... | collective-permute-start | bytes 786440 | tf_op jit(solution)/shard_map/while/body/eval_jaxpr/ppermute | solution.py:12
  574.5 12.7 %collective-permute-start.1 = (f32[8,64,128]{2,1,0:T(8,128)S(1)}, f32[8,64,128]{2,1,0:T(8,128)S(1)}, u32[]{:S(2)}, u32[]{:S(2)}) collective-permute-start(f32[8,64,128]{2,1,0:T(8,128)S(1)} %multiply_add_fusion.9), channel_id=1, source_target_pairs={{0,8},{8,16},{16,24},{24,32},{32,40},{40,48},{48,56},{56,64},{64,7... | collective-permute-start | bytes 786440 | tf_op jit(solution)/shard_map/while/body/eval_jaxpr/ppermute | solution.py:12
  587.2 11.2 %collective-permute-start.1 = (f32[8,64,128]{2,1,0:T(8,128)S(1)}, f32[8,64,128]{2,1,0:T(8,128)S(1)}, u32[]{:S(2)}, u32[]{:S(2)}) collective-permute-start(f32[8,64,128]{2,1,0:T(8,128)S(1)} %multiply_add_fusion.9), channel_id=1, source_target_pairs={{0,8},{8,16},{16,24},{24,32},{32,40},{40,48},{48,56},{56,64},{64,7... | collective-permute-start | bytes 786440 | tf_op jit(solution)/shard_map/while/body/eval_jaxpr/ppermute | solution.py:12
  598.6 10.1 collective-permute-start.1
  627.7 11.3 %collective-permute-start.1 = (f32[8,64,128]{2,1,0:T(8,128)S(1)}, f32[8,64,128]{2,1,0:T(8,128)S(1)}, u32[]{:S(2)}, u32[]{:S(2)}) collective-permute-start(f32[8,64,128]{2,1,0:T(8,128)S(1)} %multiply_add_fusion.9), channel_id=1, source_target_pairs={{0,8},{8,16},{16,24},{24,32},{32,40},{40,48},{48,56},{56,64},{64,7... | collective-permute-start | bytes 786440 | tf_op jit(solution)/shard_map/while/body/eval_jaxpr/ppermute | solution.py:12
  639.1 13.8 %collective-permute-start.1 = (f32[8,64,128]{2,1,0:T(8,128)S(1)}, f32[8,64,128]{2,1,0:T(8,128)S(1)}, u32[]{:S(2)}, u32[]{:S(2)}) collective-permute-start(f32[8,64,128]{2,1,0:T(8,128)S(1)} %multiply_add_fusion.9), channel_id=1, source_target_pairs={{0,8},{8,16},{16,24},{24,32},{32,40},{40,48},{48,56},{56,64},{64,7... | collective-permute-start | bytes 786440 | tf_op jit(solution)/shard_map/while/body/eval_jaxpr/ppermute | solution.py:12
  653.0 13.1 %collective-permute-start.1 = (f32[8,64,128]{2,1,0:T(8,128)S(1)}, f32[8,64,128]{2,1,0:T(8,128)S(1)}, u32[]{:S(2)}, u32[]{:S(2)}) collective-permute-start(f32[8,64,128]{2,1,0:T(8,128)S(1)} %multiply_add_fusion.9), channel_id=1, source_target_pairs={{0,8},{8,16},{16,24},{24,32},{32,40},{40,48},{48,56},{56,64},{64,7... | collective-permute-start | bytes 786440 | tf_op jit(solution)/shard_map/while/body/eval_jaxpr/ppermute | solution.py:12
  666.2 11.3 %collective-permute-start.1 = (f32[8,64,128]{2,1,0:T(8,128)S(1)}, f32[8,64,128]{2,1,0:T(8,128)S(1)}, u32[]{:S(2)}, u32[]{:S(2)}) collective-permute-start(f32[8,64,128]{2,1,0:T(8,128)S(1)} %multiply_add_fusion.9), channel_id=1, source_target_pairs={{0,8},{8,16},{16,24},{24,32},{32,40},{40,48},{48,56},{56,64},{64,7... | collective-permute-start | bytes 786440 | tf_op jit(solution)/shard_map/while/body/eval_jaxpr/ppermute | solution.py:12
  687.6 10.8 collective-permute-start.1
  698.4 10.4 collective-permute-start.1
  923.2 10.6 collective-permute-start.3
  (36 other events, 308.9 us)
Sparse Core Ops, SparseCore 0:
  918.3 186.3 all-reduce.2
where the time goes:
time: 1120 us
  waiting for transfers between devices  544 us (49%)
  starting transfers between devices  262 us (23%)
  local copies, waits for them, and re-layouts  142 us (13%)
  matrix products  99.3 us (9%)
  other arithmetic  52.4 us (5%)
  between operations  14.2 us (1%)
    ppermute x64, waiting for transfers between devices, passed_along(): return lax.ppermute(array, axis, pairs)  385 us
    ppermute x64, starting transfers between devices, passed_along(): return lax.ppermute(array, axis, pairs)  262 us
    psum x1, waiting for transfers between devices, body(): lax.psum((grad_inject.reshape(tokens, states), grad_readout.reshape(token...  159 us
    dynamic_update_slice x16, local copies, waits for them, and re-layouts, body(): lax.map(span_apply, (act_blocks, grad_blocks, inject_blocks, readout_bloc...  106 us
    unnamed x15, local copies, waits for them, and re-layouts  29.1 us
  transfers between devices with their start and end apart: 65, of which 64 were waited for; matrix products, arithmetic and copies ran while one was open for 5% of the time, Pallas kernels for 0%

commit v1 on v0

v1 whole, which is shorter than its diff:
```python
import functools

import jax
import jax.numpy as jnp
from jax import lax
from jax.experimental import pallas as pl
from jax.experimental.pallas import tpu as pltpu
from jax.sharding import Mesh
from jax.sharding import PartitionSpec as P

f32, bf16 = jnp.float32, jnp.bfloat16
SPAN = 256
SEQ, HG = ("z", "x"), ("y", "c")
PREV = 16

NN = (((1,), (0,)), ((), ()))
NT = (((1,), (1,)), ((), ()))
TN = (((0,), (0,)), ((), ()))


def dot(a, b, dims):
    return lax.dot_general(a, b, dims, preferred_element_type=f32)


def split(v):
    high = v.astype(bf16)
    return high, (v - high.astype(f32)).astype(bf16)


def dot2(exact, v, dims):
    high, low = split(v)
    return dot(exact, high, dims) + dot(exact, low, dims)


def dot3(ah, al, bh, bl, dims):
    return dot(ah, bh, dims) + (dot(ah, bl, dims) + dot(al, bh, dims))


def places():
    return lax.broadcasted_iota(jnp.int32, (SPAN, 1), 0).astype(f32)


def grads_kernel(grad_ref, read_ref, rate_ref, after_ref, own_ref, carry):
    step, spans = pl.program_id(0), pl.num_programs(0)
    span = spans - 1 - step

    @pl.when(step == 0)
    def _():
        carry[...] = jnp.zeros_like(carry)

    rate = rate_ref[pl.ds(span, 1), :]
    lead = jnp.exp((places() + 1.0) * rate)
    after_ref[0] = carry[...]
    fresh = dot2(read_ref[...], grad_ref[...].astype(f32) * lead, TN)
    carry[...] = jnp.exp(SPAN * rate) * carry[...] + fresh

    @pl.when(step == spans - 1)
    def _():
        own_ref[...] = carry[...]


def states_kernel(
    x_ref, prev_ref, halo_ref, inject_ref, rate_ref, weight_ref, own_grad_ref,
    act_ref, slope_ref, before_ref, pay_ref, carry, rows,
):
    span, spans = pl.program_id(0), pl.num_programs(0)

    @pl.when(span == 0)
    def _():
        carry[...] = jnp.zeros_like(carry)
        rows[0:PREV, :] = halo_ref[...].astype(f32)

    @pl.when(span > 0)
    def _():
        rows[0:PREV, :] = prev_ref[...].astype(f32)

    rows[PREV : PREV + SPAN, :] = x_ref[...].astype(f32)
    weights = weight_ref[...].astype(f32)
    preact = weights[0:1] * rows[PREV - 3 : PREV - 3 + SPAN, :]
    for k in range(1, 4):
        preact = preact + weights[k : k + 1] * rows[PREV - 3 + k : PREV - 3 + k + SPAN, :]
    squashed = 1.0 / (1.0 + jnp.exp(-preact))
    act = (preact * squashed).astype(bf16)
    act_ref[...] = act
    slope_ref[...] = squashed * (1.0 + preact * (1.0 - squashed))
    rate = rate_ref[pl.ds(span, 1), :]
    tail = jnp.exp((SPAN - 1.0 - places()) * rate)
    before_ref[0] = carry[...]
    fresh = dot2(inject_ref[...], act.astype(f32) * tail, TN)
    carry[...] = jnp.exp(SPAN * rate) * carry[...] + fresh

    @pl.when(span == spans - 1)
    def _():
        chunks, height, width = pay_ref.shape
        half = width // 2
        for d in range(chunks):
            r, l = height * (d // 2), half * (d % 2)
            pay_ref[d, :, 0:half] = carry[r : r + height, l : l + half]
            pay_ref[d, :, half:width] = own_grad_ref[r : r + height, l : l + half]


def scan_kernel(own_ref, log_ref, out_ref):
    chunks, height, width = own_ref.shape
    half = width // 2
    state = jnp.zeros((height, half), f32)
    grad = jnp.zeros((height, half), f32)
    for e in range(chunks):
        out_ref[e, :, 0:half] = state
        state = jnp.exp(log_ref[e : e + 1, :]) * state + own_ref[e, :, 0:half]
    for e in reversed(range(chunks)):
        out_ref[e, :, half:width] = grad
        grad = jnp.exp(log_ref[e : e + 1, :]) * grad + own_ref[e, :, half:width]


def local_kernel(
    grad_ref, act_ref, slope_ref, inject_ref, read_ref, rate_ref, prior_ref, later_ref,
    before_ref, after_ref,
    pre_ref, factor_ref, adh_ref, adl_ref, gdh_ref, gdl_ref, gi_ref, gr_ref,
):
    span = pl.program_id(0)
    rate = rate_ref[pl.ds(span, 1), :]
    later = jnp.exp(later_ref[pl.ds(span, 1), :])
    prior = jnp.exp(prior_ref[pl.ds(span, 1), :])
    inject, read = inject_ref[...], read_ref[...]
    grad, act = grad_ref[...].astype(f32), act_ref[...].astype(f32)
    slope = slope_ref[...]
    here = places()
    rising = jnp.exp(here * rate)
    falling = jnp.exp(-here * rate)
    tail = jnp.exp((SPAN - 1.0 - here) * rate)
    lead = jnp.exp((here + 1.0) * rate)
    lower = lax.broadcasted_iota(jnp.int32, (SPAN, SPAN), 0) >= lax.broadcasted_iota(
        jnp.int32, (SPAN, SPAN), 1
    )
    grad_up = (grad * rising).astype(bf16)
    act_down = (act * falling).astype(bf16)
    pairs = jnp.where(lower, dot(grad_up, act_down, NT), 0.0).astype(bf16)
    mixing = jnp.where(lower, dot(read, inject, NT), 0.0).astype(bf16)
    grad_act = falling * dot(mixing, grad_up, TN)
    after, before = after_ref[0], before_ref[0]
    after_h, after_l = split(after)
    before_h, before_l = split(before)
    grad_act = grad_act + tail * (dot(inject, after_h, NN) + dot(inject, after_l, NN))
    pre_ref[...] = slope * grad_act
    factor_ref[...] = slope * (tail * later)
    act_tail, grad_lead = act * tail, grad * lead
    ath, atl = split(act_tail)
    glh, gll = split(grad_lead)
    gi_ref[...] = dot(pairs, read, TN) + dot3(ath, atl, after_h, after_l, NT)
    gr_ref[...] = dot(pairs, inject, NN) + dot3(glh, gll, before_h, before_l, NT)
    adh_ref[...], adl_ref[...] = split(act_tail * later)
    gdh_ref[...], gdl_ref[...] = split(grad_lead * prior)


def final_kernel(
    core_ref, back_ref, pre_ref, factor_ref, adh_ref, adl_ref, gdh_ref, gdl_ref,
    inject_ref, gi_ref, gr_ref, weight_ref,
    out_ref, both_ref, first_ref, eh, el, ah, al, rows,
):
    del core_ref
    step, spans = pl.program_id(0), pl.num_programs(0)

    @pl.when(step == 0)
    def _():
        chunks, height, width = back_ref.shape
        half = width // 2
        for d in range(chunks):
            r, l = height * (d // 2), half * (d % 2)
            h, w = split(back_ref[d, :, 0:half])
            eh[r : r + height, l : l + half] = h
            el[r : r + height, l : l + half] = w
            h, w = split(back_ref[d, :, half:width])
            ah[r : r + height, l : l + half] = h
            al[r : r + height, l : l + half] = w
        rows[SPAN : SPAN + 8, :] = jnp.zeros((8, rows.shape[1]), f32)

    @pl.when(step > 0)
    def _():
        rows[SPAN : SPAN + 8, :] = rows[0:8, :]

    inject = inject_ref[...]
    carried = dot(inject, ah[...], NN) + dot(inject, al[...], NN)
    rows[0:SPAN, :] = pre_ref[...] + factor_ref[...] * carried
    weights = weight_ref[...].astype(f32)
    summed = weights[0:1] * rows[3 : 3 + SPAN, :]
    for k in range(1, 4):
        summed = summed + weights[k : k + 1] * rows[3 - k : 3 - k + SPAN, :]
    out_ref[...] = summed
    first_ref[...] = rows[0:8, :]
    both_ref[0] = gi_ref[...] + dot3(adh_ref[...], adl_ref[...], ah[...], al[...], NT)
    both_ref[1] = gr_ref[...] + dot3(gdh_ref[...], gdl_ref[...], eh[...], el[...], NT)


def whole(shape):
    return pl.BlockSpec(shape, lambda *_: (0,) * len(shape))


def params():
    return pltpu.CompilerParams(
        dimension_semantics=("arbitrary",), vmem_limit_bytes=48 << 20
    )


def cost(flops, nbytes):
    return pl.CostEstimate(flops=flops, bytes_accessed=nbytes, transcendentals=0)


def body(nseq, ny, nc, conv_input, grad_output, inject, readout, conv_weight, decay_codes):
    tokens, channels = conv_input.shape
    heads, spans = decay_codes.shape
    width = channels // heads
    states = inject.shape[1]
    shape = jax.ShapeDtypeStruct
    chunk = (nseq, 2 * states // nseq, channels)

    up = [(i, i + 1) for i in range(nseq - 1)]
    down = [(i + 1, i) for i in range(nseq - 1)]
    halo = lax.ppermute(conv_input[tokens - PREV :], SEQ, up)

    logs = jnp.log1p(-decay_codes.astype(f32) * 1e-6)
    own_log = SPAN * jnp.sum(logs, axis=1)
    all_logs = lax.all_gather(own_log, SEQ)
    half = lax.rem(lax.axis_index(SEQ), 2)
    half_logs = jnp.where(half == 0, all_logs[:, : heads // 2], all_logs[:, heads // 2 :])
    scan_logs = jnp.repeat(half_logs, width, axis=1)
    rates = jnp.repeat(logs.T, width, axis=1)
    order = jnp.arange(spans)
    sooner = (order[None, :] < order[:, None])[:, :, None]
    prior = SPAN * jnp.sum(jnp.where(sooner, rates[None], 0.0), axis=1)
    later = SPAN * jnp.sum(jnp.where(sooner.swapaxes(0, 1), rates[None], 0.0), axis=1)

    def token_block(cols, order):
        return pl.BlockSpec((SPAN, cols), lambda s: (order(s), 0))

    def state_block(order):
        return pl.BlockSpec((1, states, channels), lambda s: (order(s), 0, 0))

    ahead = lambda s: s
    back = lambda s: spans - 1 - s
    rate_spec = whole((spans, channels))

    after, own_grad = pl.pallas_call(
        grads_kernel,
        grid=(spans,),
        in_specs=[token_block(channels, back), token_block(states, back), rate_spec],
        out_specs=[state_block(back), whole((states, channels))],
        out_shape=[shape((spans, states, channels), f32), shape((states, channels), f32)],
        scratch_shapes=[pltpu.VMEM((states, channels), f32)],
        compiler_params=params(),
        cost_estimate=cost(4 * tokens * channels * states, 5 << 20),
        name="own_grads",
    )(grad_output, readout, rates)

    tiles = SPAN // PREV
    act, slope, before, payload = pl.pallas_call(
        states_kernel,
        grid=(spans,),
        in_specs=[
            token_block(channels, ahead),
            pl.BlockSpec((PREV, channels), lambda s: (jnp.maximum(s * tiles - 1, 0), 0)),
            whole((PREV, channels)),
            token_block(states, ahead),
            rate_spec,
            whole(conv_weight.shape),
            whole((states, channels)),
        ],
        out_specs=[
            token_block(channels, ahead), token_block(channels, ahead), state_block(ahead), whole(chunk),
        ],
        out_shape=[
            shape((tokens, channels), bf16), shape((tokens, channels), f32),
            shape((spans, states, channels), f32), shape(chunk, f32),
        ],
        scratch_shapes=[pltpu.VMEM((states, channels), f32), pltpu.VMEM((PREV + SPAN, channels), f32)],
        compiler_params=params(),
        cost_estimate=cost(4 * tokens * channels * states, 11 << 20),
        name="own_states",
    )(conv_input, conv_input, halo, inject, rates, conv_weight, own_grad)

    arrived = lax.all_to_all(payload, SEQ, 0, 0, tiled=True)

    wide, narrow = token_block(channels, ahead), token_block(states, ahead)
    pre, factor, adh, adl, gdh, gdl, gi, gr = pl.pallas_call(
        local_kernel,
        grid=(spans,),
        in_specs=[wide, wide, wide, narrow, narrow, rate_spec, rate_spec, rate_spec]
        + [state_block(ahead)] * 2,
        out_specs=[wide] * 6 + [narrow] * 2,
        out_shape=[shape((tokens, channels), f32)] * 2
        + [shape((tokens, channels), bf16)] * 4
        + [shape((tokens, states), f32)] * 2,
        compiler_params=params(),
        cost_estimate=cost(20 * tokens * channels * SPAN, 32 << 20),
        name="local_terms",
    )(grad_output, act, slope, inject, readout, rates, prior, later, before, after)

    scanned = pl.pallas_call(
        scan_kernel, out_shape=shape(chunk, f32), compiler_params=pltpu.CompilerParams(vmem_limit_bytes=16 << 20),
        cost_estimate=cost(1 << 18, 1 << 20), name="carry",
    )(arrived, scan_logs)
    returned = lax.all_to_all(scanned, SEQ, 0, 0, tiled=True)

    core = lax.axis_index("c").astype(jnp.int32).reshape(1)

    def tb(cols):
        return pl.BlockSpec((SPAN, cols), lambda s, core: (spans - 1 - s, 0))

    grad_input, both, first = pl.pallas_call(
        final_kernel,
        grid_spec=pltpu.PrefetchScalarGridSpec(
            num_scalar_prefetch=1,
            grid=(spans,),
            in_specs=[whole(chunk)] + [tb(channels)] * 6 + [tb(states)] * 3 + [whole(conv_weight.shape)],
            out_specs=[
                tb(channels),
                pl.BlockSpec((2, SPAN, states), lambda s, core: (0, spans - 1 - s, 0)),
                whole((8, channels)),
            ],
            scratch_shapes=[pltpu.VMEM((states, channels), bf16)] * 4
            + [pltpu.VMEM((SPAN + 8, channels), f32)],
        ),
        out_shape=[
            shape((tokens, channels), f32), shape((2, tokens, states), f32), shape((8, channels), f32),
        ],
        compiler_params=params(),
        cost_estimate=cost(16 * tokens * channels * states, 22 << 20),
        name="carried_terms",
    )(core, returned, pre, factor, adh, adl, gdh, gdl, inject, gi, gr, conv_weight)

    next_rows = lax.ppermute(first, SEQ, down)
    weights = conv_weight.astype(f32)
    tail_rows = []
    for row in range(3):
        tail_rows.append(sum(weights[k] * next_rows[row - k] for k in range(row + 1)))
    patch = jnp.concatenate([jnp.zeros((5, channels), f32), jnp.stack(tail_rows)], axis=0)
    last = lax.slice_in_dim(grad_input, tokens - 8, tokens) + patch
    grad_input = lax.dynamic_update_slice(grad_input, last, (tokens - 8, 0))

    mine_is_first = lax.axis_index("c") == 0
    mine = jnp.where(mine_is_first, both[0], both[1])
    theirs = jnp.where(mine_is_first, both[1], both[0])
    swap = [(i, i ^ 1) for i in range(nc)]
    chip = mine + lax.ppermute(theirs, "c", swap)
    quarters = lax.all_to_all(chip.reshape(ny, tokens // ny, states), "y", 0, 0, tiled=True)
    quarter = jnp.sum(quarters, axis=0)
    spread = jnp.broadcast_to(quarter[None], (ny,) + quarter.shape)
    done = lax.all_to_all(spread, "y", 0, 0, tiled=True).reshape(tokens, states)
    other = lax.ppermute(done, "c", swap)
    grad_inject = jnp.where(mine_is_first, done, other)
    grad_readout = jnp.where(mine_is_first, other, done)
    return grad_input, grad_inject, grad_readout


def build(devices, sizes):
    fine = Mesh(devices.reshape(sizes), ("z", "x", "y", "c"))
    nz, nx, ny, nc = sizes
    return jax.shard_map(
        functools.partial(body, nz * nx, ny, nc),
        mesh=fine,
        in_specs=(P(SEQ, HG), P(SEQ, HG), P(SEQ, None), P(SEQ, None), P(None, HG), P(HG, SEQ)),
        out_specs=(P(SEQ, HG), P(SEQ, None), P(SEQ, None)),
        check_vma=False,
    )


def solution(mesh):
    return build(mesh.devices, (8, 4, 4, 2))
```

time: 1120 us -> 205 us (0.18)
  waiting for transfers between devices: 544 us -> 6.37 us
  starting transfers between devices: 262 us -> 47.8 us
  local copies, waits for them, and re-layouts: 142 us -> 10.8 us
  matrix products: 99.3 us -> 0 us
  blocking collectives: 0 us -> 90.9 us
  other arithmetic: 52.4 us -> 4.35 us
  Pallas kernels: 0 us -> 41.9 us
  between operations: 14.2 us -> 1.49 us
    ppermute x64 -> x4, waiting for transfers between devices: 385 us -> 6.36 us  [the longest x1 4.07 us: body(): next_rows = lax.ppermute(first, SEQ, down)]
    ppermute x64 -> x4, starting transfers between devices: 262 us -> 25.1 us  [the longest x1 16.4 us: body(): chip = mine + lax.ppermute(theirs, 'c', swap)]
    psum x1 -> x0, waiting for transfers between devices: 159 us -> none  [body(): lax.psum((grad_inject.reshape(tokens, states), grad_readout.reshape(token...]
    dynamic_update_slice x16 -> x0, local copies, waits for them, and re-layouts: 106 us -> none  [body(): lax.map(span_apply, (act_blocks, grad_blocks, inject_blocks, readout_bloc...]
    dot_general x66 -> x0, matrix products: 99.3 us -> none  [the longest x8 16.2 us: span_terms(): jnp.einsum('qhp,hpn->qn', block_grad.astype(jnp.float32) * lead_decay[:,...]
    unnamed x0 -> x1, blocking collectives: none -> 57 us
    pallas_call x0 -> x5, Pallas kernels: none -> 41.9 us  [the longest x1 15.2 us: body(): pl.pallas_call(local_kernel, grid=(spans,), in_specs=[wide, wide, wide, n...]
    all_to_all x0 -> x2, blocking collectives: none -> 34 us  [the longest x1 18.2 us: body(): lax.all_to_all(chip.reshape(ny, tokens // ny, states), 'y', 0, 0, tiled=T...]
  transfers between devices with their start and end apart: 65 -> 6, of which waited for: 64 -> 2; matrix products, arithmetic and copies ran while one was open for 5% -> 2% of each run, Pallas kernels for 0% -> 9%
where the time goes in v1:
time: 205 us; the launch traced here: 204 us
  blocking collectives  90.9 us (44%)
  starting transfers between devices  47.8 us (23%)
  Pallas kernels  41.9 us (20%)
  local copies, waits for them, and re-layouts  10.8 us (5%)
  waiting for transfers between devices  6.37 us (3%)
  other arithmetic  4.35 us (2%)
    unnamed x1, blocking collectives  57 us
    all_to_all x1, blocking collectives, body(): lax.all_to_all(chip.reshape(ny, tokens // ny, states), 'y', 0, 0, tiled=T...  18.2 us
    ppermute x1, starting transfers between devices, body(): chip = mine + lax.ppermute(theirs, 'c', swap)  16.4 us
    all_to_all x1, blocking collectives, body(): done = lax.all_to_all(spread, 'y', 0, 0, tiled=True).reshape(tokens, states)  15.7 us
    pallas_call x1, Pallas kernels, body(): pl.pallas_call(local_kernel, grid=(spans,), in_specs=[wide, wide, wide, n...  15.2 us
    all_to_all x1, starting transfers between devices, body(): returned = lax.all_to_all(scanned, SEQ, 0, 0, tiled=True)  12.3 us
    pallas_call x1, Pallas kernels, body(): pl.pallas_call(final_kernel, grid_spec=pltpu.PrefetchScalarGridSpec(num_s...  11.8 us
    pallas_call x1, Pallas kernels, body(): pl.pallas_call(states_kernel, grid=(spans,), in_specs=[token_block(channe...  10.9 us
  transfers between devices with their start and end apart: 6, of which 2 were waited for; matrix products, arithmetic and copies ran while one was open for 2% of the time, Pallas kernels for 9%

profile of v1, /device:TPU:7, one launch (start us, length us, event | category | flops | bytes accessed | tf_op | source)
XLA Modules:
  0.0 203.6 jit_solution(11911378904715969989)
XLA Ops:
  0.6 0.7 slice.44
  1.4 3.4 %collective-permute-start = (bf16[16,512]{1,0:T(8,128)(2,1)S(1)}, bf16[16,512]{1,0:T(8,128)(2,1)S(1)}, u32[]{:S(2)}, u32[]{:S(2)}) collective-permute-start(bf16[16,512]{1,0:T(8,128)(2,1)S(1)} %slice.44), channel_id=1, source_target_pairs={{0,8},{8,16},{16,24},{24,32},{32,40},{40,48},{48,56},{56,64},{64,7... | collective-permute-start | bytes 49160 | tf_op jit(solution)/shard_map/ppermute | solution.py:218
  4.8 0.8 fusion.2
  5.9 1.6 copy-done.1
  7.5 1.0 copy-done.3
  8.5 3.0 %own_grads.1 = (f32[8,128,512]{2,1,0:T(8,128)S(1)}, f32[128,512]{1,0:T(8,128)S(1)}) custom-call(bf16[2048,512]{1,0:T(8,128)(2,1)S(1)} %copy-done.1, bf16[2048,128]{1,0:T(8,128)(2,1)S(1)} %copy-done.3, f32[8,512]{1,0:T(8,128)S(1)} %reshape.55.rate_ref), custom_call_target="tpu_custom_call" | custom-call | flops 536870912 | bytes 5242880 | tf_op jit(solution)/shard_map/own_grads/pallas_call | solution.py:242
  11.5 1.3 copy-done.6
  12.8 10.9 %own_states.1 = (bf16[2048,512]{1,0:T(8,128)(2,1)S(1)}, f32[2048,512]{1,0:T(8,128)}, f32[8,128,512]{2,1,0:T(8,128)S(1)}, f32[32,8,512]{2,1,0:T(8,128)}) custom-call(bf16[2048,512]{1,0:T(8,128)(2,1)} %prev_ref.1, bf16[2048,512]{1,0:T(8,128)(2,1)} %prev_ref.1, bf16[16,512]{1,0:T(8,128)(2,1)S(1)} %collective-permute-done.halo_ref, ...), custom_call_target="tpu_custom_call" | custom-call | flops 536870912 | bytes 11534336 | tf_op jit(solution)/shard_map/own_states/pallas_call | solution.py:255
  23.8 1.3 copy-done.7
  25.0 1.3 copy-done.8
  26.4 10.4 %all-to-all-start = ((f32[32,8,512]{2,1,0:T(8,128)}), f32[32,8,512]{2,1,0:T(8,128)S(1)}, u32[]{:S(2)}, u32[]{:S(2)}) async-start(f32[32,8,512]{2,1,0:T(8,128)} %get-tuple-element.21), calls=%async_computation | async-start | bytes 1048576 | tf_op jit(solution)/shard_map/all_to_all | solution.py:280
  36.8 0.6 dynamic-slice
  38.1 57.0 %all-reduce = f32[256]{0:T(256)S(1)} all-reduce(f32[256]{0:T(256)S(1)} %multiply_dynamic-update-slice_fusion), channel_id=2, replica_groups=mesh['z'=8,'x'=4,'y'=4,'c'=2] {'z','x'}, use_global_device_ids=true, to_apply=%add | all-reduce | flops 256 | bytes 2048
  95.3 0.1 reshape.56.log_ref
  95.5 0.9 carry.1
  96.4 12.3 %all-to-all-start.1 = ((f32[32,8,512]{2,1,0:T(8,128)}), f32[32,8,512]{2,1,0:T(8,128)S(1)}, u32[]{:S(2)}, u32[]{:S(2)}) async-start(f32[32,8,512]{2,1,0:T(8,128)} %carry.1), calls=%async_computation.1 | async-start | bytes 1048576 | tf_op jit(solution)/shard_map/all_to_all | solution.py:301
  108.7 0.1 select_reduce_fusion
  108.9 1.0 copy-done.4
  109.9 15.2 %local_terms.1 = (f32[2048,512]{1,0:T(8,128)}, f32[2048,512]{1,0:T(8,128)}, bf16[2048,512]{1,0:T(8,128)(2,1)S(1)}, bf16[2048,512]{1,0:T(8,128)(2,1)}, bf16[2048,...) custom-call(bf16[2048,512]{1,0:T(8,128)(2,1)} %grad_ref.3, ...), custom_call_target="tpu_custom_call" | custom-call | flops 5368709120 | bytes 33554432 | tf_op jit(solution)/shard_map/local_terms/pallas_call | solution.py:283
  125.2 1.3 copy-done
  126.5 11.8 %carried_terms.1 = (f32[2048,512]{1,0:T(8,128)}, f32[2,2048,128]{2,1,0:T(8,128)S(1)}, f32[8,512]{1,0:T(8,128)S(1)}) custom-call(s32[1]{0:T(128)} %bitcast.core_ref, f32[32,8,512]{2,1,0:T(8,128)S(1)} %all-to-all-done.1.back_ref, f32[2048,512]{1,0:T(8,128)} %get-tuple-element.26.pre_ref, f32[2048,512]{1,0:T(8,128)} %get-tuple-element.27.factor_ref, ...), custom_call_target="tpu_custom_call" | custom-call | flops 2147483648 | bytes 23068672 | tf_op jit(solution)/shard_map/carried_terms/pallas_call | solution.py:308
  138.3 0.1 select_bitcast_fusion
  138.4 16.4 %collective-permute-start.2 = (f32[2048,128]{1,0:T(8,128)S(1)}, f32[2048,128]{1,0:T(8,128)S(1)}, u32[]{:S(2)}, u32[]{:S(2)}) collective-permute-start(f32[2048,128]{1,0:T(8,128)S(1)} %select_bitcast_fusion), channel_id=1, source_target_pairs={{0,1},{1,0},{2,3},{3,2},{4,5},{5,4},{6,7},{7,6},{8,9},{9,8},{10,11... | collective-permute-start | bytes 3145736 | tf_op jit(solution)/shard_map/ppermute | solution.py:343
  154.8 2.3 %collective-permute-done.2 = f32[2048,128]{1,0:T(8,128)S(1)} collective-permute-done((f32[2048,128]{1,0:T(8,128)S(1)}, f32[2048,128]{1,0:T(8,128)S(1)}, u32[]{:S(2)}, u32[]{:S(2)}) %collective-permute-start.2) | collective-permute-done | bytes 1048608 | tf_op jit(solution)/shard_map/ppermute | solution.py:343
  157.1 0.1 bitcast_add_fusion
  157.3 18.2 %all_to_all.20 = f32[4,512,128]{2,1,0:T(8,128)S(1)} all-to-all(f32[4,512,128]{2,1,0:T(8,128)S(1)} %bitcast.17), channel_id=1, replica_groups=mesh['z'=8,'x'=4,'y'=4,'c'=2] {'y'}, dimensions={0} | all-to-all | bytes 2097152 | tf_op jit(solution)/shard_map/all_to_all | solution.py:344
  175.7 15.7 %all_to_all.21 = f32[4,512,128]{2,1,0:T(8,128)S(1)} all-to-all(f32[4,512,128]{2,1,0:T(8,128)S(1)} %broadcast_in_dim.57), channel_id=1, replica_groups=mesh['z'=8,'x'=4,'y'=4,'c'=2] {'y'}, dimensions={0} | all-to-all | bytes 2097152 | tf_op jit(solution)/shard_map/all_to_all | solution.py:347
  191.4 2.7 %collective-permute-start.3 = (f32[2048,128]{1,0:T(8,128)S(1)}, f32[2048,128]{1,0:T(8,128)S(1)}, u32[]{:S(2)}, u32[]{:S(2)}) collective-permute-start(f32[2048,128]{1,0:T(8,128)S(1)} %bitcast.16), channel_id=1, source_target_pairs={{0,1},{1,0},{2,3},{3,2},{4,5},{5,4},{6,7},{7,6},{8,9},{9,8},{10,11... | collective-permute-start | bytes 3145736 | tf_op jit(solution)/shard_map/ppermute | solution.py:348
  194.1 2.5 %collective-permute-start.1 = (f32[8,512]{1,0:T(8,128)S(1)}, f32[8,512]{1,0:T(8,128)S(1)}, u32[]{:S(2)}, u32[]{:S(2)}) collective-permute-start(f32[8,512]{1,0:T(8,128)S(1)} %get-tuple-element.35), channel_id=1, source_target_pairs={{8,0},{16,8},{24,16},{32,24},{40,32},{48,40},{56,48},{64,56},{72,6... | collective-permute-start | bytes 49160 | tf_op jit(solution)/shard_map/ppermute | solution.py:330
  196.6 4.1 %collective-permute-done.1 = f32[8,512]{1,0:T(8,128)S(1)} collective-permute-done((f32[8,512]{1,0:T(8,128)S(1)}, f32[8,512]{1,0:T(8,128)S(1)}, u32[]{:S(2)}, u32[]{:S(2)}) %collective-permute-start.1) | collective-permute-done | bytes 16416 | tf_op jit(solution)/shard_map/ppermute | solution.py:330
  200.7 1.4 fusion
  202.1 1.5 broadcast_select_fusion
  (34 shorter events, 0.8 us)
Async XLA Ops:
  0.6 12.2 %copy-start.5 = (bf16[4,512]{1,0:T(4,128)(2,1)S(1)}, bf16[4,512]{1,0:T(4,128)(2,1)}, u32[]{:S(2)}) copy-start(bf16[4,512]{1,0:T(4,128)(2,1)} %weight_ref.3) | copy-start | bytes 12292
  1.4 11.5 %collective-permute-start = (bf16[16,512]{1,0:T(8,128)(2,1)S(1)}, bf16[16,512]{1,0:T(8,128)(2,1)S(1)}, u32[]{:S(2)}, u32[]{:S(2)}) collective-permute-start(bf16[16,512]{1,0:T(8,128)(2,1)S(1)} %slice.44), channel_id=1, source_target_pairs={{0,8},{8,16},{16,24},{24,32},{32,40},{40,48},{48,56},{56,64},{64,7... | collective-permute-start | bytes 49160 | tf_op jit(solution)/shard_map/ppermute | solution.py:218
  5.9 1.6 copy-start.1
  7.5 1.0 copy-start.3
  8.5 4.3 %copy-start.2 = (bf16[2048,128]{1,0:T(8,128)(2,1)S(1)}, bf16[2048,128]{1,0:T(8,128)(2,1)}, u32[]{:S(2)}) copy-start(bf16[2048,128]{1,0:T(8,128)(2,1)} %inject_ref.5) | copy-start | bytes 1572868
  11.5 1.3 copy-start.6
  12.8 23.9 %copy-start.9 = (u32[256]{0:T(256)S(1)}, u32[256]{0:T(256)}, u32[]{:S(2)}) copy-start(u32[256]{0:T(256)} %constant.35) | copy-start | bytes 3076
  23.8 1.3 copy-start.7
  25.0 1.3 copy-start.8
  26.4 69.1 %all-to-all-start = ((f32[32,8,512]{2,1,0:T(8,128)}), f32[32,8,512]{2,1,0:T(8,128)S(1)}, u32[]{:S(2)}, u32[]{:S(2)}) async-start(f32[32,8,512]{2,1,0:T(8,128)} %get-tuple-element.21), calls=%async_computation | async-start | bytes 1048576 | tf_op jit(solution)/shard_map/all_to_all | solution.py:280
  96.4 30.1 %all-to-all-start.1 = ((f32[32,8,512]{2,1,0:T(8,128)}), f32[32,8,512]{2,1,0:T(8,128)S(1)}, u32[]{:S(2)}, u32[]{:S(2)}) async-start(f32[32,8,512]{2,1,0:T(8,128)} %carry.1), calls=%async_computation.1 | async-start | bytes 1048576 | tf_op jit(solution)/shard_map/all_to_all | solution.py:301
  108.9 1.0 copy-start.4
  125.2 1.3 copy-start
  138.4 18.7 %collective-permute-start.2 = (f32[2048,128]{1,0:T(8,128)S(1)}, f32[2048,128]{1,0:T(8,128)S(1)}, u32[]{:S(2)}, u32[]{:S(2)}) collective-permute-start(f32[2048,128]{1,0:T(8,128)S(1)} %select_bitcast_fusion), channel_id=1, source_target_pairs={{0,1},{1,0},{2,3},{3,2},{4,5},{5,4},{6,7},{7,6},{8,9},{9,8},{10,11... | collective-permute-start | bytes 3145736 | tf_op jit(solution)/shard_map/ppermute | solution.py:343
  191.4 10.7 %collective-permute-start.3 = (f32[2048,128]{1,0:T(8,128)S(1)}, f32[2048,128]{1,0:T(8,128)S(1)}, u32[]{:S(2)}, u32[]{:S(2)}) collective-permute-start(f32[2048,128]{1,0:T(8,128)S(1)} %bitcast.16), channel_id=1, source_target_pairs={{0,1},{1,0},{2,3},{3,2},{4,5},{5,4},{6,7},{7,6},{8,9},{9,8},{10,11... | collective-permute-start | bytes 3145736 | tf_op jit(solution)/shard_map/ppermute | solution.py:348
  194.1 6.6 %collective-permute-start.1 = (f32[8,512]{1,0:T(8,128)S(1)}, f32[8,512]{1,0:T(8,128)S(1)}, u32[]{:S(2)}, u32[]{:S(2)}) collective-permute-start(f32[8,512]{1,0:T(8,128)S(1)} %get-tuple-element.35), channel_id=1, source_target_pairs={{8,0},{16,8},{24,16},{32,24},{40,32},{48,40},{56,48},{64,56},{72,6... | collective-permute-start | bytes 49160 | tf_op jit(solution)/shard_map/ppermute | solution.py:330

commit v2 on v1

v2 whole, which is shorter than its diff:
```python
import functools

import jax
import jax.numpy as jnp
from jax import lax
from jax.experimental import pallas as pl
from jax.experimental.pallas import tpu as pltpu
from jax.sharding import Mesh
from jax.sharding import PartitionSpec as P

f32, bf16 = jnp.float32, jnp.bfloat16
SPAN = 256
SEQ, HG = ("z", "x"), ("y", "c")
PREV = 16

NN = (((1,), (0,)), ((), ()))
NT = (((1,), (1,)), ((), ()))
TN = (((0,), (0,)), ((), ()))


def dot(a, b, dims):
    return lax.dot_general(a, b, dims, preferred_element_type=f32)


def split(v):
    high = v.astype(bf16)
    return high, (v - high.astype(f32)).astype(bf16)


def dot2(exact, v, dims):
    high, low = split(v)
    return dot(exact, high, dims) + dot(exact, low, dims)


def dot3(ah, al, bh, bl, dims):
    return dot(ah, bh, dims) + (dot(ah, bl, dims) + dot(al, bh, dims))


def places():
    return lax.broadcasted_iota(jnp.int32, (SPAN, 1), 0).astype(f32)


def grads_kernel(grad_ref, read_ref, rate_ref, after_ref, own_ref, carry):
    step, spans = pl.program_id(0), pl.num_programs(0)
    span = spans - 1 - step

    @pl.when(step == 0)
    def _():
        carry[...] = jnp.zeros_like(carry)

    rate = rate_ref[pl.ds(span, 1), :]
    lead = jnp.exp((places() + 1.0) * rate)
    after_ref[0] = carry[...]
    fresh = dot2(read_ref[...], grad_ref[...].astype(f32) * lead, TN)
    carry[...] = jnp.exp(SPAN * rate) * carry[...] + fresh

    @pl.when(step == spans - 1)
    def _():
        own_ref[...] = carry[...]


def rebuilt(x_ref, prev_ref, halo_ref, weight_ref, rows, span):
    @pl.when(span == 0)
    def _():
        rows[0:PREV, :] = halo_ref[...].astype(f32)

    @pl.when(span > 0)
    def _():
        rows[0:PREV, :] = prev_ref[...].astype(f32)

    rows[PREV : PREV + SPAN, :] = x_ref[...].astype(f32)
    weights = weight_ref[...].astype(f32)
    preact = weights[0:1] * rows[PREV - 3 : PREV - 3 + SPAN, :]
    for k in range(1, 4):
        preact = preact + weights[k : k + 1] * rows[PREV - 3 + k : PREV - 3 + k + SPAN, :]
    return preact, jax.nn.sigmoid(preact)


def states_kernel(
    x_ref, prev_ref, halo_ref, inject_ref, rate_ref, weight_ref, own_grad_ref, log_ref,
    before_ref, pay_ref, carry, rows,
):
    span, spans = pl.program_id(0), pl.num_programs(0)

    @pl.when(span == 0)
    def _():
        carry[...] = jnp.zeros_like(carry)

    preact, squashed = rebuilt(x_ref, prev_ref, halo_ref, weight_ref, rows, span)
    act = (preact * squashed).astype(bf16)
    rate = rate_ref[pl.ds(span, 1), :]
    tail = jnp.exp((SPAN - 1.0 - places()) * rate)
    before_ref[0] = carry[...]
    fresh = dot2(inject_ref[...], act.astype(f32) * tail, TN)
    carry[...] = jnp.exp(SPAN * rate) * carry[...] + fresh

    @pl.when(span == spans - 1)
    def _():
        chunks, height, _ = pay_ref.shape
        half = carry.shape[1] // 2
        for d in range(chunks):
            r, l = height * (d // 2), half * (d % 2)
            pay_ref[d, :, 0:half] = carry[r : r + height, l : l + half]
            pay_ref[d, :, half : 2 * half] = own_grad_ref[r : r + height, l : l + half]
            for row in range(half // 128):
                at = l + 128 * row
                pay_ref[d, row : row + 1, 2 * half : 2 * half + 128] = log_ref[:, at : at + 128]


def scan_kernel(own_ref, out_ref):
    chunks, height, width = out_ref.shape
    half = width // 2

    def gain(e):
        logs = [own_ref[e, r : r + 1, width : width + 128] for r in range(half // 128)]
        return jnp.exp(jnp.concatenate(logs, axis=1))

    state = jnp.zeros((height, half), f32)
    grad = jnp.zeros((height, half), f32)
    for e in range(chunks):
        out_ref[e, :, 0:half] = state
        state = gain(e) * state + own_ref[e, :, 0:half]
    for e in reversed(range(chunks)):
        out_ref[e, :, half:width] = grad
        grad = gain(e) * grad + own_ref[e, :, half:width]


def causal():
    row = lax.broadcasted_iota(jnp.int32, (SPAN, SPAN), 0)
    return row >= lax.broadcasted_iota(jnp.int32, (SPAN, SPAN), 1)


def local_input_kernel(
    x_ref, prev_ref, halo_ref, grad_ref, inject_ref, read_ref, rate_ref, later_ref,
    after_ref, weight_ref,
    act_ref, pre_ref, factor_ref, rows,
):
    span = pl.program_id(0)
    preact, squashed = rebuilt(x_ref, prev_ref, halo_ref, weight_ref, rows, span)
    act_ref[...] = (preact * squashed).astype(bf16)
    slope = squashed * (1.0 + preact * (1.0 - squashed))
    rate = rate_ref[pl.ds(span, 1), :]
    later = jnp.exp(later_ref[pl.ds(span, 1), :])
    inject, read = inject_ref[...], read_ref[...]
    here = places()
    falling = jnp.exp(-here * rate)
    end = jnp.exp((SPAN - 1.0) * rate)
    grad_up = (grad_ref[...].astype(f32) * jnp.exp(here * rate)).astype(bf16)
    mixing = jnp.where(causal(), dot(read, inject, NT), 0.0).astype(bf16)
    high, low = split(after_ref[0] * end)
    stacked = jnp.concatenate([high, low], axis=0)
    doubled = jnp.concatenate([inject, inject], axis=1)
    steep = slope * falling
    pre_ref[...] = steep * (dot(mixing, grad_up, TN) + dot(doubled, stacked, NN))
    factor_ref[...] = steep * (end * later)


def wide_product(high, low, both, states):
    wide = dot(high, both, NT)
    return wide[:, :states] + (wide[:, states:] + dot(low, both[0:states, :], NT))


def local_shared_kernel(
    grad_ref, act_ref, inject_ref, read_ref, rate_ref, prior_ref, later_ref,
    before_ref, after_ref,
    adh_ref, adl_ref, gdh_ref, gdl_ref, gi_ref, gr_ref,
):
    span = pl.program_id(0)
    rate = rate_ref[pl.ds(span, 1), :]
    later = later_ref[pl.ds(span, 1), :]
    prior = prior_ref[pl.ds(span, 1), :]
    inject, read = inject_ref[...], read_ref[...]
    states = inject.shape[1]
    here = places()
    up = grad_ref[...].astype(f32) * jnp.exp(here * rate)
    down = act_ref[...].astype(f32) * jnp.exp(-here * rate)
    uph, upl = split(up)
    downh, downl = split(down)
    pairs = jnp.where(causal(), dot(uph, downh, NT), 0.0).astype(bf16)
    afters = jnp.concatenate(split(after_ref[0] * jnp.exp((SPAN - 1.0) * rate)), axis=0)
    befores = jnp.concatenate(split(before_ref[0] * jnp.exp(rate)), axis=0)
    gi_ref[...] = dot(pairs, read, TN) + wide_product(downh, downl, afters, states)
    gr_ref[...] = dot(pairs, inject, NN) + wide_product(uph, upl, befores, states)
    adh_ref[...], adl_ref[...] = split(down * jnp.exp((SPAN - 1.0) * rate + later))
    gdh_ref[...], gdl_ref[...] = split(up * jnp.exp(rate + prior))


def unpacked(back_ref, high, low, grads):
    chunks, height, width = back_ref.shape
    half = width // 2
    start = half if grads else 0
    states = high.shape[0] // 2 if low is None else high.shape[0]
    for d in range(chunks):
        r, l = height * (d // 2), half * (d % 2)
        h, w = split(back_ref[d, :, start : start + half])
        high[r : r + height, l : l + half] = h
        if low is None:
            high[states + r : states + r + height, l : l + half] = w
        else:
            low[r : r + height, l : l + half] = w


def shared_kernel(
    core_ref, back_ref, adh_ref, adl_ref, gdh_ref, gdl_ref, gi_ref, gr_ref,
    mine_ref, theirs_ref, grads, carried,
):
    @pl.when(pl.program_id(0) == 0)
    def _():
        unpacked(back_ref, grads, None, True)
        unpacked(back_ref, carried, None, False)

    states = gi_ref.shape[1]
    gi = gi_ref[...] + wide_product(adh_ref[...], adl_ref[...], grads[...], states)
    gr = gr_ref[...] + wide_product(gdh_ref[...], gdl_ref[...], carried[...], states)
    first = core_ref[0] == 0
    mine_ref[...] = jnp.where(first, gi, gr)
    theirs_ref[...] = jnp.where(first, gr, gi)


def input_kernel(
    back_ref, pre_ref, factor_ref, inject_ref, weight_ref, out_ref, first_ref, grads, rows
):
    @pl.when(pl.program_id(0) == 0)
    def _():
        unpacked(back_ref, grads, None, True)
        rows[SPAN : SPAN + 8, :] = jnp.zeros((8, rows.shape[1]), f32)

    @pl.when(pl.program_id(0) > 0)
    def _():
        rows[SPAN : SPAN + 8, :] = rows[0:8, :]

    inject = inject_ref[...]
    carried = dot(jnp.concatenate([inject, inject], axis=1), grads[...], NN)
    rows[0:SPAN, :] = pre_ref[...] + factor_ref[...] * carried
    weights = weight_ref[...].astype(f32)
    summed = weights[0:1] * rows[3 : 3 + SPAN, :]
    for k in range(1, 4):
        summed = summed + weights[k : k + 1] * rows[3 - k : 3 - k + SPAN, :]
    out_ref[...] = summed
    first_ref[...] = rows[0:8, :]


def whole(shape):
    return pl.BlockSpec(shape, lambda *_: (0,) * len(shape))


def params(mib=53):
    return pltpu.CompilerParams(vmem_limit_bytes=mib << 20)


def cost(flops, nbytes):
    return pl.CostEstimate(flops=flops, bytes_accessed=nbytes, transcendentals=0)


def body(nseq, ny, nc, conv_input, grad_output, inject, readout, conv_weight, decay_codes):
    tokens, channels = conv_input.shape
    heads, spans = decay_codes.shape
    width = channels // heads
    states = inject.shape[1]
    shape = jax.ShapeDtypeStruct
    height = 2 * states // nseq
    chunk = (nseq, height, channels)

    up = [(i, i + 1) for i in range(nseq - 1)]
    down = [(i + 1, i) for i in range(nseq - 1)]
    halo = lax.ppermute(conv_input[tokens - PREV :], SEQ, up)

    logs = jnp.log1p(-decay_codes.astype(f32) * 1e-6)
    rates = jnp.repeat(logs.T, width, axis=1)
    own_log = SPAN * jnp.sum(rates, axis=0, keepdims=True)
    order = jnp.arange(spans)
    sooner = (order[None, :] < order[:, None])[:, :, None]
    prior = SPAN * jnp.sum(jnp.where(sooner, rates[None], 0.0), axis=1)
    later = SPAN * jnp.sum(jnp.where(sooner.swapaxes(0, 1), rates[None], 0.0), axis=1)

    def token_block(cols, order):
        return pl.BlockSpec((SPAN, cols), lambda s, *_: (order(s), 0))

    def state_block(order):
        return pl.BlockSpec((1, states, channels), lambda s: (order(s), 0, 0))

    ahead = lambda s: s
    back = lambda s: spans - 1 - s
    rate_spec = whole((spans, channels))
    tiles = SPAN // PREV
    x_specs = [
        token_block(channels, ahead),
        pl.BlockSpec((PREV, channels), lambda s: (jnp.maximum(s * tiles - 1, 0), 0)),
        whole((PREV, channels)),
    ]
    wide, narrow = token_block(channels, ahead), token_block(states, ahead)
    rows = pltpu.VMEM((PREV + SPAN, channels), f32)

    after, own_grad = pl.pallas_call(
        grads_kernel,
        grid=(spans,),
        in_specs=[token_block(channels, back), token_block(states, back), rate_spec],
        out_specs=[state_block(back), whole((states, channels))],
        out_shape=[shape((spans, states, channels), f32), shape((states, channels), f32)],
        scratch_shapes=[pltpu.VMEM((states, channels), f32)],
        compiler_params=params(),
        cost_estimate=cost(4 * tokens * channels * states, 5 << 20),
        name="own_grads",
    )(grad_output, readout, rates)

    before, payload = pl.pallas_call(
        states_kernel,
        grid=(spans,),
        in_specs=x_specs
        + [narrow, rate_spec, whole(conv_weight.shape), whole((states, channels)), whole((1, channels))],
        out_specs=[state_block(ahead), whole((nseq, height, channels + 128))],
        out_shape=[
            shape((spans, states, channels), f32), shape((nseq, height, channels + 128), f32),
        ],
        scratch_shapes=[pltpu.VMEM((states, channels), f32), rows],
        compiler_params=params(),
        cost_estimate=cost(4 * tokens * channels * states, 11 << 20),
        name="own_states",
    )(conv_input, conv_input, halo, inject, rates, conv_weight, own_grad, own_log)

    arrived = lax.all_to_all(payload, SEQ, 0, 0, tiled=True)

    act, pre, factor = pl.pallas_call(
        local_input_kernel,
        grid=(spans,),
        in_specs=x_specs + [wide, narrow, narrow, rate_spec, rate_spec, state_block(ahead)]
        + [whole(conv_weight.shape)],
        out_specs=[wide] * 3,
        out_shape=[shape((tokens, channels), bf16)] + [shape((tokens, channels), f32)] * 2,
        scratch_shapes=[rows],
        compiler_params=params(),
        cost_estimate=cost(8 * tokens * channels * SPAN, 18 << 20),
        name="local_input",
    )(
        conv_input, conv_input, halo, grad_output, inject, readout, rates, later,
        after, conv_weight,
    )
    arrived, act = lax.optimization_barrier((arrived, act))

    adh, adl, gdh, gdl, gi, gr = pl.pallas_call(
        local_shared_kernel,
        grid=(spans,),
        in_specs=[wide, wide, narrow, narrow, rate_spec, rate_spec, rate_spec]
        + [state_block(ahead)] * 2,
        out_specs=[wide] * 4 + [narrow] * 2,
        out_shape=[shape((tokens, channels), bf16)] * 4 + [shape((tokens, states), f32)] * 2,
        compiler_params=params(),
        cost_estimate=cost(12 * tokens * channels * SPAN, 19 << 20),
        name="local_shared",
    )(grad_output, act, inject, readout, rates, prior, later, before, after)

    scanned = pl.pallas_call(
        scan_kernel, out_shape=shape(chunk, f32), compiler_params=params(8),
        cost_estimate=cost(1 << 18, 1 << 20), name="carry",
    )(arrived)
    returned = lax.all_to_all(scanned, SEQ, 0, 0, tiled=True)

    core = lax.axis_index("c").astype(jnp.int32).reshape(1)
    mine, theirs = pl.pallas_call(
        shared_kernel,
        grid_spec=pltpu.PrefetchScalarGridSpec(
            num_scalar_prefetch=1,
            grid=(spans,),
            in_specs=[whole(chunk)] + [wide] * 4 + [narrow] * 2,
            out_specs=[narrow, narrow],
            scratch_shapes=[pltpu.VMEM((2 * states, channels), bf16)] * 2,
        ),
        out_shape=[shape((tokens, states), f32)] * 2,
        compiler_params=params(),
        cost_estimate=cost(12 * tokens * channels * states, 13 << 20),
        name="shared_terms",
    )(core, returned, adh, adl, gdh, gdl, gi, gr)

    swap = [(i, i ^ 1) for i in range(nc)]
    chip = mine + lax.ppermute(theirs, "c", swap)
    here = lax.axis_index("y")
    part = tokens // ny

    def turn(array, by):
        return lax.ppermute(array, "y", [(i, (i + by) % ny) for i in range(ny)])

    def cut(array, which):
        return lax.dynamic_slice_in_dim(array, lax.rem(here + which, ny) * part, part)

    sent = [turn(cut(chip, by).astype(bf16), by) for by in range(1, ny)]

    grad_input, first = pl.pallas_call(
        input_kernel,
        grid=(spans,),
        in_specs=[
            whole(chunk), token_block(channels, back), token_block(channels, back),
            token_block(states, back), whole(conv_weight.shape),
        ],
        out_specs=[token_block(channels, back), whole((8, channels))],
        out_shape=[shape((tokens, channels), f32), shape((8, channels), f32)],
        scratch_shapes=[
            pltpu.VMEM((2 * states, channels), bf16), pltpu.VMEM((SPAN + 8, channels), f32),
        ],
        compiler_params=params(),
        cost_estimate=cost(4 * tokens * channels * states, 13 << 20),
        name="input_grads",
    )(returned, pre, factor, inject, conv_weight)

    *sent, first = lax.optimization_barrier((*sent, first))
    quarter = cut(chip, 0)
    for piece in sent:
        quarter = quarter + piece.astype(f32)
    quarter = quarter.astype(bf16)
    done = jnp.zeros((tokens, states), bf16)
    for by in range(ny):
        piece = quarter if by == 0 else turn(quarter, by)
        done = lax.dynamic_update_slice_in_dim(
            done, piece, lax.rem(here - by + ny, ny) * part, 0
        )
    other = lax.ppermute(done, "c", swap)
    mine_is_first = lax.axis_index("c") == 0
    grad_inject = jnp.where(mine_is_first, done, other).astype(f32)
    grad_readout = jnp.where(mine_is_first, other, done).astype(f32)

    next_rows = lax.ppermute(first, SEQ, down)
    weights = conv_weight.astype(f32)
    tail_rows = []
    for row in range(3):
        tail_rows.append(sum(weights[k] * next_rows[row - k] for k in range(row + 1)))
    patch = jnp.concatenate([jnp.zeros((5, channels), f32), jnp.stack(tail_rows)], axis=0)
    last = lax.slice_in_dim(grad_input, tokens - 8, tokens) + patch
    grad_input = lax.dynamic_update_slice(grad_input, last, (tokens - 8, 0))
    return grad_input, grad_inject, grad_readout


def build(devices, sizes):
    fine = Mesh(devices.reshape(sizes), ("z", "x", "y", "c"))
    nz, nx, ny, nc = sizes
    return jax.shard_map(
        functools.partial(body, nz * nx, ny, nc),
        mesh=fine,
        in_specs=(P(SEQ, HG), P(SEQ, HG), P(SEQ, None), P(SEQ, None), P(None, HG), P(HG, SEQ)),
        out_specs=(P(SEQ, HG), P(SEQ, None), P(SEQ, None)),
        check_vma=False,
    )


def solution(mesh):
    return build(mesh.devices, (8, 4, 4, 2))
```

time: 205 us -> 127 us (0.62)
  blocking collectives: 90.9 us -> 0 us
  Pallas kernels: 41.9 us -> 59.1 us
  waiting for transfers between devices: 6.37 us -> 20.9 us
  starting transfers between devices: 47.8 us -> 35.8 us
  local copies, waits for them, and re-layouts: 10.8 us -> 2.41 us
    unnamed x1 -> x0, blocking collectives: 57 us -> none
    all_to_all x2 -> x0, blocking collectives: 34 us -> none  [the longest x1 18.2 us: body(): lax.all_to_all(chip.reshape(ny, tokens // ny, states), 'y', 0, 0, tiled=T...]
    pallas_call x3 -> x5, Pallas kernels: 38 us -> 51.2 us  [the longest x1 13.1 us: body(): pl.pallas_call(local_input_kernel, grid=(spans,), in_specs=x_specs + [wid...]
    ppermute x1, starting transfers between devices: 16.4 us -> 3.27 us  [body(): chip = mine + lax.ppermute(theirs, 'c', swap)]
    unnamed x22 -> x6, local copies, waits for them, and re-layouts: 9.5 us -> 1.06 us
    ppermute x0 -> x6, starting transfers between devices: none -> 8.05 us  [turn(): return lax.ppermute(array, 'y', [(i, (i + by) % ny) for i in range(ny)])]
    all_to_all x1, starting transfers between devices: 12.3 us -> 5.92 us  [body(): returned = lax.all_to_all(scanned, SEQ, 0, 0, tiled=True)]
    ppermute x0 -> x6, waiting for transfers between devices: none -> 5.43 us  [turn(): return lax.ppermute(array, 'y', [(i, (i + by) % ny) for i in range(ny)])]
  transfers between devices with their start and end apart: 6 -> 12, of which waited for: 2 -> 5; matrix products, arithmetic and copies ran while one was open for 2% -> 2% of each run, Pallas kernels for 9% -> 32%
where the time goes in v2:
time: 127 us; the launch traced here: 124 us
  Pallas kernels  59.1 us (47%)
  starting transfers between devices  35.8 us (28%)
  waiting for transfers between devices  20.9 us (16%)
  other arithmetic  5.36 us (4%)
  local copies, waits for them, and re-layouts  2.41 us (2%)
    pallas_call x1, Pallas kernels, body(): pl.pallas_call(local_input_kernel, grid=(spans,), in_specs=x_specs + [wid...  13.1 us
    pallas_call x1, Pallas kernels, body(): pl.pallas_call(local_shared_kernel, grid=(spans,), in_specs=[wide, wide,...  10.8 us
    all_to_all x1, starting transfers between devices, body(): arrived = lax.all_to_all(payload, SEQ, 0, 0, tiled=True)  10.4 us
    pallas_call x1, Pallas kernels, body(): pl.pallas_call(states_kernel, grid=(spans,), in_specs=x_specs + [narrow,...  9.38 us
    pallas_call x1, Pallas kernels, body(): pl.pallas_call(input_kernel, grid=(spans,), in_specs=[whole(chunk), token...  9.14 us
    pallas_call x1, Pallas kernels, body(): pl.pallas_call(shared_kernel, grid_spec=pltpu.PrefetchScalarGridSpec(num_...  8.79 us
    ppermute x6, starting transfers between devices, turn(): return lax.ppermute(array, 'y', [(i, (i + by) % ny) for i in range(ny)])  8.05 us
    pallas_call x1, Pallas kernels, body(): pl.pallas_call(grads_kernel, grid=(spans,), in_specs=[token_block(channel...  6.97 us
  transfers between devices with their start and end apart: 12, of which 5 were waited for; matrix products, arithmetic and copies ran while one was open for 2% of the time, Pallas kernels for 32%

profile of v2, /device:TPU:7, one launch (start us, length us, event | category | flops | bytes accessed | tf_op | source)
XLA Modules:
  0.0 124.4 jit_solution(1825548560953934209)
XLA Ops:
  0.6 0.8 slice.30
  1.4 3.4 %collective-permute-start = (bf16[16,512]{1,0:T(8,128)(2,1)S(1)}, bf16[16,512]{1,0:T(8,128)(2,1)S(1)}, u32[]{:S(2)}, u32[]{:S(2)}) collective-permute-start(bf16[16,512]{1,0:T(8,128)(2,1)S(1)} %slice.30), channel_id=1, source_target_pairs={{0,8},{8,16},{16,24},{24,32},{32,40},{40,48},{48,56},{56,64},{64,7... | collective-permute-start | bytes 49160 | tf_op jit(solution)/shard_map/ppermute | solution.py:266
  4.9 0.8 fusion.2
  5.9 1.0 copy-done.1
  7.0 7.0 %own_grads.1 = (f32[8,128,512]{2,1,0:T(8,128)}, f32[128,512]{1,0:T(8,128)S(1)}) custom-call(bf16[2048,512]{1,0:T(8,128)(2,1)} %grad_ref.5, bf16[2048,128]{1,0:T(8,128)(2,1)S(1)} %copy-done.1, f32[8,512]{1,0:T(8,128)S(1)} %reshape.46.rate_ref), custom_call_target="tpu_custom_call" | custom-call | flops 536870912 | bytes 5242880 | tf_op jit(solution)/shard_map/own_grads/pallas_call | solution.py:294
  14.1 9.4 %own_states.1 = (f32[8,128,512]{2,1,0:T(8,128)}, f32[32,8,640]{2,1,0:T(8,128)}) custom-call(bf16[2048,512]{1,0:T(8,128)(2,1)} %prev_ref.3, bf16[2048,512]{1,0:T(8,128)(2,1)} %prev_ref.3, bf16[16,512]{1,0:T(8,128)(2,1)S(1)} %collective-permute-done.halo_ref, bf16[2048,128]{1,0:T(8,128)(2,1)S(1)} %copy-done, f32[8,512]{1,0:T(8,128)S(1)} %reshape.46.rate_ref, ...), custom_call_target="tpu_custom_call" | custom-call | flops 536870912 | bytes 11534336 | tf_op jit(solution)/shard_map/own_states/pallas_call | solution.py:306
  23.5 10.4 %all-to-all-start = ((f32[32,8,640]{2,1,0:T(8,128)}), f32[32,8,640]{2,1,0:T(8,128)S(1)}, u32[]{:S(2)}, u32[]{:S(2)}) async-start(f32[32,8,640]{2,1,0:T(8,128)} %get-tuple-element.27), calls=%async_computation | async-start | bytes 1310720 | tf_op jit(solution)/shard_map/all_to_all | solution.py:321
  33.9 0.1 select_reduce_fusion
  34.0 13.1 %local_input.1 = (bf16[2048,512]{1,0:T(8,128)(2,1)}, f32[2048,512]{1,0:T(8,128)}, f32[2048,512]{1,0:T(8,128)}) custom-call(bf16[2048,512]{1,0:T(8,128)(2,1)} %prev_ref.3, bf16[2048,512]{1,0:T(8,128)(2,1)} %prev_ref.3, bf16[16,512]{1,0:T(8,128)(2,1)S(1)} %collective-permute-done.halo_ref, bf16[2048,512]{1,0:T(8,128)(2,1)} %grad_ref.5, ...), custom_call_target="tpu_custom_call" | custom-call | flops 2147483648 | bytes 18874368 | tf_op jit(solution)/shard_map/local_input/pallas_call | solution.py:323
  47.1 5.0 %all-to-all-done.own_ref = f32[32,8,640]{2,1,0:T(8,128)S(1)} async-done(((f32[32,8,640]{2,1,0:T(8,128)}), f32[32,8,640]{2,1,0:T(8,128)S(1)}, u32[]{:S(2)}, u32[]{:S(2)}) %all-to-all-start) | async-done | bytes 655392 | tf_op jit(solution)/shard_map/all_to_all | solution.py:321
  52.1 0.9 carry.1
  53.0 5.9 %all-to-all-start.1 = ((f32[32,8,512]{2,1,0:T(8,128)}), f32[32,8,512]{2,1,0:T(8,128)S(1)}, u32[]{:S(2)}, u32[]{:S(2)}) async-start(f32[32,8,512]{2,1,0:T(8,128)} %carry.1), calls=%async_computation.1 | async-start | bytes 1048576 | tf_op jit(solution)/shard_map/all_to_all | solution.py:356
  59.0 10.8 %local_shared.1 = (bf16[2048,512]{1,0:T(8,128)(2,1)}, bf16[2048,512]{1,0:T(8,128)(2,1)}, bf16[2048,512]{1,0:T(8,128)(2,1)}, bf16[2048,512]{1,0:T(8,128)(2,1)}, f32[2048,128]{1,0:T(8,128)}, /*index=5*/f32[2048,128]{1,0:T(8,128)}) custom-call(bf16[2048,512]{1,0:T(8,128)(2,1)} %grad_ref.5, bf16[2048,512]{1,0:T(8,128)(2,1)} %get-tuple-element.34.act_ref, ...), custom_call_target="tpu_custom_call" | custom-call | flops 3221225472 | bytes 19922944 | tf_op jit(solution)/shard_map/local_shared/pallas_call | solution.py:340
  69.8 4.0 %all-to-all-done.1.back_ref = f32[32,8,512]{2,1,0:T(8,128)S(1)} async-done(((f32[32,8,512]{2,1,0:T(8,128)}), f32[32,8,512]{2,1,0:T(8,128)S(1)}, u32[]{:S(2)}, u32[]{:S(2)}) %all-to-all-start.1) | async-done | bytes 524320 | tf_op jit(solution)/shard_map/all_to_all | solution.py:356
  73.7 8.8 %shared_terms.1 = (f32[2048,128]{1,0:T(8,128)}, f32[2048,128]{1,0:T(8,128)}) custom-call(s32[1]{0:T(128)} %bitcast.3.core_ref, f32[32,8,512]{2,1,0:T(8,128)S(1)} %all-to-all-done.1.back_ref, bf16[2048,512]{1,0:T(8,128)(2,1)} %get-tuple-element.36.adh_ref, bf16[2048,512]{1,0:T(8,128)(2,1)} %get-tuple-element.37.adl_ref, ...), custom_call_target="tpu_custom_call" | custom-call | flops 1610612736 | bytes 13631488 | tf_op jit(solution)/shard_map/shared_terms/pallas_call | solution.py:359
  82.5 3.3 %collective-permute-start.1 = (f32[2048,128]{1,0:T(8,128)}, f32[2048,128]{1,0:T(8,128)S(1)}, u32[]{:S(2)}, u32[]{:S(2)}) collective-permute-start(f32[2048,128]{1,0:T(8,128)} %get-tuple-element.43), channel_id=1, source_target_pairs={{0,1},{1,0},{2,3},{3,2},{4,5},{5,4},{6,7},{7,6},{8,9},{9,8},{10,11... | collective-permute-start | bytes 3145736 | tf_op jit(solution)/shard_map/ppermute | solution.py:375
  85.8 2.5 %collective-permute-done.1 = f32[2048,128]{1,0:T(8,128)S(1)} collective-permute-done((f32[2048,128]{1,0:T(8,128)}, f32[2048,128]{1,0:T(8,128)S(1)}, u32[]{:S(2)}, u32[]{:S(2)}) %collective-permute-start.1) | collective-permute-done | bytes 1048608 | tf_op jit(solution)/shard_map/ppermute | solution.py:375
  88.3 1.4 %add.69 = f32[2048,128]{1,0:T(8,128)S(1)} add(f32[2048,128]{1,0:T(8,128)} %get-tuple-element.42, f32[2048,128]{1,0:T(8,128)S(1)} %collective-permute-done.1) | non-fusion elementwise | flops 262144 | bytes 3145728 | tf_op jit(solution)/shard_map/add | solution.py:375
  89.8 1.4 %collective-permute-start.2 = (bf16[512,128]{1,0:T(8,128)(2,1)S(1)}, bf16[512,128]{1,0:T(8,128)(2,1)S(1)}, u32[]{:S(2)}, u32[]{:S(2)}) collective-permute-start(bf16[512,128]{1,0:T(8,128)(2,1)S(1)} %get-tuple-element.57), channel_id=1, source_target_pairs={{0,2},{2,4},{4,6},{6,0},{1,3},{3,5},{5,7},{7,1},{8,10},{10,12},{12... | collective-permute-start | bytes 393224 | tf_op jit(solution)/shard_map/ppermute | solution.py:380
  91.2 2.6 %collective-permute-start.3 = (bf16[512,128]{1,0:T(8,128)(2,1)S(1)}, bf16[512,128]{1,0:T(8,128)(2,1)S(1)}, u32[]{:S(2)}, u32[]{:S(2)}) collective-permute-start(bf16[512,128]{1,0:T(8,128)(2,1)S(1)} %get-tuple-element.56), channel_id=1, source_target_pairs={{0,4},{2,6},{4,0},{6,2},{1,5},{3,7},{5,1},{7,3},{8,12},{10,14},{12... | collective-permute-start | bytes 393224 | tf_op jit(solution)/shard_map/ppermute | solution.py:380
  93.8 1.1 collective-permute-start.4
  94.9 9.1 %input_grads.1 = (f32[2048,512]{1,0:T(8,128)}, f32[8,512]{1,0:T(8,128)S(1)}) custom-call(f32[32,8,512]{2,1,0:T(8,128)S(1)} %all-to-all-done.1.back_ref, f32[2048,512]{1,0:T(8,128)} %get-tuple-element.31.pre_ref, f32[2048,512]{1,0:T(8,128)} %get-tuple-element.32.factor_ref, bf16[2048,128]{1,0:T(8,128)(2,1)} %inject_ref.7, bf16[4,512]{1,0:T(4,128)(2,1)S(1)} %copy-done.2), custom_call_target="tpu_custom_call" | custom-call | flops 536870912 | bytes 13631488 | tf_op jit(solution)/shard_map/input_grads/pallas_call | solution.py:387
  104.1 0.1 constant_dynamic-update-slice_fusion.3
  104.2 0.5 collective-permute-start.6
  104.7 0.8 collective-permute-start.7
  105.5 1.7 %collective-permute-start.8 = (bf16[512,128]{1,0:T(8,128)(2,1)S(1)}, bf16[512,128]{1,0:T(8,128)(2,1)S(1)}, u32[]{:S(2)}, u32[]{:S(2)}) collective-permute-start(bf16[512,128]{1,0:T(8,128)(2,1)S(1)} %get-tuple-element.52), channel_id=1, source_target_pairs={{0,6},{2,0},{4,2},{6,4},{1,7},{3,1},{5,3},{7,5},{8,14},{10,8},{12,... | collective-permute-start | bytes 393224 | tf_op jit(solution)/shard_map/ppermute | solution.py:380
  107.2 5.4 %collective-permute-done.6 = bf16[512,128]{1,0:T(8,128)(2,1)S(1)} collective-permute-done((bf16[512,128]{1,0:T(8,128)(2,1)S(1)}, bf16[512,128]{1,0:T(8,128)(2,1)S(1)}, u32[]{:S(2)}, u32[]{:S(2)}) %collective-permute-start.6) | collective-permute-done | bytes 131104 | tf_op jit(solution)/shard_map/ppermute | solution.py:380
  112.7 2.3 %collective-permute-start.9 = (bf16[2048,128]{1,0:T(8,128)(2,1)S(1)}, bf16[2048,128]{1,0:T(8,128)(2,1)S(1)}, u32[]{:S(2)}, u32[]{:S(2)}) collective-permute-start(bf16[2048,128]{1,0:T(8,128)(2,1)S(1)} %constant_dynamic-update-slice_fusion), channel_id=1, source_target_pairs={{0,1},{1,0},{2,3},{3,2},{4,5},{5,4},{6,7},{7,6},{8,9},{9,8},{10,11... | collective-permute-start | bytes 1572872 | tf_op jit(solution)/shard_map/ppermute | solution.py:415
  114.9 2.5 %collective-permute-start.5 = (f32[8,512]{1,0:T(8,128)S(1)}, f32[8,512]{1,0:T(8,128)S(1)}, u32[]{:S(2)}, u32[]{:S(2)}) collective-permute-start(f32[8,512]{1,0:T(8,128)S(1)} %get-tuple-element.45), channel_id=1, source_target_pairs={{8,0},{16,8},{24,16},{32,24},{40,32},{48,40},{56,48},{64,56},{72,6... | collective-permute-start | bytes 49160 | tf_op jit(solution)/shard_map/ppermute | solution.py:420
  117.5 4.1 %collective-permute-done.5 = f32[8,512]{1,0:T(8,128)S(1)} collective-permute-done((f32[8,512]{1,0:T(8,128)S(1)}, f32[8,512]{1,0:T(8,128)S(1)}, u32[]{:S(2)}, u32[]{:S(2)}) %collective-permute-start.5) | collective-permute-done | bytes 16416 | tf_op jit(solution)/shard_map/ppermute | solution.py:420
  121.5 1.4 %fusion = f32[2048,512]{1,0:T(8,128)} fusion(f32[2048,512]{1,0:T(8,128)} %get-tuple-element.33, f32[1,512]{1,0:T(1,128)S(1)} %get-tuple-element.59, f32[1,512]{1,0:T(1,128)S(1)} %get-tuple-element.60, f32[1,512]{1,0:T(1,128)S(1)} %get-tuple-element.58, f32[8]{0:T(128)S(1)} %pad.clone), kind=kLoop, calls=%fused_computation.9 | loop fusion | flops 16384 | bytes 38944 | tf_op jit(solution)/shard_map/dynamic_update_slice | solution.py:427
  122.9 1.5 %select_convert_fusion = (f32[2048,128]{1,0:T(8,128)}, f32[2048,128]{1,0:T(8,128)}) fusion(bf16[2048,128]{1,0:T(8,128)(2,1)S(1)} %collective-permute-done.9, bf16[2048,128]{1,0:T(8,128)(2,1)S(1)} %constant_dynamic-update-slice_fusion, pred[]{:T(512)S(6)} %eq.3), kind=kLoop, calls=%fused_computation | loop fusion | flops 1048576 | bytes 3145729 | tf_op jit(solution)/shard_map/convert_element_type | solution.py:418
  (30 shorter events, 0.6 us)
Async XLA Ops:
  0.6 13.5 %copy-start = (bf16[2048,128]{1,0:T(8,128)(2,1)S(1)}, bf16[2048,128]{1,0:T(8,128)(2,1)}, u32[]{:S(2)}) copy-start(bf16[2048,128]{1,0:T(8,128)(2,1)} %inject_ref.7) | copy-start | bytes 1572868
  1.4 12.7 %collective-permute-start = (bf16[16,512]{1,0:T(8,128)(2,1)S(1)}, bf16[16,512]{1,0:T(8,128)(2,1)S(1)}, u32[]{:S(2)}, u32[]{:S(2)}) collective-permute-start(bf16[16,512]{1,0:T(8,128)(2,1)S(1)} %slice.30), channel_id=1, source_target_pairs={{0,8},{8,16},{16,24},{24,32},{32,40},{40,48},{48,56},{56,64},{64,7... | collective-permute-start | bytes 49160 | tf_op jit(solution)/shard_map/ppermute | solution.py:266
  5.9 1.1 copy-start.1
  7.0 7.1 %copy-start.2 = (bf16[4,512]{1,0:T(4,128)(2,1)S(1)}, bf16[4,512]{1,0:T(4,128)(2,1)}, u32[]{:S(2)}) copy-start(bf16[4,512]{1,0:T(4,128)(2,1)} %weight_ref.5) | copy-start | bytes 12292
  23.5 28.6 %all-to-all-start = ((f32[32,8,640]{2,1,0:T(8,128)}), f32[32,8,640]{2,1,0:T(8,128)S(1)}, u32[]{:S(2)}, u32[]{:S(2)}) async-start(f32[32,8,640]{2,1,0:T(8,128)} %get-tuple-element.27), calls=%async_computation | async-start | bytes 1310720 | tf_op jit(solution)/shard_map/all_to_all | solution.py:321
  53.0 20.7 %all-to-all-start.1 = ((f32[32,8,512]{2,1,0:T(8,128)}), f32[32,8,512]{2,1,0:T(8,128)S(1)}, u32[]{:S(2)}, u32[]{:S(2)}) async-start(f32[32,8,512]{2,1,0:T(8,128)} %carry.1), calls=%async_computation.1 | async-start | bytes 1048576 | tf_op jit(solution)/shard_map/all_to_all | solution.py:356
  82.5 5.8 %collective-permute-start.1 = (f32[2048,128]{1,0:T(8,128)}, f32[2048,128]{1,0:T(8,128)S(1)}, u32[]{:S(2)}, u32[]{:S(2)}) collective-permute-start(f32[2048,128]{1,0:T(8,128)} %get-tuple-element.43), channel_id=1, source_target_pairs={{0,1},{1,0},{2,3},{3,2},{4,5},{5,4},{6,7},{7,6},{8,9},{9,8},{10,11... | collective-permute-start | bytes 3145736 | tf_op jit(solution)/shard_map/ppermute | solution.py:375
  89.8 14.2 %collective-permute-start.2 = (bf16[512,128]{1,0:T(8,128)(2,1)S(1)}, bf16[512,128]{1,0:T(8,128)(2,1)S(1)}, u32[]{:S(2)}, u32[]{:S(2)}) collective-permute-start(bf16[512,128]{1,0:T(8,128)(2,1)S(1)} %get-tuple-element.57), channel_id=1, source_target_pairs={{0,2},{2,4},{4,6},{6,0},{1,3},{3,5},{5,7},{7,1},{8,10},{10,12},{12... | collective-permute-start | bytes 393224 | tf_op jit(solution)/shard_map/ppermute | solution.py:380
  91.2 12.8 %collective-permute-start.3 = (bf16[512,128]{1,0:T(8,128)(2,1)S(1)}, bf16[512,128]{1,0:T(8,128)(2,1)S(1)}, u32[]{:S(2)}, u32[]{:S(2)}) collective-permute-start(bf16[512,128]{1,0:T(8,128)(2,1)S(1)} %get-tuple-element.56), channel_id=1, source_target_pairs={{0,4},{2,6},{4,0},{6,2},{1,5},{3,7},{5,1},{7,3},{8,12},{10,14},{12... | collective-permute-start | bytes 393224 | tf_op jit(solution)/shard_map/ppermute | solution.py:380
  93.8 10.2 %collective-permute-start.4 = (bf16[512,128]{1,0:T(8,128)(2,1)S(1)}, bf16[512,128]{1,0:T(8,128)(2,1)S(1)}, u32[]{:S(2)}, u32[]{:S(2)}) collective-permute-start(bf16[512,128]{1,0:T(8,128)(2,1)S(1)} %get-tuple-element.55), channel_id=1, source_target_pairs={{0,6},{2,0},{4,2},{6,4},{1,7},{3,1},{5,3},{7,5},{8,14},{10,8},{12,... | collective-permute-start | bytes 393224 | tf_op jit(solution)/shard_map/ppermute | solution.py:380
  104.2 8.4 %collective-permute-start.6 = (bf16[512,128]{1,0:T(8,128)(2,1)S(1)}, bf16[512,128]{1,0:T(8,128)(2,1)S(1)}, u32[]{:S(2)}, u32[]{:S(2)}) collective-permute-start(bf16[512,128]{1,0:T(8,128)(2,1)S(1)} %get-tuple-element.52), channel_id=1, source_target_pairs={{0,2},{2,4},{4,6},{6,0},{1,3},{3,5},{5,7},{7,1},{8,10},{10,12},{12... | collective-permute-start | bytes 393224 | tf_op jit(solution)/shard_map/ppermute | solution.py:380
  104.7 7.9 %collective-permute-start.7 = (bf16[512,128]{1,0:T(8,128)(2,1)S(1)}, bf16[512,128]{1,0:T(8,128)(2,1)S(1)}, u32[]{:S(2)}, u32[]{:S(2)}) collective-permute-start(bf16[512,128]{1,0:T(8,128)(2,1)S(1)} %get-tuple-element.52), channel_id=1, source_target_pairs={{0,4},{2,6},{4,0},{6,2},{1,5},{3,7},{5,1},{7,3},{8,12},{10,14},{12... | collective-permute-start | bytes 393224 | tf_op jit(solution)/shard_map/ppermute | solution.py:380
  105.5 7.2 %collective-permute-start.8 = (bf16[512,128]{1,0:T(8,128)(2,1)S(1)}, bf16[512,128]{1,0:T(8,128)(2,1)S(1)}, u32[]{:S(2)}, u32[]{:S(2)}) collective-permute-start(bf16[512,128]{1,0:T(8,128)(2,1)S(1)} %get-tuple-element.52), channel_id=1, source_target_pairs={{0,6},{2,0},{4,2},{6,4},{1,7},{3,1},{5,3},{7,5},{8,14},{10,8},{12,... | collective-permute-start | bytes 393224 | tf_op jit(solution)/shard_map/ppermute | solution.py:380
  112.7 10.3 %collective-permute-start.9 = (bf16[2048,128]{1,0:T(8,128)(2,1)S(1)}, bf16[2048,128]{1,0:T(8,128)(2,1)S(1)}, u32[]{:S(2)}, u32[]{:S(2)}) collective-permute-start(bf16[2048,128]{1,0:T(8,128)(2,1)S(1)} %constant_dynamic-update-slice_fusion), channel_id=1, source_target_pairs={{0,1},{1,0},{2,3},{3,2},{4,5},{5,4},{6,7},{7,6},{8,9},{9,8},{10,11... | collective-permute-start | bytes 1572872 | tf_op jit(solution)/shard_map/ppermute | solution.py:415
  114.9 6.6 %collective-permute-start.5 = (f32[8,512]{1,0:T(8,128)S(1)}, f32[8,512]{1,0:T(8,128)S(1)}, u32[]{:S(2)}, u32[]{:S(2)}) collective-permute-start(f32[8,512]{1,0:T(8,128)S(1)} %get-tuple-element.45), channel_id=1, source_target_pairs={{8,0},{16,8},{24,16},{32,24},{40,32},{48,40},{56,48},{64,56},{72,6... | collective-permute-start | bytes 49160 | tf_op jit(solution)/shard_map/ppermute | solution.py:420

commit v3 on v2

v3 whole, which is shorter than its diff:
```python
import functools

import jax
import jax.numpy as jnp
from jax import lax
from jax.experimental import pallas as pl
from jax.experimental.pallas import tpu as pltpu
from jax.sharding import Mesh
from jax.sharding import PartitionSpec as P

f32, bf16 = jnp.float32, jnp.bfloat16
SPAN = 256
SEQ, HG = ("z", "x"), ("y", "c")
PREV = 16

NN = (((1,), (0,)), ((), ()))
NT = (((1,), (1,)), ((), ()))
TN = (((0,), (0,)), ((), ()))


def dot(a, b, dims):
    return lax.dot_general(a, b, dims, preferred_element_type=f32)


def split(v):
    high = v.astype(bf16)
    return high, (v - high.astype(f32)).astype(bf16)


def dot2(exact, v, dims):
    high, low = split(v)
    return dot(exact, high, dims) + dot(exact, low, dims)


def dot3(ah, al, bh, bl, dims):
    return dot(ah, bh, dims) + (dot(ah, bl, dims) + dot(al, bh, dims))


def places():
    return lax.broadcasted_iota(jnp.int32, (SPAN, 1), 0).astype(f32)


def span_at(span):
    return pl.ds(pl.multiple_of(span * SPAN, SPAN), SPAN)


def each_span(spans, step, backwards=False):
    def visit(i, _):
        step(spans - 1 - i if backwards else i)
        return 0

    lax.fori_loop(0, spans, visit, 0)


def by_span(source, target, sems):
    def piece(span):
        if len(source.shape) == 3:
            return pltpu.make_async_copy(source.at[span], target.at[span], sems.at[span])
        rows = span_at(span)
        return pltpu.make_async_copy(source.at[rows, :], target.at[rows, :], sems.at[span])

    return piece


def fetch(spans, whole, pieces, backwards=False):
    for copy in whole:
        copy.start()
    for i in range(spans):
        for piece in pieces:
            piece(spans - 1 - i if backwards else i).start()
    for copy in whole:
        copy.wait()


def drain(spans, pieces):
    for span in range(spans):
        for piece in pieces:
            piece(span).wait()


def grads_kernel(
    code_hbm, grad_hbm, read_hbm, rate_ref, prior_ref, later_ref, log_ref, carry,
    code_ref, grad_ref, read_ref, csem, gsem, rsem,
):
    heads, spans = code_ref.shape
    channels = carry.shape[1]
    pieces = [by_span(grad_hbm, grad_ref, gsem), by_span(read_hbm, read_ref, rsem)]
    fetch(spans, [pltpu.make_async_copy(code_hbm, code_ref, csem)], pieces, backwards=True)
    logs = jnp.log1p(-code_ref[...].astype(f32) * 1e-6)
    lane = lax.broadcasted_iota(jnp.int32, (heads, channels), 1)
    row = lax.broadcasted_iota(jnp.int32, (heads, channels), 0)
    width = channels // heads
    owns = jnp.where((lane >= row * width) & (lane < (row + 1) * width), 1.0, 0.0)
    rate_ref[...] = lax.dot_general(
        logs, owns, TN, precision=lax.Precision.HIGHEST, preferred_element_type=f32
    )
    total = jnp.zeros((1, channels), f32)
    for span in range(spans):
        prior_ref[span : span + 1, :] = total
        total = total + SPAN * rate_ref[span : span + 1, :]
    log_ref[...] = total
    total = jnp.zeros((1, channels), f32)
    for span in reversed(range(spans)):
        later_ref[span : span + 1, :] = total
        total = total + SPAN * rate_ref[span : span + 1, :]
    carry[...] = jnp.zeros_like(carry)

    def step(span):
        for piece in pieces:
            piece(span).wait()
        rate = rate_ref[pl.ds(span, 1), :]
        up = grad_ref[span_at(span), :].astype(f32) * jnp.exp(places() * rate)
        fresh = dot2(read_ref[span_at(span), :], up, TN)
        carry[...] = jnp.exp(SPAN * rate) * carry[...] + jnp.exp(rate) * fresh

    each_span(spans, step, backwards=True)


def convolved(x, before, weights):
    rows = jnp.concatenate([before, x], axis=0)
    preact = weights[0:1] * pltpu.roll(rows, 3, axis=0)[8:]
    for k in range(1, 3):
        preact = preact + weights[k : k + 1] * pltpu.roll(rows, 3 - k, axis=0)[8:]
    return preact + weights[3:4] * x


def states_kernel(
    x_hbm, halo_hbm, inject_hbm, rate_hbm, weight_hbm, own_grad_hbm, log_hbm,
    pay_ref,
    x_ref, halo_ref, inject_ref, rate_ref, weight_ref, own_grad_ref, log_ref, carry, prev,
    xsem, isem, sems,
):
    spans = rate_ref.shape[0]
    pieces = [by_span(x_hbm, x_ref, xsem), by_span(inject_hbm, inject_ref, isem)]
    late = pltpu.make_async_copy(own_grad_hbm, own_grad_ref, sems.at[4])
    fetch(
        spans,
        [
            pltpu.make_async_copy(halo_hbm, halo_ref, sems.at[0]),
            pltpu.make_async_copy(rate_hbm, rate_ref, sems.at[1]),
            pltpu.make_async_copy(weight_hbm, weight_ref, sems.at[2]),
            pltpu.make_async_copy(log_hbm, log_ref, sems.at[3]),
        ],
        pieces,
    )
    late.start()
    carry[...] = jnp.zeros_like(carry)
    prev[...] = halo_ref[...].astype(f32)[PREV - 8 :]
    weights = weight_ref[...].astype(f32)

    def step(span):
        for piece in pieces:
            piece(span).wait()
        x = x_ref[span_at(span), :].astype(f32)
        preact = convolved(x, prev[...], weights)
        prev[...] = x[SPAN - 8 :]
        act = (preact * jax.nn.sigmoid(preact)).astype(bf16)
        rate = rate_ref[pl.ds(span, 1), :]
        tail = jnp.exp((SPAN - 1.0 - places()) * rate)
        fresh = dot2(inject_ref[span_at(span), :], act.astype(f32) * tail, TN)
        carry[...] = jnp.exp(SPAN * rate) * carry[...] + fresh

    each_span(spans, step)
    late.wait()
    chunks, height, _ = pay_ref.shape
    half = carry.shape[1] // 2
    for d in range(chunks):
        r, l = height * (d // 2), half * (d % 2)
        pay_ref[d, :, 0:half] = carry[r : r + height, l : l + half]
        pay_ref[d, :, half : 2 * half] = own_grad_ref[r : r + height, l : l + half]
        for row in range(half // 128):
            at = l + 128 * row
            pay_ref[d, row : row + 1, 2 * half : 2 * half + 128] = log_ref[:, at : at + 128]


def scan_kernel(own_ref, out_ref):
    chunks, height, width = out_ref.shape
    half = width // 2

    def gain(e):
        logs = [own_ref[e, r : r + 1, width : width + 128] for r in range(half // 128)]
        return jnp.exp(jnp.concatenate(logs, axis=1))

    state = jnp.zeros((height, half), f32)
    grad = jnp.zeros((height, half), f32)
    for e in range(chunks):
        out_ref[e, :, 0:half] = state
        state = gain(e) * state + own_ref[e, :, 0:half]
    for e in reversed(range(chunks)):
        out_ref[e, :, half:width] = grad
        grad = gain(e) * grad + own_ref[e, :, half:width]


def causal():
    row = lax.broadcasted_iota(jnp.int32, (SPAN, SPAN), 0)
    return row >= lax.broadcasted_iota(jnp.int32, (SPAN, SPAN), 1)


def local_input_kernel(
    x_hbm, halo_hbm, grad_hbm, inject_hbm, read_hbm, rate_hbm, later_hbm, weight_hbm,
    act_hbm, pre_hbm, factor_hbm, after_hbm,
    x_ref, halo_ref, grad_ref, inject_ref, read_ref, rate_ref, later_ref, weight_ref,
    act_ref, pre_ref, factor_ref, after_ref, carry,
    xsem, gsem, isem, rsem, sems, osems,
):
    spans = rate_ref.shape[0]
    pieces = [
        by_span(x_hbm, x_ref, xsem), by_span(grad_hbm, grad_ref, gsem),
        by_span(inject_hbm, inject_ref, isem), by_span(read_hbm, read_ref, rsem),
    ]
    outs = [
        by_span(act_ref, act_hbm, osems.at[0]), by_span(pre_ref, pre_hbm, osems.at[1]),
        by_span(factor_ref, factor_hbm, osems.at[2]), by_span(after_ref, after_hbm, osems.at[3]),
    ]
    fetch(
        spans,
        [
            pltpu.make_async_copy(halo_hbm, halo_ref, sems.at[0]),
            pltpu.make_async_copy(rate_hbm, rate_ref, sems.at[1]),
            pltpu.make_async_copy(weight_hbm, weight_ref, sems.at[2]),
            pltpu.make_async_copy(later_hbm, later_ref, sems.at[3]),
        ],
        pieces,
        backwards=True,
    )
    carry[...] = jnp.zeros_like(carry)
    weights = weight_ref[...].astype(f32)
    pieces[0](spans - 1).wait()

    def step(span):
        @pl.when(span > 0)
        def _():
            pieces[0](jnp.maximum(span - 1, 0)).wait()

        for piece in pieces[1:]:
            piece(span).wait()
        rows = span_at(span)
        x = x_ref[rows, :].astype(f32)
        start = pl.multiple_of(jnp.maximum(span * SPAN - PREV, 0), PREV)
        last = jnp.where(span == 0, halo_ref[...].astype(f32), x_ref[pl.ds(start, PREV), :].astype(f32))
        preact = convolved(x, last[PREV - 8 :], weights)
        squashed = jax.nn.sigmoid(preact)
        act_ref[rows, :] = (preact * squashed).astype(bf16)
        slope = squashed * (1.0 + preact * (1.0 - squashed))
        rate = rate_ref[pl.ds(span, 1), :]
        later = jnp.exp(later_ref[pl.ds(span, 1), :])
        inject, read = inject_ref[rows, :], read_ref[rows, :]
        here = places()
        steep = slope * jnp.exp(-here * rate)
        end = jnp.exp((SPAN - 1.0) * rate)
        up_high, up_low = split(grad_ref[rows, :].astype(f32) * jnp.exp(here * rate))
        mixing = jnp.where(causal(), dot(read, inject, NT), 0.0).astype(bf16)
        after = carry[...]
        after_ref[span] = after
        stacked = jnp.concatenate(split(after * end), axis=0)
        doubled = jnp.concatenate([inject, inject], axis=1)
        pre_ref[rows, :] = steep * (dot(mixing, up_high, TN) + dot(doubled, stacked, NN))
        factor_ref[rows, :] = steep * (end * later)
        fresh = dot(read, up_high, TN) + dot(read, up_low, TN)
        carry[...] = jnp.exp(SPAN * rate) * after + jnp.exp(rate) * fresh
        for out in outs:
            out(span).start()

    each_span(spans, step, backwards=True)
    drain(spans, outs)


def wide_product(high, low, both, states):
    wide = dot(high, both, NT)
    return wide[:, :states] + (wide[:, states:] + dot(low, both[0:states, :], NT))


def local_shared_kernel(
    grad_hbm, act_hbm, inject_hbm, read_hbm, after_hbm, rate_hbm, prior_hbm, later_hbm,
    adh_hbm, adl_hbm, gdh_hbm, gdl_hbm, gi_hbm, gr_hbm,
    grad_ref, act_ref, inject_ref, read_ref, after_ref, rate_ref, prior_ref, later_ref,
    adh_ref, adl_ref, gdh_ref, gdl_ref, gi_ref, gr_ref, carry,
    isems, sems, osems,
):
    spans = rate_ref.shape[0]
    sources = [grad_hbm, act_hbm, inject_hbm, read_hbm, after_hbm]
    targets = [grad_ref, act_ref, inject_ref, read_ref, after_ref]
    pieces = [by_span(a, b, isems.at[k]) for k, (a, b) in enumerate(zip(sources, targets))]
    made = [adh_ref, adl_ref, gdh_ref, gdl_ref, gi_ref, gr_ref]
    places_to = [adh_hbm, adl_hbm, gdh_hbm, gdl_hbm, gi_hbm, gr_hbm]
    outs = [by_span(a, b, osems.at[k]) for k, (a, b) in enumerate(zip(made, places_to))]
    fetch(
        spans,
        [
            pltpu.make_async_copy(rate_hbm, rate_ref, sems.at[0]),
            pltpu.make_async_copy(prior_hbm, prior_ref, sems.at[1]),
            pltpu.make_async_copy(later_hbm, later_ref, sems.at[2]),
        ],
        pieces,
    )
    carry[...] = jnp.zeros_like(carry)

    def step(span):
        for piece in pieces:
            piece(span).wait()
        rows = span_at(span)
        rate = rate_ref[pl.ds(span, 1), :]
        later = later_ref[pl.ds(span, 1), :]
        prior = prior_ref[pl.ds(span, 1), :]
        inject, read = inject_ref[rows, :], read_ref[rows, :]
        states = inject.shape[1]
        here = places()
        up = grad_ref[rows, :].astype(f32) * jnp.exp(here * rate)
        down = act_ref[rows, :].astype(f32) * jnp.exp(-here * rate)
        uph, upl = split(up)
        downh, downl = split(down)
        pairs = jnp.where(causal(), dot(uph, downh, NT), 0.0).astype(bf16)
        end = jnp.exp((SPAN - 1.0) * rate)
        afters = jnp.concatenate(split(after_ref[span] * end), axis=0)
        before = carry[...]
        befores = jnp.concatenate(split(before * jnp.exp(rate)), axis=0)
        gi_ref[rows, :] = dot(pairs, read, TN) + wide_product(downh, downl, afters, states)
        gr_ref[rows, :] = dot(pairs, inject, NN) + wide_product(uph, upl, befores, states)
        fresh = dot(inject, downh, TN) + dot(inject, downl, TN)
        carry[...] = jnp.exp(SPAN * rate) * before + end * fresh
        adh_ref[rows, :], adl_ref[rows, :] = split(down * jnp.exp((SPAN - 1.0) * rate + later))
        gdh_ref[rows, :], gdl_ref[rows, :] = split(up * jnp.exp(rate + prior))
        for out in outs:
            out(span).start()

    each_span(spans, step)
    drain(spans, outs)


def unpacked(back_ref, high, low, grads):
    chunks, height, width = back_ref.shape
    half = width // 2
    start = half if grads else 0
    states = high.shape[0] // 2 if low is None else high.shape[0]
    for d in range(chunks):
        r, l = height * (d // 2), half * (d % 2)
        h, w = split(back_ref[d, :, start : start + half])
        high[r : r + height, l : l + half] = h
        if low is None:
            high[states + r : states + r + height, l : l + half] = w
        else:
            low[r : r + height, l : l + half] = w


def shared_kernel(
    core_ref, back_ref, adh_hbm, adl_hbm, gdh_hbm, gdl_hbm, gi_hbm, gr_hbm,
    mine_ref, theirs_ref,
    adh_ref, adl_ref, gdh_ref, gdl_ref, gi_ref, gr_ref, grads, carried, isems,
):
    tokens, states = gi_ref.shape
    spans = tokens // SPAN
    sources = [adh_hbm, adl_hbm, gdh_hbm, gdl_hbm, gi_hbm, gr_hbm]
    targets = [adh_ref, adl_ref, gdh_ref, gdl_ref, gi_ref, gr_ref]
    pieces = [by_span(a, b, isems.at[k]) for k, (a, b) in enumerate(zip(sources, targets))]
    fetch(spans, [], pieces)
    unpacked(back_ref, grads, None, True)
    unpacked(back_ref, carried, None, False)
    first = core_ref[0] == 0

    def step(span):
        for piece in pieces:
            piece(span).wait()
        rows = span_at(span)
        gi = gi_ref[rows, :] + wide_product(adh_ref[rows, :], adl_ref[rows, :], grads[...], states)
        gr = gr_ref[rows, :] + wide_product(gdh_ref[rows, :], gdl_ref[rows, :], carried[...], states)
        mine_ref[rows, :] = jnp.where(first, gi, gr)
        theirs_ref[rows, :] = jnp.where(first, gr, gi)

    each_span(spans, step)


def input_kernel(
    back_ref, pre_hbm, factor_hbm, inject_hbm, weight_ref,
    out_hbm, first_ref,
    pre_ref, factor_ref, inject_ref, grads, after, made, isems, osems,
):
    spans = pre_ref.shape[0] // SPAN
    pieces = [
        by_span(pre_hbm, pre_ref, isems.at[0]), by_span(factor_hbm, factor_ref, isems.at[1]),
        by_span(inject_hbm, inject_ref, isems.at[2]),
    ]
    out = by_span(made, out_hbm, osems)
    fetch(spans, [], pieces, backwards=True)
    unpacked(back_ref, grads, None, True)
    after[...] = jnp.zeros_like(after)
    weights = weight_ref[...].astype(f32)

    def step(span):
        for piece in pieces:
            piece(span).wait()
        rows = span_at(span)
        inject = inject_ref[rows, :]
        carried = dot(jnp.concatenate([inject, inject], axis=1), grads[...], NN)
        now = pre_ref[rows, :] + factor_ref[rows, :] * carried
        joined = jnp.concatenate([now, after[...]], axis=0)
        summed = weights[3:4] * now
        for k in range(3):
            ahead = pltpu.roll(joined, SPAN + 8 - (3 - k), axis=0)[:SPAN]
            summed = summed + weights[k : k + 1] * ahead
        after[...] = now[0:8]
        made[rows, :] = summed
        out(span).start()

    each_span(spans, step, backwards=True)
    first_ref[...] = after[...]
    drain(spans, [out])


def params(mib=53):
    return pltpu.CompilerParams(vmem_limit_bytes=mib << 20)


def cost(flops, nbytes):
    return pl.CostEstimate(flops=flops, bytes_accessed=nbytes, transcendentals=0)


def body(nseq, ny, nc, conv_input, grad_output, inject, readout, conv_weight, decay_codes):
    tokens, channels = conv_input.shape
    spans = decay_codes.shape[1]
    states = inject.shape[1]
    shape = jax.ShapeDtypeStruct
    height = 2 * states // nseq
    chunk = (nseq, height, channels)
    smem = pl.BlockSpec(memory_space=pltpu.SMEM)
    wide, wide16 = shape((tokens, channels), f32), shape((tokens, channels), bf16)
    narrow, row = shape((tokens, states), f32), shape((spans, channels), f32)
    local = shape((spans, states, channels), f32)
    state = shape((states, channels), f32)

    up = [(i, i + 1) for i in range(nseq - 1)]
    down = [(i + 1, i) for i in range(nseq - 1)]
    halo = lax.ppermute(conv_input[tokens - PREV :], SEQ, up)

    anywhere = pl.BlockSpec(memory_space=pl.ANY)
    hbm = pl.BlockSpec(memory_space=pltpu.HBM)
    plain = pl.BlockSpec()
    wide_v, wide16_v = pltpu.VMEM(wide.shape, f32), pltpu.VMEM(wide.shape, bf16)
    narrow_v, narrow16_v = pltpu.VMEM(narrow.shape, f32), pltpu.VMEM(narrow.shape, bf16)
    row_v, state_v = pltpu.VMEM(row.shape, f32), pltpu.VMEM(state.shape, f32)
    local_v = pltpu.VMEM(local.shape, f32)
    halo_v, weight_v = pltpu.VMEM((PREV, channels), bf16), pltpu.VMEM(conv_weight.shape, bf16)
    dma = pltpu.SemaphoreType.DMA

    rates, prior, later, own_log, own_grad = pl.pallas_call(
        grads_kernel,
        in_specs=[hbm] * 3,
        out_specs=[plain] * 5,
        out_shape=[row, row, row, shape((1, channels), f32), state],
        scratch_shapes=[
            pltpu.VMEM(decay_codes.shape, jnp.int32), wide16_v, narrow16_v,
            dma, dma((spans,)), dma((spans,)),
        ],
        compiler_params=params(),
        cost_estimate=cost(4 * tokens * channels * states, 3 << 20),
        name="own_grads",
    )(decay_codes, grad_output, readout)

    payload = pl.pallas_call(
        states_kernel,
        in_specs=[hbm, anywhere, hbm, anywhere, hbm, anywhere, anywhere],
        out_specs=plain,
        out_shape=shape((nseq, height, channels + 128), f32),
        scratch_shapes=[
            wide16_v, halo_v, narrow16_v, row_v, weight_v, state_v, pltpu.VMEM((1, channels), f32),
            state_v, pltpu.VMEM((8, channels), f32), dma((spans,)), dma((spans,)), dma((5,)),
        ],
        compiler_params=params(),
        cost_estimate=cost(4 * tokens * channels * states, 4 << 20),
        name="own_states",
    )(conv_input, halo, inject, rates, conv_weight, own_grad, own_log)

    arrived = lax.all_to_all(payload, SEQ, 0, 0, tiled=True)

    act, pre, factor, after = pl.pallas_call(
        local_input_kernel,
        in_specs=[hbm, anywhere, hbm, hbm, hbm, anywhere, anywhere, hbm],
        out_specs=[hbm] * 4,
        out_shape=[wide16, wide, wide, local],
        scratch_shapes=[
            wide16_v, halo_v, wide16_v, narrow16_v, narrow16_v, row_v, row_v, weight_v,
            wide16_v, wide_v, wide_v, local_v, state_v,
        ]
        + [dma((spans,))] * 4 + [dma((4,)), dma((4, spans))],
        compiler_params=params(),
        cost_estimate=cost(8 * tokens * channels * SPAN, 18 << 20),
        name="local_input",
    )(conv_input, halo, grad_output, inject, readout, rates, later, conv_weight)
    arrived, act = lax.optimization_barrier((arrived, act))

    adh, adl, gdh, gdl, gi, gr = pl.pallas_call(
        local_shared_kernel,
        in_specs=[hbm] * 5 + [anywhere] * 3,
        out_specs=[hbm] * 6,
        out_shape=[wide16] * 4 + [narrow] * 2,
        scratch_shapes=[wide16_v] * 2 + [narrow16_v] * 2 + [local_v] + [row_v] * 3
        + [wide16_v] * 4 + [narrow_v] * 2 + [state_v]
        + [dma((5, spans)), dma((3,)), dma((6, spans))],
        compiler_params=params(),
        cost_estimate=cost(12 * tokens * channels * SPAN, 19 << 20),
        name="local_shared",
    )(grad_output, act, inject, readout, after, rates, prior, later)

    scanned = pl.pallas_call(
        scan_kernel,
        out_shape=shape(chunk, f32),
        compiler_params=params(8),
        cost_estimate=cost(1 << 18, 1 << 20),
        name="carry",
    )(arrived)
    returned = lax.all_to_all(scanned, SEQ, 0, 0, tiled=True)

    core = lax.axis_index("c").astype(jnp.int32).reshape(1)
    stacked = pltpu.VMEM((2 * states, channels), bf16)
    mine, theirs = pl.pallas_call(
        shared_kernel,
        in_specs=[smem, plain] + [hbm] * 6,
        out_specs=[plain] * 2,
        out_shape=[narrow] * 2,
        scratch_shapes=[wide16_v] * 4 + [narrow_v] * 2 + [stacked] * 2 + [dma((6, spans))],
        compiler_params=params(),
        cost_estimate=cost(12 * tokens * channels * states, 13 << 20),
        name="shared_terms",
    )(core, returned, adh, adl, gdh, gdl, gi, gr)

    swap = [(i, i ^ 1) for i in range(nc)]
    chip = mine + lax.ppermute(theirs, "c", swap)
    here = lax.axis_index("y")
    part = tokens // ny

    def turn(array, by):
        return lax.ppermute(array, "y", [(i, (i + by) % ny) for i in range(ny)])

    def cut(array, which):
        return lax.dynamic_slice_in_dim(array, lax.rem(here + which, ny) * part, part)

    sent = [turn(cut(chip, by).astype(bf16), by) for by in range(1, ny)]

    grad_input, first = pl.pallas_call(
        input_kernel,
        in_specs=[plain] + [hbm] * 3 + [plain],
        out_specs=[hbm, plain],
        out_shape=[wide, shape((8, channels), f32)],
        scratch_shapes=[
            wide_v, wide_v, narrow16_v, stacked, pltpu.VMEM((8, channels), f32), wide_v,
            dma((3, spans)), dma((spans,)),
        ],
        compiler_params=params(),
        cost_estimate=cost(4 * tokens * channels * states, 13 << 20),
        name="input_grads",
    )(returned, pre, factor, inject, conv_weight)

    *sent, first = lax.optimization_barrier((*sent, first))
    quarter = cut(chip, 0)
    for piece in sent:
        quarter = quarter + piece.astype(f32)
    quarter = quarter.astype(bf16)
    turned = [turn(quarter, by) for by in range(1, ny)]
    next_rows = lax.ppermute(first, SEQ, down)
    *turned, next_rows = lax.optimization_barrier((*turned, next_rows))
    done = jnp.zeros((tokens, states), bf16)
    for by, piece in enumerate([quarter] + turned):
        done = lax.dynamic_update_slice_in_dim(
            done, piece, lax.rem(here - by + ny, ny) * part, 0
        )
    other = lax.ppermute(done, "c", swap)
    mine_is_first = lax.axis_index("c") == 0
    grad_inject = jnp.where(mine_is_first, done, other).astype(f32)
    grad_readout = jnp.where(mine_is_first, other, done).astype(f32)

    weights = conv_weight.astype(f32)
    tail_rows = []
    for row in range(3):
        tail_rows.append(sum(weights[k] * next_rows[row - k] for k in range(row + 1)))
    patch = jnp.concatenate([jnp.zeros((5, channels), f32), jnp.stack(tail_rows)], axis=0)
    last = lax.slice_in_dim(grad_input, tokens - 8, tokens) + patch
    grad_input = lax.dynamic_update_slice(grad_input, last, (tokens - 8, 0))
    return grad_input, grad_inject, grad_readout


def build(devices, sizes):
    fine = Mesh(devices.reshape(sizes), ("z", "x", "y", "c"))
    nz, nx, ny, nc = sizes
    return jax.shard_map(
        functools.partial(body, nz * nx, ny, nc),
        mesh=fine,
        in_specs=(P(SEQ, HG), P(SEQ, HG), P(SEQ, None), P(SEQ, None), P(None, HG), P(HG, SEQ)),
        out_specs=(P(SEQ, HG), P(SEQ, None), P(SEQ, None)),
        check_vma=False,
    )


def solution(mesh):
    return build(mesh.devices, (8, 4, 4, 2))
```

time: 127 us -> 111 us (0.87); the launches traced: 124 us -> 110 us
  Pallas kernels: 59.1 us -> 46.9 us
  waiting for transfers between devices: 20.9 us -> 18.2 us
  starting transfers between devices: 35.8 us -> 37.3 us
    pallas_call x6, Pallas kernels: 58.2 us -> 46 us  [the longest x1 11.3 us: body(): pl.pallas_call(local_shared_kernel, in_specs=[hbm] * 5 + [anywhere] * 3,...]
    ppermute x6, waiting for transfers between devices: 5.43 us -> 0.02 us  [turn(): return lax.ppermute(array, 'y', [(i, (i + by) % ny) for i in range(ny)])]
    all_to_all x1, waiting for transfers between devices: 4.96 us -> 8 us  [body(): arrived = lax.all_to_all(payload, SEQ, 0, 0, tiled=True)]
    ppermute x1, starting transfers between devices: 2.25 us -> 3.55 us  [body(): other = lax.ppermute(done, 'c', swap)]
  transfers between devices with their start and end apart: 12 -> 12, of which waited for: 5 -> 5; matrix products, arithmetic and copies ran while one was open for 2% -> 1% of each run, Pallas kernels for 32% -> 29%
where the time goes in v3:
time: 111 us; the launch traced here: 110 us
  Pallas kernels  46.9 us (42%)
  starting transfers between devices  37.3 us (34%)
  waiting for transfers between devices  18.2 us (16%)
  other arithmetic  4.38 us (4%)
  local copies, waits for them, and re-layouts  2.72 us (2%)
    pallas_call x1, Pallas kernels, body(): pl.pallas_call(local_shared_kernel, in_specs=[hbm] * 5 + [anywhere] * 3,...  11.3 us
    all_to_all x1, starting transfers between devices, body(): arrived = lax.all_to_all(payload, SEQ, 0, 0, tiled=True)  10.4 us
    pallas_call x1, Pallas kernels, body(): pl.pallas_call(local_input_kernel, in_specs=[hbm, anywhere, hbm, hbm, hbm...  10.3 us
    ppermute x6, starting transfers between devices, turn(): return lax.ppermute(array, 'y', [(i, (i + by) % ny) for i in range(ny)])  8.13 us
    all_to_all x1, waiting for transfers between devices, body(): arrived = lax.all_to_all(payload, SEQ, 0, 0, tiled=True)  8 us
    pallas_call x1, Pallas kernels, body(): pl.pallas_call(states_kernel, in_specs=[hbm, anywhere, hbm, anywhere, hbm...  7.61 us
    pallas_call x1, Pallas kernels, body(): pl.pallas_call(shared_kernel, in_specs=[smem, plain] + [hbm] * 6, out_spe...  6.8 us
    pallas_call x1, Pallas kernels, body(): pl.pallas_call(input_kernel, in_specs=[plain] + [hbm] * 3 + [plain], out_...  5.99 us
  transfers between devices with their start and end apart: 12, of which 5 were waited for; matrix products, arithmetic and copies ran while one was open for 1% of the time, Pallas kernels for 29%

profile of v3, /device:TPU:7, one launch (start us, length us, event | category | flops | bytes accessed | tf_op | source)
XLA Modules:
  0.0 110.3 jit_solution(5149673371673370483)
XLA Ops:
  0.6 0.8 slice.30
  1.4 3.4 %collective-permute-start = (bf16[16,512]{1,0:T(8,128)(2,1)S(1)}, bf16[16,512]{1,0:T(8,128)(2,1)S(1)}, u32[]{:S(2)}, u32[]{:S(2)}) collective-permute-start(bf16[16,512]{1,0:T(8,128)(2,1)S(1)} %slice.30), channel_id=1, source_target_pairs={{0,8},{8,16},{16,24},{24,32},{32,40},{40,48},{48,56},{56,64},{64,7... | collective-permute-start | bytes 49160 | tf_op jit(solution)/shard_map/ppermute | solution.py:432
  4.9 1.0 copy-done.1
  5.9 0.7 copy-done.3
  6.6 4.0 %own_grads.1 = (f32[8,512]{1,0:T(8,128)S(1)}, f32[8,512]{1,0:T(8,128)S(1)}, f32[8,512]{1,0:T(8,128)S(1)}, f32[1,512]{1,0:T(1,128)S(1)}, f32[128,512]{1,0:T(8,128)S(1)}) custom-call(s32[8,8]{1,0:T(8,128)S(1)} %copy-done.3, bf16[2048,512]{1,0:T(8,128)(2,1)} %grad_hbm.5, bf16[2048,128]{1,0:T(8,128)(2,1)S(1)} %copy-done.1), custom_call_target="tpu_custom_call" | custom-call | flops 536870912 | bytes 3145728 | tf_op jit(solution)/shard_map/own_grads/pallas_call | solution.py:444
  10.7 7.6 %own_states.1 = f32[32,8,640]{2,1,0:T(8,128)} custom-call(bf16[2048,512]{1,0:T(8,128)(2,1)} %x_hbm.3, bf16[16,512]{1,0:T(8,128)(2,1)S(1)} %collective-permute-done.halo_hbm, bf16[2048,128]{1,0:T(8,128)(2,1)S(1)} %copy-done, f32[8,512]{1,0:T(8,128)S(1)} %get-tuple-element.32.rate_hbm, bf16[4,512]{1,0:T(4,128)(2,1)S(1)} %copy-done.2, ...), custom_call_target="tpu_custom_call" | custom-call | flops 536870912 | bytes 4194304 | tf_op jit(solution)/shard_map/own_states/pallas_call | solution.py:458
  18.3 10.4 %all-to-all-start = ((f32[32,8,640]{2,1,0:T(8,128)}), f32[32,8,640]{2,1,0:T(8,128)S(1)}, u32[]{:S(2)}, u32[]{:S(2)}) async-start(f32[32,8,640]{2,1,0:T(8,128)} %own_states.1), calls=%async_computation | async-start | bytes 1310720 | tf_op jit(solution)/shard_map/all_to_all | solution.py:472
  28.7 10.3 %local_input.1 = (bf16[2048,512]{1,0:T(8,128)(2,1)}, f32[2048,512]{1,0:T(8,128)}, f32[2048,512]{1,0:T(8,128)}, f32[8,128,512]{2,1,0:T(8,128)}) custom-call(bf16[2048,512]{1,0:T(8,128)(2,1)} %x_hbm.3, bf16[16,512]{1,0:T(8,128)(2,1)S(1)} %collective-permute-done.halo_hbm, bf16[2048,512]{1,0:T(8,128)(2,1)} %grad_hbm.5, bf16[2048,128]{1,0:T(8,128)(2,1)S(1)} %copy-done, ...), custom_call_target="tpu_custom_call" | custom-call | flops 2147483648 | bytes 18874368 | tf_op jit(solution)/shard_map/local_input/pallas_call | solution.py:474
  39.0 8.0 %all-to-all-done.own_ref = f32[32,8,640]{2,1,0:T(8,128)S(1)} async-done(((f32[32,8,640]{2,1,0:T(8,128)}), f32[32,8,640]{2,1,0:T(8,128)S(1)}, u32[]{:S(2)}, u32[]{:S(2)}) %all-to-all-start) | async-done | bytes 655392 | tf_op jit(solution)/shard_map/all_to_all | solution.py:472
  47.0 0.9 carry.1
  47.9 5.9 %all-to-all-start.1 = ((f32[32,8,512]{2,1,0:T(8,128)}), f32[32,8,512]{2,1,0:T(8,128)S(1)}, u32[]{:S(2)}, u32[]{:S(2)}) async-start(f32[32,8,512]{2,1,0:T(8,128)} %carry.1), calls=%async_computation.1 | async-start | bytes 1048576 | tf_op jit(solution)/shard_map/all_to_all | solution.py:510
  53.8 11.3 %local_shared.1 = (bf16[2048,512]{1,0:T(8,128)(2,1)}, bf16[2048,512]{1,0:T(8,128)(2,1)}, bf16[2048,512]{1,0:T(8,128)(2,1)}, bf16[2048,512]{1,0:T(8,128)(2,1)}, f32[2048,128]{1,0:T(8,128)}, /*index=5*/f32[2048,128]{1,0:T(8,128)}) custom-call(bf16[2048,512]{1,0:T(8,128)(2,1)} %grad_hbm.5, bf16[2048,512]{1,0:T(8,128)(2,1)} %get-tuple-element.41.act_hbm, ...), custom_call_target="tpu_custom_call" | custom-call | flops 3221225472 | bytes 19922944 | tf_op jit(solution)/shard_map/local_shared/pallas_call | solution.py:490
  65.1 3.5 %all-to-all-done.1.back_ref = f32[32,8,512]{2,1,0:T(8,128)S(1)} async-done(((f32[32,8,512]{2,1,0:T(8,128)}), f32[32,8,512]{2,1,0:T(8,128)S(1)}, u32[]{:S(2)}, u32[]{:S(2)}) %all-to-all-start.1) | async-done | bytes 524320 | tf_op jit(solution)/shard_map/all_to_all | solution.py:510
  68.6 6.8 %shared_terms.1 = (f32[2048,128]{1,0:T(8,128)}, f32[2048,128]{1,0:T(8,128)}) custom-call(s32[1]{0:T(128)} %bitcast.core_ref, f32[32,8,512]{2,1,0:T(8,128)S(1)} %all-to-all-done.1.back_ref, bf16[2048,512]{1,0:T(8,128)(2,1)} %get-tuple-element.44.adh_hbm, bf16[2048,512]{1,0:T(8,128)(2,1)} %get-tuple-element.45.adl_hbm, ...), custom_call_target="tpu_custom_call" | custom-call | flops 1610612736 | bytes 13631488 | tf_op jit(solution)/shard_map/shared_terms/pallas_call | solution.py:514
  75.4 3.4 %collective-permute-start.1 = (f32[2048,128]{1,0:T(8,128)}, f32[2048,128]{1,0:T(8,128)S(1)}, u32[]{:S(2)}, u32[]{:S(2)}) collective-permute-start(f32[2048,128]{1,0:T(8,128)} %get-tuple-element.51), channel_id=1, source_target_pairs={{0,1},{1,0},{2,3},{3,2},{4,5},{5,4},{6,7},{7,6},{8,9},{9,8},{10,11... | collective-permute-start | bytes 3145736 | tf_op jit(solution)/shard_map/ppermute | solution.py:526
  78.8 2.5 %collective-permute-done.1 = f32[2048,128]{1,0:T(8,128)S(1)} collective-permute-done((f32[2048,128]{1,0:T(8,128)}, f32[2048,128]{1,0:T(8,128)S(1)}, u32[]{:S(2)}, u32[]{:S(2)}) %collective-permute-start.1) | collective-permute-done | bytes 1048608 | tf_op jit(solution)/shard_map/ppermute | solution.py:526
  81.3 1.4 %add.69 = f32[2048,128]{1,0:T(8,128)S(1)} add(f32[2048,128]{1,0:T(8,128)} %get-tuple-element.50, f32[2048,128]{1,0:T(8,128)S(1)} %collective-permute-done.1) | non-fusion elementwise | flops 262144 | bytes 3145728 | tf_op jit(solution)/shard_map/add | solution.py:526
  82.7 1.4 %collective-permute-start.2 = (bf16[512,128]{1,0:T(8,128)(2,1)S(1)}, bf16[512,128]{1,0:T(8,128)(2,1)S(1)}, u32[]{:S(2)}, u32[]{:S(2)}) collective-permute-start(bf16[512,128]{1,0:T(8,128)(2,1)S(1)} %get-tuple-element.67), channel_id=1, source_target_pairs={{0,2},{2,4},{4,6},{6,0},{1,3},{3,5},{5,7},{7,1},{8,10},{10,12},{12... | collective-permute-start | bytes 393224 | tf_op jit(solution)/shard_map/ppermute | solution.py:531
  84.1 2.6 %collective-permute-start.3 = (bf16[512,128]{1,0:T(8,128)(2,1)S(1)}, bf16[512,128]{1,0:T(8,128)(2,1)S(1)}, u32[]{:S(2)}, u32[]{:S(2)}) collective-permute-start(bf16[512,128]{1,0:T(8,128)(2,1)S(1)} %get-tuple-element.66), channel_id=1, source_target_pairs={{0,4},{2,6},{4,0},{6,2},{1,5},{3,7},{5,1},{7,3},{8,12},{10,14},{12... | collective-permute-start | bytes 393224 | tf_op jit(solution)/shard_map/ppermute | solution.py:531
  86.7 1.1 collective-permute-start.4
  87.7 6.0 %input_grads.1 = (f32[2048,512]{1,0:T(8,128)}, f32[8,512]{1,0:T(8,128)S(1)}) custom-call(f32[32,8,512]{2,1,0:T(8,128)S(1)} %all-to-all-done.1.back_ref, f32[2048,512]{1,0:T(8,128)} %get-tuple-element.38.pre_hbm, f32[2048,512]{1,0:T(8,128)} %get-tuple-element.39.factor_hbm, bf16[2048,128]{1,0:T(8,128)(2,1)} %inject_hbm.7, bf16[4,512]{1,0:T(4,128)(2,1)S(1)} %copy-done.2), custom_call_target="tpu_custom_call" | custom-call | flops 536870912 | bytes 13631488 | tf_op jit(solution)/shard_map/input_grads/pallas_call | solution.py:538
  93.8 0.1 broadcast_in_dim.7
  93.9 0.1 constant_dynamic-update-slice_fusion.3
  94.0 0.5 collective-permute-start.5
  94.4 1.7 %collective-permute-start.6 = (bf16[512,128]{1,0:T(8,128)(2,1)S(1)}, bf16[512,128]{1,0:T(8,128)(2,1)S(1)}, u32[]{:S(2)}, u32[]{:S(2)}) collective-permute-start(bf16[512,128]{1,0:T(8,128)(2,1)S(1)} %get-tuple-element.62), channel_id=1, source_target_pairs={{0,4},{2,6},{4,0},{6,2},{1,5},{3,7},{5,1},{7,3},{8,12},{10,14},{12... | collective-permute-start | bytes 393224 | tf_op jit(solution)/shard_map/ppermute | solution.py:531
  96.2 0.9 collective-permute-start.7
  97.1 2.5 %collective-permute-start.8 = (f32[8,512]{1,0:T(8,128)S(1)}, f32[8,512]{1,0:T(8,128)S(1)}, u32[]{:S(2)}, u32[]{:S(2)}) collective-permute-start(f32[8,512]{1,0:T(8,128)S(1)} %get-tuple-element.56), channel_id=1, source_target_pairs={{8,0},{16,8},{24,16},{32,24},{40,32},{48,40},{56,48},{64,56},{72,6... | collective-permute-start | bytes 49160 | tf_op jit(solution)/shard_map/ppermute | solution.py:558
  99.6 4.1 %collective-permute-done.8 = f32[8,512]{1,0:T(8,128)S(1)} collective-permute-done((f32[8,512]{1,0:T(8,128)S(1)}, f32[8,512]{1,0:T(8,128)S(1)}, u32[]{:S(2)}, u32[]{:S(2)}) %collective-permute-start.8) | collective-permute-done | bytes 16416 | tf_op jit(solution)/shard_map/ppermute | solution.py:558
  103.8 3.6 %collective-permute-start.9 = (bf16[2048,128]{1,0:T(8,128)(2,1)S(1)}, bf16[2048,128]{1,0:T(8,128)(2,1)S(1)}, u32[]{:S(2)}, u32[]{:S(2)}) collective-permute-start(bf16[2048,128]{1,0:T(8,128)(2,1)S(1)} %constant_dynamic-update-slice_fusion), channel_id=1, source_target_pairs={{0,1},{1,0},{2,3},{3,2},{4,5},{5,4},{6,7},{7,6},{8,9},{9,8},{10,11... | collective-permute-start | bytes 1572872 | tf_op jit(solution)/shard_map/ppermute | solution.py:565
  107.3 1.4 %fusion = f32[2048,512]{1,0:T(8,128)} fusion(f32[2048,512]{1,0:T(8,128)} %get-tuple-element.40, f32[1,512]{1,0:T(1,128)S(1)} %get-tuple-element.69, f32[1,512]{1,0:T(1,128)S(1)} %get-tuple-element.70, f32[1,512]{1,0:T(1,128)S(1)} %get-tuple-element.68, f32[8]{0:T(128)S(1)} %pad.clone), kind=kLoop, calls=%fused_computation.7 | loop fusion | flops 16384 | bytes 38944 | tf_op jit(solution)/shard_map/dynamic_update_slice | solution.py:576
  108.7 0.1 collective-permute-done.9
  108.9 1.5 %select_convert_fusion = (f32[2048,128]{1,0:T(8,128)}, f32[2048,128]{1,0:T(8,128)}) fusion(bf16[2048,128]{1,0:T(8,128)(2,1)S(1)} %collective-permute-done.9, bf16[2048,128]{1,0:T(8,128)(2,1)S(1)} %constant_dynamic-update-slice_fusion, pred[]{:T(512)S(6)} %eq.3), kind=kLoop, calls=%fused_computation | loop fusion | flops 1048576 | bytes 3145729 | tf_op jit(solution)/shard_map/convert_element_type | solution.py:568
  (21 shorter events, 0.2 us)
Async XLA Ops:
  0.6 10.0 %copy-start = (bf16[2048,128]{1,0:T(8,128)(2,1)S(1)}, bf16[2048,128]{1,0:T(8,128)(2,1)}, u32[]{:S(2)}) copy-start(bf16[2048,128]{1,0:T(8,128)(2,1)} %inject_hbm.7) | copy-start | bytes 1572868
  1.4 9.2 %collective-permute-start = (bf16[16,512]{1,0:T(8,128)(2,1)S(1)}, bf16[16,512]{1,0:T(8,128)(2,1)S(1)}, u32[]{:S(2)}, u32[]{:S(2)}) collective-permute-start(bf16[16,512]{1,0:T(8,128)(2,1)S(1)} %slice.30), channel_id=1, source_target_pairs={{0,8},{8,16},{16,24},{24,32},{32,40},{40,48},{48,56},{56,64},{64,7... | collective-permute-start | bytes 49160 | tf_op jit(solution)/shard_map/ppermute | solution.py:432
  4.9 1.0 copy-start.1
  5.9 0.7 copy-start.3
  6.6 4.0 %copy-start.2 = (bf16[4,512]{1,0:T(4,128)(2,1)S(1)}, bf16[4,512]{1,0:T(4,128)(2,1)}, u32[]{:S(2)}) copy-start(bf16[4,512]{1,0:T(4,128)(2,1)} %weight_ref.1) | copy-start | bytes 12292
  18.3 28.7 %all-to-all-start = ((f32[32,8,640]{2,1,0:T(8,128)}), f32[32,8,640]{2,1,0:T(8,128)S(1)}, u32[]{:S(2)}, u32[]{:S(2)}) async-start(f32[32,8,640]{2,1,0:T(8,128)} %own_states.1), calls=%async_computation | async-start | bytes 1310720 | tf_op jit(solution)/shard_map/all_to_all | solution.py:472
  47.9 20.7 %all-to-all-start.1 = ((f32[32,8,512]{2,1,0:T(8,128)}), f32[32,8,512]{2,1,0:T(8,128)S(1)}, u32[]{:S(2)}, u32[]{:S(2)}) async-start(f32[32,8,512]{2,1,0:T(8,128)} %carry.1), calls=%async_computation.1 | async-start | bytes 1048576 | tf_op jit(solution)/shard_map/all_to_all | solution.py:510
  75.4 5.9 %collective-permute-start.1 = (f32[2048,128]{1,0:T(8,128)}, f32[2048,128]{1,0:T(8,128)S(1)}, u32[]{:S(2)}, u32[]{:S(2)}) collective-permute-start(f32[2048,128]{1,0:T(8,128)} %get-tuple-element.51), channel_id=1, source_target_pairs={{0,1},{1,0},{2,3},{3,2},{4,5},{5,4},{6,7},{7,6},{8,9},{9,8},{10,11... | collective-permute-start | bytes 3145736 | tf_op jit(solution)/shard_map/ppermute | solution.py:526
  82.7 11.0 %collective-permute-start.2 = (bf16[512,128]{1,0:T(8,128)(2,1)S(1)}, bf16[512,128]{1,0:T(8,128)(2,1)S(1)}, u32[]{:S(2)}, u32[]{:S(2)}) collective-permute-start(bf16[512,128]{1,0:T(8,128)(2,1)S(1)} %get-tuple-element.67), channel_id=1, source_target_pairs={{0,2},{2,4},{4,6},{6,0},{1,3},{3,5},{5,7},{7,1},{8,10},{10,12},{12... | collective-permute-start | bytes 393224 | tf_op jit(solution)/shard_map/ppermute | solution.py:531
  84.1 9.7 %collective-permute-start.3 = (bf16[512,128]{1,0:T(8,128)(2,1)S(1)}, bf16[512,128]{1,0:T(8,128)(2,1)S(1)}, u32[]{:S(2)}, u32[]{:S(2)}) collective-permute-start(bf16[512,128]{1,0:T(8,128)(2,1)S(1)} %get-tuple-element.66), channel_id=1, source_target_pairs={{0,4},{2,6},{4,0},{6,2},{1,5},{3,7},{5,1},{7,3},{8,12},{10,14},{12... | collective-permute-start | bytes 393224 | tf_op jit(solution)/shard_map/ppermute | solution.py:531
  86.7 7.1 %collective-permute-start.4 = (bf16[512,128]{1,0:T(8,128)(2,1)S(1)}, bf16[512,128]{1,0:T(8,128)(2,1)S(1)}, u32[]{:S(2)}, u32[]{:S(2)}) collective-permute-start(bf16[512,128]{1,0:T(8,128)(2,1)S(1)} %get-tuple-element.65), channel_id=1, source_target_pairs={{0,6},{2,0},{4,2},{6,4},{1,7},{3,1},{5,3},{7,5},{8,14},{10,8},{12,... | collective-permute-start | bytes 393224 | tf_op jit(solution)/shard_map/ppermute | solution.py:531
  94.0 9.7 %collective-permute-start.5 = (bf16[512,128]{1,0:T(8,128)(2,1)S(1)}, bf16[512,128]{1,0:T(8,128)(2,1)S(1)}, u32[]{:S(2)}, u32[]{:S(2)}) collective-permute-start(bf16[512,128]{1,0:T(8,128)(2,1)S(1)} %get-tuple-element.62), channel_id=1, source_target_pairs={{0,2},{2,4},{4,6},{6,0},{1,3},{3,5},{5,7},{7,1},{8,10},{10,12},{12... | collective-permute-start | bytes 393224 | tf_op jit(solution)/shard_map/ppermute | solution.py:531
  94.4 9.2 %collective-permute-start.6 = (bf16[512,128]{1,0:T(8,128)(2,1)S(1)}, bf16[512,128]{1,0:T(8,128)(2,1)S(1)}, u32[]{:S(2)}, u32[]{:S(2)}) collective-permute-start(bf16[512,128]{1,0:T(8,128)(2,1)S(1)} %get-tuple-element.62), channel_id=1, source_target_pairs={{0,4},{2,6},{4,0},{6,2},{1,5},{3,7},{5,1},{7,3},{8,12},{10,14},{12... | collective-permute-start | bytes 393224 | tf_op jit(solution)/shard_map/ppermute | solution.py:531
  96.2 7.5 %collective-permute-start.7 = (bf16[512,128]{1,0:T(8,128)(2,1)S(1)}, bf16[512,128]{1,0:T(8,128)(2,1)S(1)}, u32[]{:S(2)}, u32[]{:S(2)}) collective-permute-start(bf16[512,128]{1,0:T(8,128)(2,1)S(1)} %get-tuple-element.62), channel_id=1, source_target_pairs={{0,6},{2,0},{4,2},{6,4},{1,7},{3,1},{5,3},{7,5},{8,14},{10,8},{12,... | collective-permute-start | bytes 393224 | tf_op jit(solution)/shard_map/ppermute | solution.py:531
  97.1 6.6 %collective-permute-start.8 = (f32[8,512]{1,0:T(8,128)S(1)}, f32[8,512]{1,0:T(8,128)S(1)}, u32[]{:S(2)}, u32[]{:S(2)}) collective-permute-start(f32[8,512]{1,0:T(8,128)S(1)} %get-tuple-element.56), channel_id=1, source_target_pairs={{8,0},{16,8},{24,16},{32,24},{40,32},{48,40},{56,48},{64,56},{72,6... | collective-permute-start | bytes 49160 | tf_op jit(solution)/shard_map/ppermute | solution.py:558
  103.8 5.1 %collective-permute-start.9 = (bf16[2048,128]{1,0:T(8,128)(2,1)S(1)}, bf16[2048,128]{1,0:T(8,128)(2,1)S(1)}, u32[]{:S(2)}, u32[]{:S(2)}) collective-permute-start(bf16[2048,128]{1,0:T(8,128)(2,1)S(1)} %constant_dynamic-update-slice_fusion), channel_id=1, source_target_pairs={{0,1},{1,0},{2,3},{3,2},{4,5},{5,4},{6,7},{7,6},{8,9},{9,8},{10,11... | collective-permute-start | bytes 1572872 | tf_op jit(solution)/shard_map/ppermute | solution.py:565

commit v4 on v3

--- a/solution.py
+++ b/solution.py
@@ -11,6 +11,7 @@
 f32, bf16 = jnp.float32, jnp.bfloat16
 SPAN = 256
 SEQ, HG = ("z", "x"), ("y", "c")
+LANES = 128
 PREV = 16
 
 NN = (((1,), (0,)), ((), ()))
@@ -76,6 +77,36 @@
     for span in range(spans):
         for piece in pieces:
             piece(span).wait()
+
+
+TOP = 32000.0
+STEPS = 4096.0
+
+
+def coded(v, axis):
+    most = jnp.max(jnp.abs(v), axis=axis, keepdims=True)
+    power = jnp.ceil(jnp.log2(jnp.maximum(most, 2.0**-120)))
+    whole = jnp.round(v * jnp.exp2(-power) * TOP).astype(jnp.int32)
+    return whole.astype(jnp.int16), power
+
+
+def decoded(whole, power):
+    return whole.astype(f32) * (jnp.exp2(power.astype(f32)) * (1.0 / TOP))
+
+
+def log_codes(log):
+    steps = log * -STEPS
+    high = jnp.floor(steps)
+    return high, jnp.round((steps - high) * TOP)
+
+
+def log_of(high, low):
+    return (high.astype(f32) + low.astype(f32) * (1.0 / TOP)) * (-1.0 / STEPS)
+
+
+def side_tile(height, rows):
+    blank = jnp.zeros((height - len(rows), rows[0].shape[1]), f32)
+    return jnp.concatenate(rows + [blank], axis=0).astype(jnp.int32).astype(jnp.int16)
 
 
 def grads_kernel(
@@ -163,32 +194,41 @@
     each_span(spans, step)
     late.wait()
     chunks, height, _ = pay_ref.shape
-    half = carry.shape[1] // 2
+    state_codes, state_power = coded(carry[...], 0)
+    grad_codes, grad_power = coded(own_grad_ref[...], 0)
+    side = side_tile(height, [state_power, grad_power, *log_codes(log_ref[...])])
     for d in range(chunks):
-        r, l = height * (d // 2), half * (d % 2)
-        pay_ref[d, :, 0:half] = carry[r : r + height, l : l + half]
-        pay_ref[d, :, half : 2 * half] = own_grad_ref[r : r + height, l : l + half]
-        for row in range(half // 128):
-            at = l + 128 * row
-            pay_ref[d, row : row + 1, 2 * half : 2 * half + 128] = log_ref[:, at : at + 128]
-
-
-def scan_kernel(own_ref, out_ref):
-    chunks, height, width = out_ref.shape
-    half = width // 2
-
-    def gain(e):
-        logs = [own_ref[e, r : r + 1, width : width + 128] for r in range(half // 128)]
-        return jnp.exp(jnp.concatenate(logs, axis=1))
-
-    state = jnp.zeros((height, half), f32)
-    grad = jnp.zeros((height, half), f32)
+        rows, lanes = chunk_place(d, height)
+        pay_ref[d, :, 0:LANES] = state_codes[rows, lanes]
+        pay_ref[d, :, LANES : 2 * LANES] = grad_codes[rows, lanes]
+        pay_ref[d, :, 2 * LANES :] = side[:, lanes]
+
+
+def chunk_place(d, height):
+    r, l = height * (d // 4), LANES * (d % 4)
+    return slice(r, r + height), slice(l, l + LANES)
+
+
+def scan_kernel(own_ref, out_ref, made):
+    chunks, height, _ = out_ref.shape
+    gains, states, grads = [], [], []
     for e in range(chunks):
-        out_ref[e, :, 0:half] = state
-        state = gain(e) * state + own_ref[e, :, 0:half]
+        side = own_ref[e, :, 2 * LANES :].astype(f32)
+        gains.append(jnp.exp(log_of(side[2:3], side[3:4])))
+        states.append(decoded(own_ref[e, :, 0:LANES], side[0:1]))
+        grads.append(decoded(own_ref[e, :, LANES : 2 * LANES], side[1:2]))
+    state = jnp.zeros((height, LANES), f32)
+    grad = jnp.zeros((height, LANES), f32)
+    for e in range(chunks):
+        made[e, :, 0:LANES] = state
+        state = gains[e] * state + states[e]
     for e in reversed(range(chunks)):
-        out_ref[e, :, half:width] = grad
-        grad = gain(e) * grad + own_ref[e, :, half:width]
+        made[e, :, LANES:] = grad
+        grad = gains[e] * grad + grads[e]
+    for e in range(chunks):
+        codes, power = coded(made[e], 0)
+        out_ref[e, :, 0 : 2 * LANES] = codes
+        out_ref[e, :, 2 * LANES :] = side_tile(height, [power[:, :LANES], power[:, LANES:]])
 
 
 def causal():
@@ -271,28 +311,18 @@
 
 
 def local_shared_kernel(
-    grad_hbm, act_hbm, inject_hbm, read_hbm, after_hbm, rate_hbm, prior_hbm, later_hbm,
-    adh_hbm, adl_hbm, gdh_hbm, gdl_hbm, gi_hbm, gr_hbm,
-    grad_ref, act_ref, inject_ref, read_ref, after_ref, rate_ref, prior_ref, later_ref,
-    adh_ref, adl_ref, gdh_ref, gdl_ref, gi_ref, gr_ref, carry,
-    isems, sems, osems,
+    grad_hbm, act_hbm, inject_hbm, read_hbm, after_hbm, rate_hbm,
+    gi_hbm, gr_hbm,
+    grad_ref, act_ref, inject_ref, read_ref, after_ref, rate_ref,
+    gi_ref, gr_ref, carry,
+    isems, sem, osems,
 ):
     spans = rate_ref.shape[0]
     sources = [grad_hbm, act_hbm, inject_hbm, read_hbm, after_hbm]
     targets = [grad_ref, act_ref, inject_ref, read_ref, after_ref]
     pieces = [by_span(a, b, isems.at[k]) for k, (a, b) in enumerate(zip(sources, targets))]
-    made = [adh_ref, adl_ref, gdh_ref, gdl_ref, gi_ref, gr_ref]
-    places_to = [adh_hbm, adl_hbm, gdh_hbm, gdl_hbm, gi_hbm, gr_hbm]
-    outs = [by_span(a, b, osems.at[k]) for k, (a, b) in enumerate(zip(made, places_to))]
-    fetch(
-        spans,
-        [
-            pltpu.make_async_copy(rate_hbm, rate_ref, sems.at[0]),
-            pltpu.make_async_copy(prior_hbm, prior_ref, sems.at[1]),
-            pltpu.make_async_copy(later_hbm, later_ref, sems.at[2]),
-        ],
-        pieces,
-    )
+    outs = [by_span(gi_ref, gi_hbm, osems.at[0]), by_span(gr_ref, gr_hbm, osems.at[1])]
+    fetch(spans, [pltpu.make_async_copy(rate_hbm, rate_ref, sem)], pieces)
     carry[...] = jnp.zeros_like(carry)
 
     def step(span):
@@ -300,8 +330,6 @@
             piece(span).wait()
         rows = span_at(span)
         rate = rate_ref[pl.ds(span, 1), :]
-        later = later_ref[pl.ds(span, 1), :]
-        prior = prior_ref[pl.ds(span, 1), :]
         inject, read = inject_ref[rows, :], read_ref[rows, :]
         states = inject.shape[1]
         here = places()
@@ -318,8 +346,6 @@
         gr_ref[rows, :] = dot(pairs, inject, NN) + wide_product(uph, upl, befores, states)
         fresh = dot(inject, downh, TN) + dot(inject, downl, TN)
         carry[...] = jnp.exp(SPAN * rate) * before + end * fresh
-        adh_ref[rows, :], adl_ref[rows, :] = split(down * jnp.exp((SPAN - 1.0) * rate + later))
-        gdh_ref[rows, :], gdl_ref[rows, :] = split(up * jnp.exp(rate + prior))
         for out in outs:
             out(span).start()
 
@@ -327,44 +353,61 @@
     drain(spans, outs)
 
 
-def unpacked(back_ref, high, low, grads):
-    chunks, height, width = back_ref.shape
-    half = width // 2
-    start = half if grads else 0
-    states = high.shape[0] // 2 if low is None else high.shape[0]
+def unpacked(back_ref, both, which):
+    chunks, height, _ = back_ref.shape
+    states = both.shape[0] // 2
     for d in range(chunks):
-        r, l = height * (d // 2), half * (d % 2)
-        h, w = split(back_ref[d, :, start : start + half])
-        high[r : r + height, l : l + half] = h
-        if low is None:
-            high[states + r : states + r + height, l : l + half] = w
-        else:
-            low[r : r + height, l : l + half] = w
+        rows, lanes = chunk_place(d, height)
+        power = back_ref[d, :, 2 * LANES :].astype(f32)[which : which + 1]
+        v = decoded(back_ref[d, :, LANES * which : LANES * which + LANES], power)
+        high, low = split(v)
+        both[rows, lanes] = high
+        both[states + rows.start : states + rows.stop, lanes] = low
 
 
 def shared_kernel(
-    core_ref, back_ref, adh_hbm, adl_hbm, gdh_hbm, gdl_hbm, gi_hbm, gr_hbm,
-    mine_ref, theirs_ref,
-    adh_ref, adl_ref, gdh_ref, gdl_ref, gi_ref, gr_ref, grads, carried, isems,
+    grads_turn, core_ref, back_ref, grad_hbm, act_hbm, gr_hbm, gi_hbm, rate_hbm, prior_hbm, later_hbm,
+    out_ref,
+    in_ref, sum_ref, rate_ref, prior_ref, later_ref, both, isems, sems,
 ):
-    tokens, states = gi_ref.shape
+    tokens, states = sum_ref.shape
     spans = tokens // SPAN
-    sources = [adh_hbm, adl_hbm, gdh_hbm, gdl_hbm, gi_hbm, gr_hbm]
-    targets = [adh_ref, adl_ref, gdh_ref, gdl_ref, gi_ref, gr_ref]
-    pieces = [by_span(a, b, isems.at[k]) for k, (a, b) in enumerate(zip(sources, targets))]
-    fetch(spans, [], pieces)
-    unpacked(back_ref, grads, None, True)
-    unpacked(back_ref, carried, None, False)
-    first = core_ref[0] == 0
+    readouts = core_ref[0] == grads_turn
+    small = [
+        pltpu.make_async_copy(rate_hbm, rate_ref, sems.at[0]),
+        pltpu.make_async_copy(prior_hbm, prior_ref, sems.at[1]),
+        pltpu.make_async_copy(later_hbm, later_ref, sems.at[2]),
+    ]
+    for copy in small:
+        copy.start()
+
+    @pl.when(readouts)
+    def _():
+        pieces = [by_span(grad_hbm, in_ref, isems.at[0]), by_span(gr_hbm, sum_ref, isems.at[1])]
+        fetch(spans, [], pieces)
+        unpacked(back_ref, both, 0)
+
+    @pl.when(jnp.logical_not(readouts))
+    def _():
+        pieces = [by_span(act_hbm, in_ref, isems.at[0]), by_span(gi_hbm, sum_ref, isems.at[1])]
+        fetch(spans, [], pieces)
+        unpacked(back_ref, both, 1)
+
+    for copy in small:
+        copy.wait()
+    arriving = [by_span(grad_hbm, in_ref, isems.at[0]), by_span(gr_hbm, sum_ref, isems.at[1])]
 
     def step(span):
-        for piece in pieces:
+        for piece in arriving:
             piece(span).wait()
         rows = span_at(span)
-        gi = gi_ref[rows, :] + wide_product(adh_ref[rows, :], adl_ref[rows, :], grads[...], states)
-        gr = gr_ref[rows, :] + wide_product(gdh_ref[rows, :], gdl_ref[rows, :], carried[...], states)
-        mine_ref[rows, :] = jnp.where(first, gi, gr)
-        theirs_ref[rows, :] = jnp.where(first, gr, gi)
+        rate = rate_ref[pl.ds(span, 1), :]
+        ahead = rate + prior_ref[pl.ds(span, 1), :]
+        behind = (SPAN - 1.0) * rate + later_ref[pl.ds(span, 1), :]
+        slope = jnp.where(readouts, rate, -rate)
+        offset = jnp.where(readouts, ahead, behind)
+        high, low = split(in_ref[rows, :].astype(f32) * jnp.exp(places() * slope + offset))
+        out_ref[rows, :] = sum_ref[rows, :] + wide_product(high, low, both[...], states)
 
     each_span(spans, step)
 
@@ -381,7 +424,7 @@
     ]
     out = by_span(made, out_hbm, osems)
     fetch(spans, [], pieces, backwards=True)
-    unpacked(back_ref, grads, None, True)
+    unpacked(back_ref, grads, 1)
     after[...] = jnp.zeros_like(after)
     weights = weight_ref[...].astype(f32)
 
@@ -406,7 +449,7 @@
     drain(spans, [out])
 
 
-def params(mib=53):
+def params(mib=54):
     return pltpu.CompilerParams(vmem_limit_bytes=mib << 20)
 
 
@@ -419,8 +462,8 @@
     spans = decay_codes.shape[1]
     states = inject.shape[1]
     shape = jax.ShapeDtypeStruct
-    height = 2 * states // nseq
-    chunk = (nseq, height, channels)
+    height = 4 * states // nseq
+    chunk = (nseq, height, 3 * LANES)
     smem = pl.BlockSpec(memory_space=pltpu.SMEM)
     wide, wide16 = shape((tokens, channels), f32), shape((tokens, channels), bf16)
     narrow, row = shape((tokens, states), f32), shape((spans, channels), f32)
@@ -459,7 +502,7 @@
         states_kernel,
         in_specs=[hbm, anywhere, hbm, anywhere, hbm, anywhere, anywhere],
         out_specs=plain,
-        out_shape=shape((nseq, height, channels + 128), f32),
+        out_shape=shape(chunk, jnp.int16),
         scratch_shapes=[
             wide16_v, halo_v, narrow16_v, row_v, weight_v, state_v, pltpu.VMEM((1, channels), f32),
             state_v, pltpu.VMEM((8, channels), f32), dma((spans,)), dma((spans,)), dma((5,)),
@@ -487,22 +530,22 @@
     )(conv_input, halo, grad_output, inject, readout, rates, later, conv_weight)
     arrived, act = lax.optimization_barrier((arrived, act))
 
-    adh, adl, gdh, gdl, gi, gr = pl.pallas_call(
+    gi, gr = pl.pallas_call(
         local_shared_kernel,
-        in_specs=[hbm] * 5 + [anywhere] * 3,
-        out_specs=[hbm] * 6,
-        out_shape=[wide16] * 4 + [narrow] * 2,
-        scratch_shapes=[wide16_v] * 2 + [narrow16_v] * 2 + [local_v] + [row_v] * 3
-        + [wide16_v] * 4 + [narrow_v] * 2 + [state_v]
-        + [dma((5, spans)), dma((3,)), dma((6, spans))],
+        in_specs=[hbm] * 5 + [anywhere],
+        out_specs=[hbm] * 2,
+        out_shape=[narrow] * 2,
+        scratch_shapes=[wide16_v] * 2 + [narrow16_v] * 2 + [local_v, row_v]
+        + [narrow_v] * 2 + [state_v] + [dma((5, spans)), dma, dma((2, spans))],
         compiler_params=params(),
-        cost_estimate=cost(12 * tokens * channels * SPAN, 19 << 20),
+        cost_estimate=cost(12 * tokens * channels * SPAN, 9 << 20),
         name="local_shared",
-    )(grad_output, act, inject, readout, after, rates, prior, later)
+    )(grad_output, act, inject, readout, after, rates)
 
     scanned = pl.pallas_call(
         scan_kernel,
-        out_shape=shape(chunk, f32),
+        out_shape=shape(chunk, jnp.int16),
+        scratch_shapes=[pltpu.VMEM((nseq, height, 2 * LANES), f32)],
         compiler_params=params(8),
         cost_estimate=cost(1 << 18, 1 << 20),
         name="carry",
@@ -511,19 +554,22 @@
 
     core = lax.axis_index("c").astype(jnp.int32).reshape(1)
     stacked = pltpu.VMEM((2 * states, channels), bf16)
-    mine, theirs = pl.pallas_call(
-        shared_kernel,
-        in_specs=[smem, plain] + [hbm] * 6,
-        out_specs=[plain] * 2,
-        out_shape=[narrow] * 2,
-        scratch_shapes=[wide16_v] * 4 + [narrow_v] * 2 + [stacked] * 2 + [dma((6, spans))],
-        compiler_params=params(),
-        cost_estimate=cost(12 * tokens * channels * states, 13 << 20),
-        name="shared_terms",
-    )(core, returned, adh, adl, gdh, gdl, gi, gr)
+
+    def shared(turn):
+        return pl.pallas_call(
+            functools.partial(shared_kernel, turn),
+            in_specs=[smem, plain] + [hbm] * 4 + [anywhere] * 3,
+            out_specs=plain,
+            out_shape=narrow,
+            scratch_shapes=[wide16_v, narrow_v] + [row_v] * 3 + [stacked, dma((2, spans)), dma((3,))],
+            compiler_params=params(53),
+            cost_estimate=cost(6 * tokens * channels * states, 4 << 20),
+            name=f"shared_terms_{turn}",
+        )(core, returned, grad_output, act, gr, gi, rates, prior, later)
 
     swap = [(i, i ^ 1) for i in range(nc)]
-    chip = mine + lax.ppermute(theirs, "c", swap)
+    swapped = lax.ppermute(shared(0), "c", swap)
+    chip = shared(1) + swapped
     here = lax.axis_index("y")
     part = tokens // ny
 
@@ -544,7 +590,7 @@
             wide_v, wide_v, narrow16_v, stacked, pltpu.VMEM((8, channels), f32), wide_v,
             dma((3, spans)), dma((spans,)),
         ],
-        compiler_params=params(),
+        compiler_params=params(53),
         cost_estimate=cost(4 * tokens * channels * states, 13 << 20),
         name="input_grads",
     )(returned, pre, factor, inject, conv_weight)

time: 111 us -> 105 us (0.946)
  waiting for transfers between devices: 18.2 us -> 6.37 us
  Pallas kernels: 46.9 us -> 52.6 us
  starting transfers between devices: 37.3 us -> 39.1 us
  local copies, waits for them, and re-layouts: 2.72 us -> 1.55 us
    all_to_all x1, waiting for transfers between devices: 8 us -> 1.43 us  [body(): arrived = lax.all_to_all(payload, SEQ, 0, 0, tiled=True)]
    pallas_call x3 -> x4, Pallas kernels: 19 us -> 22.2 us  [the longest x1 11.3 us: body(): pl.pallas_call(local_shared_kernel, in_specs=[hbm] * 5 + [anywhere], out_...]
    all_to_all x1, waiting for transfers between devices: 3.47 us -> 0.74 us  [body(): returned = lax.all_to_all(scanned, SEQ, 0, 0, tiled=True)]
    ppermute x1, waiting for transfers between devices: 2.5 us -> 0.01 us  [body(): swapped = lax.ppermute(shared(0), 'c', swap)]
    all_to_all x1, starting transfers between devices: 5.91 us -> 7.79 us  [body(): returned = lax.all_to_all(scanned, SEQ, 0, 0, tiled=True)]
    pallas_call x1, Pallas kernels: 4.01 us -> 5.34 us  [body(): pl.pallas_call(grads_kernel, in_specs=[hbm] * 3, out_specs=[plain] * 5, o...]
    unnamed x8 -> x12, local copies, waits for them, and re-layouts: 1.73 us -> 0.61 us
  transfers between devices with their start and end apart: 12 -> 12, of which waited for: 5 -> 4; matrix products, arithmetic and copies ran while one was open for 1% -> 1% of each run, Pallas kernels for 29% -> 37%
where the time goes in v4:
time: 105 us
  Pallas kernels  52.6 us (50%)
  starting transfers between devices  39.1 us (37%)
  waiting for transfers between devices  6.37 us (6%)
  other arithmetic  4.35 us (4%)
  local copies, waits for them, and re-layouts  1.55 us (1%)
    pallas_call x1, Pallas kernels, body(): pl.pallas_call(local_shared_kernel, in_specs=[hbm] * 5 + [anywhere], out_...  11.3 us
    pallas_call x1, Pallas kernels, body(): pl.pallas_call(local_input_kernel, in_specs=[hbm, anywhere, hbm, hbm, hbm...  11.1 us
    all_to_all x1, starting transfers between devices, body(): arrived = lax.all_to_all(payload, SEQ, 0, 0, tiled=True)  10.4 us
    pallas_call x2, Pallas kernels, shared(): pl.pallas_call(functools.partial(shared_kernel, turn), in_specs=[smem, pl...  9.8 us
    ppermute x6, starting transfers between devices, turn(): return lax.ppermute(array, 'y', [(i, (i + by) % ny) for i in range(ny)])  8.48 us
    pallas_call x1, Pallas kernels, body(): pl.pallas_call(states_kernel, in_specs=[hbm, anywhere, hbm, anywhere, hbm...  8 us
    all_to_all x1, starting transfers between devices, body(): returned = lax.all_to_all(scanned, SEQ, 0, 0, tiled=True)  7.79 us
    pallas_call x1, Pallas kernels, body(): pl.pallas_call(input_kernel, in_specs=[plain] + [hbm] * 3 + [plain], out_...  5.98 us
  transfers between devices with their start and end apart: 12, of which 4 were waited for; matrix products, arithmetic and copies ran while one was open for 1% of the time, Pallas kernels for 37%

profile of v4, /device:TPU:7, one launch (start us, length us, event | category | flops | bytes accessed | tf_op | source)
XLA Modules:
  0.0 104.8 jit_solution(6458331541540475553)
XLA Ops:
  0.6 0.7 slice.30
  1.4 3.4 %collective-permute-start = (bf16[16,512]{1,0:T(8,128)(2,1)S(1)}, bf16[16,512]{1,0:T(8,128)(2,1)S(1)}, u32[]{:S(2)}, u32[]{:S(2)}) collective-permute-start(bf16[16,512]{1,0:T(8,128)(2,1)S(1)} %slice.30), channel_id=1, source_target_pairs={{0,8},{8,16},{16,24},{24,32},{32,40},{40,48},{48,56},{56,64},{64,7... | collective-permute-start | bytes 49160 | tf_op jit(solution)/shard_map/ppermute | solution.py:475
  4.8 5.3 %own_grads.1 = (f32[8,512]{1,0:T(8,128)}, f32[8,512]{1,0:T(8,128)}, f32[8,512]{1,0:T(8,128)}, f32[1,512]{1,0:T(1,128)}, f32[128,512]{1,0:T(8,128)}) custom-call(s32[8,8]{1,0:T(8,128)} %code_hbm.1, bf16[2048,512]{1,0:T(8,128)(2,1)} %grad_hbm.9, bf16[2048,128]{1,0:T(8,128)(2,1)} %read_hbm.5), custom_call_target="tpu_custom_call" | custom-call | flops 536870912 | bytes 3145728 | tf_op jit(solution)/shard_map/own_grads/pallas_call | solution.py:487
  10.2 0.6 copy-done.5
  10.8 8.0 %own_states.1 = s16[32,16,384]{2,1,0:T(8,128)(2,1)} custom-call(bf16[2048,512]{1,0:T(8,128)(2,1)} %x_hbm.3, bf16[16,512]{1,0:T(8,128)(2,1)} %copy-done.5, bf16[2048,128]{1,0:T(8,128)(2,1)} %inject_hbm.7, f32[8,512]{1,0:T(8,128)} %get-tuple-element.26.rate_hbm, bf16[4,512]{1,0:T(4,128)(2,1)} %weight_ref.1, f32[128,512]{1,0:T(8,128)} %get-tuple-element.27.own_grad_hbm, ...), custom_call_target="tpu_custom_call" | custom-call | flops 536870912 | bytes 4194304 | tf_op jit(solution)/shard_map/own_states/pallas_call | solution.py:501
  18.8 10.4 %all-to-all-start = ((s16[32,16,384]{2,1,0:T(8,128)(2,1)}), s16[32,16,384]{2,1,0:T(8,128)(2,1)S(1)}, u32[]{:S(2)}, u32[]{:S(2)}) async-start(s16[32,16,384]{2,1,0:T(8,128)(2,1)} %own_states.1), calls=%async_computation | async-start | bytes 786432 | tf_op jit(solution)/shard_map/all_to_all | solution.py:515
  29.2 11.1 %local_input.1 = (bf16[2048,512]{1,0:T(8,128)(2,1)}, f32[2048,512]{1,0:T(8,128)}, f32[2048,512]{1,0:T(8,128)}, f32[8,128,512]{2,1,0:T(8,128)}) custom-call(bf16[2048,512]{1,0:T(8,128)(2,1)} %x_hbm.3, bf16[16,512]{1,0:T(8,128)(2,1)} %copy-done.5, bf16[2048,512]{1,0:T(8,128)(2,1)} %grad_hbm.9, bf16[2048,128]{1,0:T(8,128)(2,1)} %inject_hbm.7, ...), custom_call_target="tpu_custom_call" | custom-call | flops 2147483648 | bytes 18874368 | tf_op jit(solution)/shard_map/local_input/pallas_call | solution.py:517
  40.3 1.4 %all-to-all-done.own_ref = s16[32,16,384]{2,1,0:T(8,128)(2,1)S(1)} async-done(((s16[32,16,384]{2,1,0:T(8,128)(2,1)}), s16[32,16,384]{2,1,0:T(8,128)(2,1)S(1)}, u32[]{:S(2)}, u32[]{:S(2)}) %all-to-all-start) | async-done | bytes 393248 | tf_op jit(solution)/shard_map/all_to_all | solution.py:515
  41.7 1.1 %carry.1 = s16[32,16,384]{2,1,0:T(8,128)(2,1)} custom-call(s16[32,16,384]{2,1,0:T(8,128)(2,1)S(1)} %all-to-all-done.own_ref), custom_call_target="tpu_custom_call" | custom-call | flops 262144 | bytes 1048576 | tf_op jit(solution)/shard_map/carry/pallas_call | solution.py:545
  42.8 7.8 %all-to-all-start.1 = ((s16[32,16,384]{2,1,0:T(8,128)(2,1)}), s16[32,16,384]{2,1,0:T(8,128)(2,1)S(1)}, u32[]{:S(2)}, u32[]{:S(2)}) async-start(s16[32,16,384]{2,1,0:T(8,128)(2,1)} %carry.1), calls=%async_computation.1 | async-start | bytes 786432 | tf_op jit(solution)/shard_map/all_to_all | solution.py:553
  50.6 11.3 %local_shared.1 = (f32[2048,128]{1,0:T(8,128)}, f32[2048,128]{1,0:T(8,128)}) custom-call(bf16[2048,512]{1,0:T(8,128)(2,1)} %grad_hbm.9, bf16[2048,512]{1,0:T(8,128)(2,1)} %get-tuple-element.35.act_hbm, bf16[2048,128]{1,0:T(8,128)(2,1)} %inject_hbm.7, bf16[2048,128]{1,0:T(8,128)(2,1)} %read_hbm.5, f32[8,128,512]{2,1,0:T(8,128)} %get-tuple-element.36.after_hbm, ...), custom_call_target="tpu_custom_call" | custom-call | flops 3221225472 | bytes 9437184 | tf_op jit(solution)/shard_map/local_shared/pallas_call | solution.py:533
  61.9 0.7 all-to-all-done.1.back_ref
  62.7 4.8 %shared_terms_0.1 = f32[2048,128]{1,0:T(8,128)} custom-call(s32[1]{0:T(128)} %bitcast.core_ref, s16[32,16,384]{2,1,0:T(8,128)(2,1)S(1)} %all-to-all-done.1.back_ref, bf16[2048,512]{1,0:T(8,128)(2,1)} %grad_hbm.9, bf16[2048,512]{1,0:T(8,128)(2,1)} %get-tuple-element.35.act_hbm, f32[2048,128]{1,0:T(8,128)} %get-tuple-element.37.gr_hbm, ...), custom_call_target="tpu_custom_call" | custom-call | flops 805306368 | bytes 4194304 | tf_op jit(solution)/shard_map/shared_terms_0/pallas_call | solution.py:559
  67.5 3.3 %collective-permute-start.1 = (f32[2048,128]{1,0:T(8,128)}, f32[2048,128]{1,0:T(8,128)S(1)}, u32[]{:S(2)}, u32[]{:S(2)}) collective-permute-start(f32[2048,128]{1,0:T(8,128)} %shared_terms_0.1), channel_id=1, source_target_pairs={{0,1},{1,0},{2,3},{3,2},{4,5},{5,4},{6,7},{7,6},{8,9},{9,8},{10,11... | collective-permute-start | bytes 3145736 | tf_op jit(solution)/shard_map/ppermute | solution.py:571
  70.8 4.9 %shared_terms_1.1 = f32[2048,128]{1,0:T(8,128)} custom-call(s32[1]{0:T(128)} %bitcast.core_ref, s16[32,16,384]{2,1,0:T(8,128)(2,1)S(1)} %all-to-all-done.1.back_ref, bf16[2048,512]{1,0:T(8,128)(2,1)} %grad_hbm.9, bf16[2048,512]{1,0:T(8,128)(2,1)} %get-tuple-element.35.act_hbm, f32[2048,128]{1,0:T(8,128)} %get-tuple-element.37.gr_hbm, ...), custom_call_target="tpu_custom_call" | custom-call | flops 805306368 | bytes 4194304 | tf_op jit(solution)/shard_map/shared_terms_1/pallas_call | solution.py:559
  75.8 1.4 %add.69 = f32[2048,128]{1,0:T(8,128)S(1)} add(f32[2048,128]{1,0:T(8,128)} %shared_terms_1.1, f32[2048,128]{1,0:T(8,128)S(1)} %collective-permute-done.1) | non-fusion elementwise | flops 262144 | bytes 3145728 | tf_op jit(solution)/shard_map/add | solution.py:572
  77.1 0.1 dynamic-slice_convert_fusion
  77.2 1.4 %collective-permute-start.2 = (bf16[512,128]{1,0:T(8,128)(2,1)S(1)}, bf16[512,128]{1,0:T(8,128)(2,1)S(1)}, u32[]{:S(2)}, u32[]{:S(2)}) collective-permute-start(bf16[512,128]{1,0:T(8,128)(2,1)S(1)} %get-tuple-element.55), channel_id=1, source_target_pairs={{0,2},{2,4},{4,6},{6,0},{1,3},{3,5},{5,7},{7,1},{8,10},{10,12},{12... | collective-permute-start | bytes 393224 | tf_op jit(solution)/shard_map/ppermute | solution.py:577
  78.6 2.6 %collective-permute-start.3 = (bf16[512,128]{1,0:T(8,128)(2,1)S(1)}, bf16[512,128]{1,0:T(8,128)(2,1)S(1)}, u32[]{:S(2)}, u32[]{:S(2)}) collective-permute-start(bf16[512,128]{1,0:T(8,128)(2,1)S(1)} %get-tuple-element.54), channel_id=1, source_target_pairs={{0,4},{2,6},{4,0},{6,2},{1,5},{3,7},{5,1},{7,3},{8,12},{10,14},{12... | collective-permute-start | bytes 393224 | tf_op jit(solution)/shard_map/ppermute | solution.py:577
  81.2 1.1 %collective-permute-start.4 = (bf16[512,128]{1,0:T(8,128)(2,1)S(1)}, bf16[512,128]{1,0:T(8,128)(2,1)S(1)}, u32[]{:S(2)}, u32[]{:S(2)}) collective-permute-start(bf16[512,128]{1,0:T(8,128)(2,1)S(1)} %get-tuple-element.53), channel_id=1, source_target_pairs={{0,6},{2,0},{4,2},{6,4},{1,7},{3,1},{5,3},{7,5},{8,14},{10,8},{12,... | collective-permute-start | bytes 393224 | tf_op jit(solution)/shard_map/ppermute | solution.py:577
  82.3 6.0 %input_grads.1 = (f32[2048,512]{1,0:T(8,128)}, f32[8,512]{1,0:T(8,128)S(1)}) custom-call(s16[32,16,384]{2,1,0:T(8,128)(2,1)S(1)} %all-to-all-done.1.back_ref, f32[2048,512]{1,0:T(8,128)} %get-tuple-element.32.pre_hbm, f32[2048,512]{1,0:T(8,128)} %get-tuple-element.33.factor_hbm, bf16[2048,128]{1,0:T(8,128)(2,1)S(1)} %copy-done, bf16[4,512]{1,0:T(4,128)(2,1)S(1)} %copy-done.4), custom_call_target="tpu_custom_call" | custom-call | flops 536870912 | bytes 13631488 | tf_op jit(solution)/shard_map/input_grads/pallas_call | solution.py:584
  88.3 0.1 broadcast_in_dim.7
  88.4 0.1 constant_dynamic-update-slice_fusion.3
  88.5 0.5 collective-permute-start.5
  88.9 2.0 %collective-permute-start.6 = (bf16[512,128]{1,0:T(8,128)(2,1)S(1)}, bf16[512,128]{1,0:T(8,128)(2,1)S(1)}, u32[]{:S(2)}, u32[]{:S(2)}) collective-permute-start(bf16[512,128]{1,0:T(8,128)(2,1)S(1)} %get-tuple-element.50), channel_id=1, source_target_pairs={{0,4},{2,6},{4,0},{6,2},{1,5},{3,7},{5,1},{7,3},{8,12},{10,14},{12... | collective-permute-start | bytes 393224 | tf_op jit(solution)/shard_map/ppermute | solution.py:577
  91.0 0.9 collective-permute-start.7
  91.9 2.5 %collective-permute-start.8 = (f32[8,512]{1,0:T(8,128)S(1)}, f32[8,512]{1,0:T(8,128)S(1)}, u32[]{:S(2)}, u32[]{:S(2)}) collective-permute-start(f32[8,512]{1,0:T(8,128)S(1)} %get-tuple-element.44), channel_id=1, source_target_pairs={{8,0},{16,8},{24,16},{32,24},{40,32},{48,40},{56,48},{64,56},{72,6... | collective-permute-start | bytes 49160 | tf_op jit(solution)/shard_map/ppermute | solution.py:604
  94.4 4.1 %collective-permute-done.8 = f32[8,512]{1,0:T(8,128)S(1)} collective-permute-done((f32[8,512]{1,0:T(8,128)S(1)}, f32[8,512]{1,0:T(8,128)S(1)}, u32[]{:S(2)}, u32[]{:S(2)}) %collective-permute-start.8) | collective-permute-done | bytes 16416 | tf_op jit(solution)/shard_map/ppermute | solution.py:604
  98.6 3.3 %collective-permute-start.9 = (bf16[2048,128]{1,0:T(8,128)(2,1)S(1)}, bf16[2048,128]{1,0:T(8,128)(2,1)S(1)}, u32[]{:S(2)}, u32[]{:S(2)}) collective-permute-start(bf16[2048,128]{1,0:T(8,128)(2,1)S(1)} %constant_dynamic-update-slice_fusion), channel_id=1, source_target_pairs={{0,1},{1,0},{2,3},{3,2},{4,5},{5,4},{6,7},{7,6},{8,9},{9,8},{10,11... | collective-permute-start | bytes 1572872 | tf_op jit(solution)/shard_map/ppermute | solution.py:611
  101.9 1.4 %fusion = f32[2048,512]{1,0:T(8,128)} fusion(f32[2048,512]{1,0:T(8,128)} %get-tuple-element.34, f32[1,512]{1,0:T(1,128)S(1)} %get-tuple-element.57, f32[1,512]{1,0:T(1,128)S(1)} %get-tuple-element.58, f32[1,512]{1,0:T(1,128)S(1)} %get-tuple-element.56, f32[8]{0:T(128)S(1)} %pad.clone), kind=kLoop, calls=%fused_computation.7 | loop fusion | flops 16384 | bytes 38944 | tf_op jit(solution)/shard_map/dynamic_update_slice | solution.py:622
  103.3 0.1 collective-permute-done.9
  103.4 1.5 %select_convert_fusion = (f32[2048,128]{1,0:T(8,128)}, f32[2048,128]{1,0:T(8,128)}) fusion(bf16[2048,128]{1,0:T(8,128)(2,1)S(1)} %collective-permute-done.9, bf16[2048,128]{1,0:T(8,128)(2,1)S(1)} %constant_dynamic-update-slice_fusion, pred[]{:T(512)S(6)} %eq.3), kind=kLoop, calls=%fused_computation | loop fusion | flops 1048576 | bytes 3145729 | tf_op jit(solution)/shard_map/convert_element_type | solution.py:614
  (26 shorter events, 0.1 us)
Async XLA Ops:
  1.4 8.8 %collective-permute-start = (bf16[16,512]{1,0:T(8,128)(2,1)S(1)}, bf16[16,512]{1,0:T(8,128)(2,1)S(1)}, u32[]{:S(2)}, u32[]{:S(2)}) collective-permute-start(bf16[16,512]{1,0:T(8,128)(2,1)S(1)} %slice.30), channel_id=1, source_target_pairs={{0,8},{8,16},{16,24},{24,32},{32,40},{40,48},{48,56},{56,64},{64,7... | collective-permute-start | bytes 49160 | tf_op jit(solution)/shard_map/ppermute | solution.py:475
  10.2 0.6 copy-start.5
  18.8 22.9 %all-to-all-start = ((s16[32,16,384]{2,1,0:T(8,128)(2,1)}), s16[32,16,384]{2,1,0:T(8,128)(2,1)S(1)}, u32[]{:S(2)}, u32[]{:S(2)}) async-start(s16[32,16,384]{2,1,0:T(8,128)(2,1)} %own_states.1), calls=%async_computation | async-start | bytes 786432 | tf_op jit(solution)/shard_map/all_to_all | solution.py:515
  42.8 19.9 %all-to-all-start.1 = ((s16[32,16,384]{2,1,0:T(8,128)(2,1)}), s16[32,16,384]{2,1,0:T(8,128)(2,1)S(1)}, u32[]{:S(2)}, u32[]{:S(2)}) async-start(s16[32,16,384]{2,1,0:T(8,128)(2,1)} %carry.1), calls=%async_computation.1 | async-start | bytes 786432 | tf_op jit(solution)/shard_map/all_to_all | solution.py:553
  50.6 12.1 %copy-start.1 = (f32[8,512]{1,0:T(8,128)S(1)}, f32[8,512]{1,0:T(8,128)}, u32[]{:S(2)}) copy-start(f32[8,512]{1,0:T(8,128)} %get-tuple-element.26.rate_hbm) | copy-start | bytes 49156
  50.6 12.1 %copy-start.2 = (f32[8,512]{1,0:T(8,128)S(1)}, f32[8,512]{1,0:T(8,128)}, u32[]{:S(2)}) copy-start(f32[8,512]{1,0:T(8,128)} %get-tuple-element.39.prior_hbm) | copy-start | bytes 49156
  50.6 12.1 %copy-start.3 = (f32[8,512]{1,0:T(8,128)S(1)}, f32[8,512]{1,0:T(8,128)}, u32[]{:S(2)}) copy-start(f32[8,512]{1,0:T(8,128)} %get-tuple-element.29.later_hbm) | copy-start | bytes 49156
  67.5 8.2 %collective-permute-start.1 = (f32[2048,128]{1,0:T(8,128)}, f32[2048,128]{1,0:T(8,128)S(1)}, u32[]{:S(2)}, u32[]{:S(2)}) collective-permute-start(f32[2048,128]{1,0:T(8,128)} %shared_terms_0.1), channel_id=1, source_target_pairs={{0,1},{1,0},{2,3},{3,2},{4,5},{5,4},{6,7},{7,6},{8,9},{9,8},{10,11... | collective-permute-start | bytes 3145736 | tf_op jit(solution)/shard_map/ppermute | solution.py:571
  70.8 11.5 %copy-start = (bf16[2048,128]{1,0:T(8,128)(2,1)S(1)}, bf16[2048,128]{1,0:T(8,128)(2,1)}, u32[]{:S(2)}) copy-start(bf16[2048,128]{1,0:T(8,128)(2,1)} %inject_hbm.7) | copy-start | bytes 1572868
  70.8 11.5 %copy-start.4 = (bf16[4,512]{1,0:T(4,128)(2,1)S(1)}, bf16[4,512]{1,0:T(4,128)(2,1)}, u32[]{:S(2)}) copy-start(bf16[4,512]{1,0:T(4,128)(2,1)} %weight_ref.1) | copy-start | bytes 12292
  77.2 11.1 %collective-permute-start.2 = (bf16[512,128]{1,0:T(8,128)(2,1)S(1)}, bf16[512,128]{1,0:T(8,128)(2,1)S(1)}, u32[]{:S(2)}, u32[]{:S(2)}) collective-permute-start(bf16[512,128]{1,0:T(8,128)(2,1)S(1)} %get-tuple-element.55), channel_id=1, source_target_pairs={{0,2},{2,4},{4,6},{6,0},{1,3},{3,5},{5,7},{7,1},{8,10},{10,12},{12... | collective-permute-start | bytes 393224 | tf_op jit(solution)/shard_map/ppermute | solution.py:577
  78.6 9.7 %collective-permute-start.3 = (bf16[512,128]{1,0:T(8,128)(2,1)S(1)}, bf16[512,128]{1,0:T(8,128)(2,1)S(1)}, u32[]{:S(2)}, u32[]{:S(2)}) collective-permute-start(bf16[512,128]{1,0:T(8,128)(2,1)S(1)} %get-tuple-element.54), channel_id=1, source_target_pairs={{0,4},{2,6},{4,0},{6,2},{1,5},{3,7},{5,1},{7,3},{8,12},{10,14},{12... | collective-permute-start | bytes 393224 | tf_op jit(solution)/shard_map/ppermute | solution.py:577
  81.2 7.1 %collective-permute-start.4 = (bf16[512,128]{1,0:T(8,128)(2,1)S(1)}, bf16[512,128]{1,0:T(8,128)(2,1)S(1)}, u32[]{:S(2)}, u32[]{:S(2)}) collective-permute-start(bf16[512,128]{1,0:T(8,128)(2,1)S(1)} %get-tuple-element.53), channel_id=1, source_target_pairs={{0,6},{2,0},{4,2},{6,4},{1,7},{3,1},{5,3},{7,5},{8,14},{10,8},{12,... | collective-permute-start | bytes 393224 | tf_op jit(solution)/shard_map/ppermute | solution.py:577
  88.5 10.0 %collective-permute-start.5 = (bf16[512,128]{1,0:T(8,128)(2,1)S(1)}, bf16[512,128]{1,0:T(8,128)(2,1)S(1)}, u32[]{:S(2)}, u32[]{:S(2)}) collective-permute-start(bf16[512,128]{1,0:T(8,128)(2,1)S(1)} %get-tuple-element.50), channel_id=1, source_target_pairs={{0,2},{2,4},{4,6},{6,0},{1,3},{3,5},{5,7},{7,1},{8,10},{10,12},{12... | collective-permute-start | bytes 393224 | tf_op jit(solution)/shard_map/ppermute | solution.py:577
  88.9 9.5 %collective-permute-start.6 = (bf16[512,128]{1,0:T(8,128)(2,1)S(1)}, bf16[512,128]{1,0:T(8,128)(2,1)S(1)}, u32[]{:S(2)}, u32[]{:S(2)}) collective-permute-start(bf16[512,128]{1,0:T(8,128)(2,1)S(1)} %get-tuple-element.50), channel_id=1, source_target_pairs={{0,4},{2,6},{4,0},{6,2},{1,5},{3,7},{5,1},{7,3},{8,12},{10,14},{12... | collective-permute-start | bytes 393224 | tf_op jit(solution)/shard_map/ppermute | solution.py:577
  91.0 7.5 %collective-permute-start.7 = (bf16[512,128]{1,0:T(8,128)(2,1)S(1)}, bf16[512,128]{1,0:T(8,128)(2,1)S(1)}, u32[]{:S(2)}, u32[]{:S(2)}) collective-permute-start(bf16[512,128]{1,0:T(8,128)(2,1)S(1)} %get-tuple-element.50), channel_id=1, source_target_pairs={{0,6},{2,0},{4,2},{6,4},{1,7},{3,1},{5,3},{7,5},{8,14},{10,8},{12,... | collective-permute-start | bytes 393224 | tf_op jit(solution)/shard_map/ppermute | solution.py:577
  91.9 6.6 %collective-permute-start.8 = (f32[8,512]{1,0:T(8,128)S(1)}, f32[8,512]{1,0:T(8,128)S(1)}, u32[]{:S(2)}, u32[]{:S(2)}) collective-permute-start(f32[8,512]{1,0:T(8,128)S(1)} %get-tuple-element.44), channel_id=1, source_target_pairs={{8,0},{16,8},{24,16},{32,24},{40,32},{48,40},{56,48},{64,56},{72,6... | collective-permute-start | bytes 49160 | tf_op jit(solution)/shard_map/ppermute | solution.py:604
  98.6 4.8 %collective-permute-start.9 = (bf16[2048,128]{1,0:T(8,128)(2,1)S(1)}, bf16[2048,128]{1,0:T(8,128)(2,1)S(1)}, u32[]{:S(2)}, u32[]{:S(2)}) collective-permute-start(bf16[2048,128]{1,0:T(8,128)(2,1)S(1)} %constant_dynamic-update-slice_fusion), channel_id=1, source_target_pairs={{0,1},{1,0},{2,3},{3,2},{4,5},{5,4},{6,7},{7,6},{8,9},{9,8},{10,11... | collective-permute-start | bytes 1572872 | tf_op jit(solution)/shard_map/ppermute | solution.py:611

commit v5 on v4

--- a/solution.py
+++ b/solution.py
@@ -45,12 +45,31 @@
     return pl.ds(pl.multiple_of(span * SPAN, SPAN), SPAN)
 
 
-def each_span(spans, step, backwards=False):
+AHEAD = 3
+
+
+def each_span(spans, step, start, pieces, backwards=False, ahead=AHEAD):
     def visit(i, _):
-        step(spans - 1 - i if backwards else i)
+        span = spans - 1 - i if backwards else i
+        for piece in pieces:
+            piece(span).wait()
+
+        @pl.when(i + ahead < spans)
+        def _():
+            start(span - ahead if backwards else span + ahead)
+
+        step(span)
         return 0
 
     lax.fori_loop(0, spans, visit, 0)
+
+
+def starting(pieces):
+    def start(span):
+        for piece in pieces:
+            piece(span).start()
+
+    return start
 
 
 def by_span(source, target, sems):
@@ -63,12 +82,11 @@
     return piece
 
 
-def fetch(spans, whole, pieces, backwards=False):
+def fetch(spans, whole, start, backwards=False, ahead=AHEAD):
     for copy in whole:
         copy.start()
-    for i in range(spans):
-        for piece in pieces:
-            piece(spans - 1 - i if backwards else i).start()
+    for i in range(min(ahead, spans)):
+        start(spans - 1 - i if backwards else i)
     for copy in whole:
         copy.wait()
 
@@ -110,13 +128,15 @@
 
 
 def grads_kernel(
-    code_hbm, grad_hbm, read_hbm, rate_ref, prior_ref, later_ref, log_ref, carry,
-    code_ref, grad_ref, read_ref, csem, gsem, rsem,
+    code_hbm, grad_hbm, read_hbm, rate_ref, prior_ref, later_ref, log_ref, carry, after_hbm,
+    code_ref, grad_ref, read_ref, after_ref, csem, gsem, rsem, asem,
 ):
     heads, spans = code_ref.shape
+    sending = by_span(after_ref, after_hbm, asem)
     channels = carry.shape[1]
     pieces = [by_span(grad_hbm, grad_ref, gsem), by_span(read_hbm, read_ref, rsem)]
-    fetch(spans, [pltpu.make_async_copy(code_hbm, code_ref, csem)], pieces, backwards=True)
+    start = starting(pieces)
+    fetch(spans, [pltpu.make_async_copy(code_hbm, code_ref, csem)], start, backwards=True)
     logs = jnp.log1p(-code_ref[...].astype(f32) * 1e-6)
     lane = lax.broadcasted_iota(jnp.int32, (heads, channels), 1)
     row = lax.broadcasted_iota(jnp.int32, (heads, channels), 0)
@@ -137,32 +157,38 @@
     carry[...] = jnp.zeros_like(carry)
 
     def step(span):
-        for piece in pieces:
-            piece(span).wait()
         rate = rate_ref[pl.ds(span, 1), :]
+        after = carry[...]
+        after_ref[span] = after
+        sending(span).start()
         up = grad_ref[span_at(span), :].astype(f32) * jnp.exp(places() * rate)
         fresh = dot2(read_ref[span_at(span), :], up, TN)
-        carry[...] = jnp.exp(SPAN * rate) * carry[...] + jnp.exp(rate) * fresh
-
-    each_span(spans, step, backwards=True)
+        carry[...] = jnp.exp(SPAN * rate) * after + jnp.exp(rate) * fresh
+
+    each_span(spans, step, start, pieces, backwards=True)
+    drain(spans, [sending])
 
 
 def convolved(x, before, weights):
     rows = jnp.concatenate([before, x], axis=0)
-    preact = weights[0:1] * pltpu.roll(rows, 3, axis=0)[8:]
-    for k in range(1, 3):
-        preact = preact + weights[k : k + 1] * pltpu.roll(rows, 3 - k, axis=0)[8:]
-    return preact + weights[3:4] * x
+    one = pltpu.roll(rows, 1, axis=0)
+    older = weights[1:2] * rows + weights[0:1] * one
+    return (weights[3:4] * x + weights[2:3] * one[8:]) + pltpu.roll(older, 2, axis=0)[8:]
 
 
 def states_kernel(
     x_hbm, halo_hbm, inject_hbm, rate_hbm, weight_hbm, own_grad_hbm, log_hbm,
-    pay_ref,
+    pay_ref, act_hbm, slope_hbm, before_hbm,
     x_ref, halo_ref, inject_ref, rate_ref, weight_ref, own_grad_ref, log_ref, carry, prev,
-    xsem, isem, sems,
+    act_ref, slope_ref, before_ref, xsem, isem, sems, osems,
 ):
     spans = rate_ref.shape[0]
     pieces = [by_span(x_hbm, x_ref, xsem), by_span(inject_hbm, inject_ref, isem)]
+    outs = [
+        by_span(act_ref, act_hbm, osems.at[0]), by_span(slope_ref, slope_hbm, osems.at[1]),
+        by_span(before_ref, before_hbm, osems.at[2]),
+    ]
+    start = starting(pieces)
     late = pltpu.make_async_copy(own_grad_hbm, own_grad_ref, sems.at[4])
     fetch(
         spans,
@@ -172,7 +198,7 @@
             pltpu.make_async_copy(weight_hbm, weight_ref, sems.at[2]),
             pltpu.make_async_copy(log_hbm, log_ref, sems.at[3]),
         ],
-        pieces,
+        start,
     )
     late.start()
     carry[...] = jnp.zeros_like(carry)
@@ -180,18 +206,23 @@
     weights = weight_ref[...].astype(f32)
 
     def step(span):
-        for piece in pieces:
-            piece(span).wait()
         x = x_ref[span_at(span), :].astype(f32)
         preact = convolved(x, prev[...], weights)
         prev[...] = x[SPAN - 8 :]
-        act = (preact * jax.nn.sigmoid(preact)).astype(bf16)
+        squashed = jax.nn.sigmoid(preact)
+        act = (preact * squashed).astype(bf16)
+        act_ref[span_at(span), :] = act
+        slope_ref[span_at(span), :] = squashed * (1.0 + preact * (1.0 - squashed))
         rate = rate_ref[pl.ds(span, 1), :]
         tail = jnp.exp((SPAN - 1.0 - places()) * rate)
+        before = carry[...]
+        before_ref[span] = before
+        for out in outs:
+            out(span).start()
         fresh = dot2(inject_ref[span_at(span), :], act.astype(f32) * tail, TN)
-        carry[...] = jnp.exp(SPAN * rate) * carry[...] + fresh
-
-    each_span(spans, step)
+        carry[...] = jnp.exp(SPAN * rate) * before + fresh
+
+    each_span(spans, step, start, pieces)
     late.wait()
     chunks, height, _ = pay_ref.shape
     state_codes, state_power = coded(carry[...], 0)
@@ -202,6 +233,7 @@
         pay_ref[d, :, 0:LANES] = state_codes[rows, lanes]
         pay_ref[d, :, LANES : 2 * LANES] = grad_codes[rows, lanes]
         pay_ref[d, :, 2 * LANES :] = side[:, lanes]
+    drain(spans, outs)
 
 
 def chunk_place(d, height):
@@ -237,71 +269,45 @@
 
 
 def local_input_kernel(
-    x_hbm, halo_hbm, grad_hbm, inject_hbm, read_hbm, rate_hbm, later_hbm, weight_hbm,
-    act_hbm, pre_hbm, factor_hbm, after_hbm,
-    x_ref, halo_ref, grad_ref, inject_ref, read_ref, rate_ref, later_ref, weight_ref,
-    act_ref, pre_ref, factor_ref, after_ref, carry,
-    xsem, gsem, isem, rsem, sems, osems,
+    slope_hbm, grad_hbm, inject_hbm, read_hbm, after_hbm, rate_hbm, later_hbm,
+    pre_hbm, factor_hbm,
+    slope_ref, grad_ref, inject_ref, read_ref, after_ref, rate_ref, later_ref,
+    pre_ref, factor_ref, isems, sems, osems,
 ):
     spans = rate_ref.shape[0]
-    pieces = [
-        by_span(x_hbm, x_ref, xsem), by_span(grad_hbm, grad_ref, gsem),
-        by_span(inject_hbm, inject_ref, isem), by_span(read_hbm, read_ref, rsem),
-    ]
-    outs = [
-        by_span(act_ref, act_hbm, osems.at[0]), by_span(pre_ref, pre_hbm, osems.at[1]),
-        by_span(factor_ref, factor_hbm, osems.at[2]), by_span(after_ref, after_hbm, osems.at[3]),
-    ]
+    sources = [slope_hbm, grad_hbm, inject_hbm, read_hbm, after_hbm]
+    targets = [slope_ref, grad_ref, inject_ref, read_ref, after_ref]
+    pieces = [by_span(a, b, isems.at[k]) for k, (a, b) in enumerate(zip(sources, targets))]
+    start = starting(pieces)
+    outs = [by_span(pre_ref, pre_hbm, osems.at[0]), by_span(factor_ref, factor_hbm, osems.at[1])]
     fetch(
         spans,
         [
-            pltpu.make_async_copy(halo_hbm, halo_ref, sems.at[0]),
-            pltpu.make_async_copy(rate_hbm, rate_ref, sems.at[1]),
-            pltpu.make_async_copy(weight_hbm, weight_ref, sems.at[2]),
-            pltpu.make_async_copy(later_hbm, later_ref, sems.at[3]),
+            pltpu.make_async_copy(rate_hbm, rate_ref, sems.at[0]),
+            pltpu.make_async_copy(later_hbm, later_ref, sems.at[1]),
         ],
-        pieces,
-        backwards=True,
+        start,
     )
-    carry[...] = jnp.zeros_like(carry)
-    weights = weight_ref[...].astype(f32)
-    pieces[0](spans - 1).wait()
 
     def step(span):
-        @pl.when(span > 0)
-        def _():
-            pieces[0](jnp.maximum(span - 1, 0)).wait()
-
-        for piece in pieces[1:]:
-            piece(span).wait()
         rows = span_at(span)
-        x = x_ref[rows, :].astype(f32)
-        start = pl.multiple_of(jnp.maximum(span * SPAN - PREV, 0), PREV)
-        last = jnp.where(span == 0, halo_ref[...].astype(f32), x_ref[pl.ds(start, PREV), :].astype(f32))
-        preact = convolved(x, last[PREV - 8 :], weights)
-        squashed = jax.nn.sigmoid(preact)
-        act_ref[rows, :] = (preact * squashed).astype(bf16)
-        slope = squashed * (1.0 + preact * (1.0 - squashed))
         rate = rate_ref[pl.ds(span, 1), :]
         later = jnp.exp(later_ref[pl.ds(span, 1), :])
         inject, read = inject_ref[rows, :], read_ref[rows, :]
         here = places()
-        steep = slope * jnp.exp(-here * rate)
+        steep = slope_ref[rows, :] * jnp.exp(-here * rate)
         end = jnp.exp((SPAN - 1.0) * rate)
-        up_high, up_low = split(grad_ref[rows, :].astype(f32) * jnp.exp(here * rate))
+        up = (grad_ref[rows, :].astype(f32) * jnp.exp(here * rate)).astype(bf16)
         mixing = jnp.where(causal(), dot(read, inject, NT), 0.0).astype(bf16)
-        after = carry[...]
-        after_ref[span] = after
-        stacked = jnp.concatenate(split(after * end), axis=0)
+        stacked = jnp.concatenate(split(after_ref[span] * end), axis=0)
         doubled = jnp.concatenate([inject, inject], axis=1)
-        pre_ref[rows, :] = steep * (dot(mixing, up_high, TN) + dot(doubled, stacked, NN))
-        factor_ref[rows, :] = steep * (end * later)
-        fresh = dot(read, up_high, TN) + dot(read, up_low, TN)
-        carry[...] = jnp.exp(SPAN * rate) * after + jnp.exp(rate) * fresh
+        pre = steep * (dot(mixing, up, TN) + dot(doubled, stacked, NN))
+        pre_ref[rows, :] = pre.astype(bf16)
+        factor_ref[rows, :] = (steep * (end * later)).astype(bf16)
         for out in outs:
             out(span).start()
 
-    each_span(spans, step, backwards=True)
+    each_span(spans, step, start, pieces)
     drain(spans, outs)
 
 
@@ -311,23 +317,21 @@
 
 
 def local_shared_kernel(
-    grad_hbm, act_hbm, inject_hbm, read_hbm, after_hbm, rate_hbm,
+    grad_hbm, act_hbm, inject_hbm, read_hbm, after_hbm, before_hbm, rate_hbm,
     gi_hbm, gr_hbm,
-    grad_ref, act_ref, inject_ref, read_ref, after_ref, rate_ref,
-    gi_ref, gr_ref, carry,
+    grad_ref, act_ref, inject_ref, read_ref, after_ref, before_ref, rate_ref,
+    gi_ref, gr_ref,
     isems, sem, osems,
 ):
     spans = rate_ref.shape[0]
-    sources = [grad_hbm, act_hbm, inject_hbm, read_hbm, after_hbm]
-    targets = [grad_ref, act_ref, inject_ref, read_ref, after_ref]
+    sources = [grad_hbm, act_hbm, inject_hbm, read_hbm, after_hbm, before_hbm]
+    targets = [grad_ref, act_ref, inject_ref, read_ref, after_ref, before_ref]
     pieces = [by_span(a, b, isems.at[k]) for k, (a, b) in enumerate(zip(sources, targets))]
+    start = starting(pieces)
     outs = [by_span(gi_ref, gi_hbm, osems.at[0]), by_span(gr_ref, gr_hbm, osems.at[1])]
-    fetch(spans, [pltpu.make_async_copy(rate_hbm, rate_ref, sem)], pieces)
-    carry[...] = jnp.zeros_like(carry)
+    fetch(spans, [pltpu.make_async_copy(rate_hbm, rate_ref, sem)], start)
 
     def step(span):
-        for piece in pieces:
-            piece(span).wait()
         rows = span_at(span)
         rate = rate_ref[pl.ds(span, 1), :]
         inject, read = inject_ref[rows, :], read_ref[rows, :]
@@ -340,16 +344,13 @@
         pairs = jnp.where(causal(), dot(uph, downh, NT), 0.0).astype(bf16)
         end = jnp.exp((SPAN - 1.0) * rate)
         afters = jnp.concatenate(split(after_ref[span] * end), axis=0)
-        before = carry[...]
-        befores = jnp.concatenate(split(before * jnp.exp(rate)), axis=0)
+        befores = jnp.concatenate(split(before_ref[span] * jnp.exp(rate)), axis=0)
         gi_ref[rows, :] = dot(pairs, read, TN) + wide_product(downh, downl, afters, states)
         gr_ref[rows, :] = dot(pairs, inject, NN) + wide_product(uph, upl, befores, states)
-        fresh = dot(inject, downh, TN) + dot(inject, downl, TN)
-        carry[...] = jnp.exp(SPAN * rate) * before + end * fresh
         for out in outs:
             out(span).start()
 
-    each_span(spans, step)
+    each_span(spans, step, start, pieces)
     drain(spans, outs)
 
 
@@ -367,8 +368,8 @@
 
 def shared_kernel(
     grads_turn, core_ref, back_ref, grad_hbm, act_hbm, gr_hbm, gi_hbm, rate_hbm, prior_hbm, later_hbm,
-    out_ref,
-    in_ref, sum_ref, rate_ref, prior_ref, later_ref, both, isems, sems,
+    out_hbm,
+    in_ref, sum_ref, rate_ref, prior_ref, later_ref, both, out_ref, isems, sems, osems,
 ):
     tokens, states = sum_ref.shape
     spans = tokens // SPAN
@@ -381,25 +382,33 @@
     for copy in small:
         copy.start()
 
+    pieces = [by_span(grad_hbm, in_ref, isems.at[0]), by_span(gr_hbm, sum_ref, isems.at[1])]
+    others = [by_span(act_hbm, in_ref, isems.at[0]), by_span(gi_hbm, sum_ref, isems.at[1])]
+
+    def start(span):
+        @pl.when(readouts)
+        def _():
+            starting(pieces)(span)
+
+        @pl.when(jnp.logical_not(readouts))
+        def _():
+            starting(others)(span)
+
+    fetch(spans, [], start, ahead=spans)
+
     @pl.when(readouts)
     def _():
-        pieces = [by_span(grad_hbm, in_ref, isems.at[0]), by_span(gr_hbm, sum_ref, isems.at[1])]
-        fetch(spans, [], pieces)
         unpacked(back_ref, both, 0)
 
     @pl.when(jnp.logical_not(readouts))
     def _():
-        pieces = [by_span(act_hbm, in_ref, isems.at[0]), by_span(gi_hbm, sum_ref, isems.at[1])]
-        fetch(spans, [], pieces)
         unpacked(back_ref, both, 1)
 
     for copy in small:
         copy.wait()
-    arriving = [by_span(grad_hbm, in_ref, isems.at[0]), by_span(gr_hbm, sum_ref, isems.at[1])]
+    sending = by_span(out_ref, out_hbm, osems)
 
     def step(span):
-        for piece in arriving:
-            piece(span).wait()
         rows = span_at(span)
         rate = rate_ref[pl.ds(span, 1), :]
         ahead = rate + prior_ref[pl.ds(span, 1), :]
@@ -408,8 +417,10 @@
         offset = jnp.where(readouts, ahead, behind)
         high, low = split(in_ref[rows, :].astype(f32) * jnp.exp(places() * slope + offset))
         out_ref[rows, :] = sum_ref[rows, :] + wide_product(high, low, both[...], states)
-
-    each_span(spans, step)
+        sending(span).start()
+
+    each_span(spans, step, start, pieces, ahead=spans)
+    drain(spans, [sending])
 
 
 def input_kernel(
@@ -423,18 +434,17 @@
         by_span(inject_hbm, inject_ref, isems.at[2]),
     ]
     out = by_span(made, out_hbm, osems)
-    fetch(spans, [], pieces, backwards=True)
+    start = starting(pieces)
+    fetch(spans, [], start, backwards=True, ahead=spans)
     unpacked(back_ref, grads, 1)
     after[...] = jnp.zeros_like(after)
     weights = weight_ref[...].astype(f32)
 
     def step(span):
-        for piece in pieces:
-            piece(span).wait()
         rows = span_at(span)
         inject = inject_ref[rows, :]
         carried = dot(jnp.concatenate([inject, inject], axis=1), grads[...], NN)
-        now = pre_ref[rows, :] + factor_ref[rows, :] * carried
+        now = pre_ref[rows, :].astype(f32) + factor_ref[rows, :].astype(f32) * carried
         joined = jnp.concatenate([now, after[...]], axis=0)
         summed = weights[3:4] * now
         for k in range(3):
@@ -444,7 +454,7 @@
         made[rows, :] = summed
         out(span).start()
 
-    each_span(spans, step, backwards=True)
+    each_span(spans, step, start, pieces, backwards=True, ahead=spans)
     first_ref[...] = after[...]
     drain(spans, [out])
 
@@ -484,28 +494,29 @@
     halo_v, weight_v = pltpu.VMEM((PREV, channels), bf16), pltpu.VMEM(conv_weight.shape, bf16)
     dma = pltpu.SemaphoreType.DMA
 
-    rates, prior, later, own_log, own_grad = pl.pallas_call(
+    rates, prior, later, own_log, own_grad, after = pl.pallas_call(
         grads_kernel,
         in_specs=[hbm] * 3,
-        out_specs=[plain] * 5,
-        out_shape=[row, row, row, shape((1, channels), f32), state],
+        out_specs=[plain] * 5 + [hbm],
+        out_shape=[row, row, row, shape((1, channels), f32), state, local],
         scratch_shapes=[
-            pltpu.VMEM(decay_codes.shape, jnp.int32), wide16_v, narrow16_v,
-            dma, dma((spans,)), dma((spans,)),
+            pltpu.VMEM(decay_codes.shape, jnp.int32), wide16_v, narrow16_v, local_v,
+            dma, dma((spans,)), dma((spans,)), dma((spans,)),
         ],
         compiler_params=params(),
         cost_estimate=cost(4 * tokens * channels * states, 3 << 20),
         name="own_grads",
     )(decay_codes, grad_output, readout)
 
-    payload = pl.pallas_call(
+    payload, act, slope, before = pl.pallas_call(
         states_kernel,
         in_specs=[hbm, anywhere, hbm, anywhere, hbm, anywhere, anywhere],
-        out_specs=plain,
-        out_shape=shape(chunk, jnp.int16),
+        out_specs=[plain] + [hbm] * 3,
+        out_shape=[shape(chunk, jnp.int16), wide16, wide, local],
         scratch_shapes=[
             wide16_v, halo_v, narrow16_v, row_v, weight_v, state_v, pltpu.VMEM((1, channels), f32),
-            state_v, pltpu.VMEM((8, channels), f32), dma((spans,)), dma((spans,)), dma((5,)),
+            state_v, pltpu.VMEM((8, channels), f32), wide16_v, wide_v, local_v,
+            dma((spans,)), dma((spans,)), dma((5,)), dma((3, spans)),
         ],
         compiler_params=params(),
         cost_estimate=cost(4 * tokens * channels * states, 4 << 20),
@@ -514,33 +525,30 @@
 
     arrived = lax.all_to_all(payload, SEQ, 0, 0, tiled=True)
 
-    act, pre, factor, after = pl.pallas_call(
+    pre, factor = pl.pallas_call(
         local_input_kernel,
-        in_specs=[hbm, anywhere, hbm, hbm, hbm, anywhere, anywhere, hbm],
-        out_specs=[hbm] * 4,
-        out_shape=[wide16, wide, wide, local],
-        scratch_shapes=[
-            wide16_v, halo_v, wide16_v, narrow16_v, narrow16_v, row_v, row_v, weight_v,
-            wide16_v, wide_v, wide_v, local_v, state_v,
-        ]
-        + [dma((spans,))] * 4 + [dma((4,)), dma((4, spans))],
+        in_specs=[hbm] * 5 + [anywhere] * 2,
+        out_specs=[hbm] * 2,
+        out_shape=[wide16] * 2,
+        scratch_shapes=[wide_v, wide16_v, narrow16_v, narrow16_v, local_v, row_v, row_v]
+        + [wide16_v] * 2 + [dma((5, spans)), dma((2,)), dma((2, spans))],
         compiler_params=params(),
-        cost_estimate=cost(8 * tokens * channels * SPAN, 18 << 20),
+        cost_estimate=cost(8 * tokens * channels * SPAN, 13 << 20),
         name="local_input",
-    )(conv_input, halo, grad_output, inject, readout, rates, later, conv_weight)
-    arrived, act = lax.optimization_barrier((arrived, act))
+    )(slope, grad_output, inject, readout, after, rates, later)
+    arrived, pre = lax.optimization_barrier((arrived, pre))
 
     gi, gr = pl.pallas_call(
         local_shared_kernel,
-        in_specs=[hbm] * 5 + [anywhere],
+        in_specs=[hbm] * 6 + [anywhere],
         out_specs=[hbm] * 2,
         out_shape=[narrow] * 2,
-        scratch_shapes=[wide16_v] * 2 + [narrow16_v] * 2 + [local_v, row_v]
-        + [narrow_v] * 2 + [state_v] + [dma((5, spans)), dma, dma((2, spans))],
+        scratch_shapes=[wide16_v] * 2 + [narrow16_v] * 2 + [local_v, local_v, row_v]
+        + [narrow_v] * 2 + [dma((6, spans)), dma, dma((2, spans))],
         compiler_params=params(),
         cost_estimate=cost(12 * tokens * channels * SPAN, 9 << 20),
         name="local_shared",
-    )(grad_output, act, inject, readout, after, rates)
+    )(grad_output, act, inject, readout, after, before, rates)
 
     scanned = pl.pallas_call(
         scan_kernel,
@@ -559,9 +567,10 @@
         return pl.pallas_call(
             functools.partial(shared_kernel, turn),
             in_specs=[smem, plain] + [hbm] * 4 + [anywhere] * 3,
-            out_specs=plain,
+            out_specs=anywhere,
             out_shape=narrow,
-            scratch_shapes=[wide16_v, narrow_v] + [row_v] * 3 + [stacked, dma((2, spans)), dma((3,))],
+            scratch_shapes=[wide16_v, narrow_v] + [row_v] * 3
+            + [stacked, narrow_v, dma((2, spans)), dma((3,)), dma((spans,))],
             compiler_params=params(53),
             cost_estimate=cost(6 * tokens * channels * states, 4 << 20),
             name=f"shared_terms_{turn}",
@@ -587,7 +596,7 @@
         out_specs=[hbm, plain],
         out_shape=[wide, shape((8, channels), f32)],
         scratch_shapes=[
-            wide_v, wide_v, narrow16_v, stacked, pltpu.VMEM((8, channels), f32), wide_v,
+            wide16_v, wide16_v, narrow16_v, stacked, pltpu.VMEM((8, channels), f32), wide_v,
             dma((3, spans)), dma((spans,)),
         ],
         compiler_params=params(53),

time: 105 us -> 104 us (level)
  waiting for transfers between devices: 6.37 us -> 11.8 us
  Pallas kernels: 52.6 us -> 47.7 us
  starting transfers between devices: 39.1 us -> 37.6 us
    pallas_call x3, Pallas kernels: 27.7 us -> 22.6 us  [the longest x1 9.72 us: body(): pl.pallas_call(local_shared_kernel, in_specs=[hbm] * 6 + [anywhere], out_...]
    all_to_all x1, waiting for transfers between devices: 1.43 us -> 5.27 us  [body(): arrived = lax.all_to_all(payload, SEQ, 0, 0, tiled=True)]
    all_to_all x1, waiting for transfers between devices: 0.74 us -> 2.3 us  [body(): returned = lax.all_to_all(scanned, SEQ, 0, 0, tiled=True)]
    all_to_all x1, starting transfers between devices: 7.79 us -> 6.28 us  [body(): returned = lax.all_to_all(scanned, SEQ, 0, 0, tiled=True)]
  transfers between devices with their start and end apart: 12 -> 12, of which waited for: 4 -> 4; matrix products, arithmetic and copies ran while one was open for 1% -> 1% of each run, Pallas kernels for 37% -> 32%
where the time goes in v5:
time: 104 us
  Pallas kernels  47.7 us (46%)
  starting transfers between devices  37.6 us (36%)
  waiting for transfers between devices  11.8 us (11%)
  other arithmetic  4.36 us (4%)
  local copies, waits for them, and re-layouts  1.55 us (1%)
    all_to_all x1, starting transfers between devices, body(): arrived = lax.all_to_all(payload, SEQ, 0, 0, tiled=True)  10.4 us
    pallas_call x1, Pallas kernels, body(): pl.pallas_call(local_shared_kernel, in_specs=[hbm] * 6 + [anywhere], out_...  9.72 us
    pallas_call x2, Pallas kernels, shared(): pl.pallas_call(functools.partial(shared_kernel, turn), in_specs=[smem, pl...  9.24 us
    pallas_call x1, Pallas kernels, body(): pl.pallas_call(states_kernel, in_specs=[hbm, anywhere, hbm, anywhere, hbm...  8.76 us
    ppermute x6, starting transfers between devices, turn(): return lax.ppermute(array, 'y', [(i, (i + by) % ny) for i in range(ny)])  8.46 us
    pallas_call x1, Pallas kernels, body(): pl.pallas_call(local_input_kernel, in_specs=[hbm] * 5 + [anywhere] * 2, o...  7.23 us
    all_to_all x1, starting transfers between devices, body(): returned = lax.all_to_all(scanned, SEQ, 0, 0, tiled=True)  6.28 us
    pallas_call x1, Pallas kernels, body(): pl.pallas_call(input_kernel, in_specs=[plain] + [hbm] * 3 + [plain], out_...  6.02 us
  transfers between devices with their start and end apart: 12, of which 4 were waited for; matrix products, arithmetic and copies ran while one was open for 1% of the time, Pallas kernels for 32%

profile of v5, /device:TPU:7, one launch (start us, length us, event | category | flops | bytes accessed | tf_op | source)
XLA Modules:
  0.0 103.8 jit_solution(8134116067304796784)
XLA Ops:
  0.6 0.7 slice.30
  1.4 3.4 %collective-permute-start = (bf16[16,512]{1,0:T(8,128)(2,1)S(1)}, bf16[16,512]{1,0:T(8,128)(2,1)S(1)}, u32[]{:S(2)}, u32[]{:S(2)}) collective-permute-start(bf16[16,512]{1,0:T(8,128)(2,1)S(1)} %slice.30), channel_id=1, source_target_pairs={{0,8},{8,16},{16,24},{24,32},{32,40},{40,48},{48,56},{56,64},{64,7... | collective-permute-start | bytes 49160 | tf_op jit(solution)/shard_map/ppermute | solution.py:485
  4.8 5.6 %own_grads.1 = (f32[8,512]{1,0:T(8,128)}, f32[8,512]{1,0:T(8,128)}, f32[8,512]{1,0:T(8,128)}, f32[1,512]{1,0:T(1,128)}, f32[128,512]{1,0:T(8,128)}, /*index=5*/f32[8,128,512]{2,1,0:T(8,128)}) custom-call(s32[8,8]{1,0:T(8,128)} %code_hbm.1, bf16[2048,512]{1,0:T(8,128)(2,1)} %grad_hbm.9, bf16[2048,128]{1,0:T(8,128)(2,1)} %read_hbm.5), custom_call_target="tpu_custom_call" | custom-call | flops 536870912 | bytes 3145728 | tf_op jit(solution)/shard_map/own_grads/pallas_call | solution.py:497
  10.5 0.6 copy-done.5
  11.0 8.8 %own_states.1 = (s16[32,16,384]{2,1,0:T(8,128)(2,1)}, bf16[2048,512]{1,0:T(8,128)(2,1)}, f32[2048,512]{1,0:T(8,128)}, f32[8,128,512]{2,1,0:T(8,128)}) custom-call(bf16[2048,512]{1,0:T(8,128)(2,1)} %x_hbm.1, bf16[16,512]{1,0:T(8,128)(2,1)} %copy-done.5, bf16[2048,128]{1,0:T(8,128)(2,1)} %inject_hbm.7, f32[8,512]{1,0:T(8,128)} %get-tuple-element.29.rate_hbm, ...), custom_call_target="tpu_custom_call" | custom-call | flops 536870912 | bytes 4194304 | tf_op jit(solution)/shard_map/own_states/pallas_call | solution.py:511
  19.8 10.4 %all-to-all-start = ((s16[32,16,384]{2,1,0:T(8,128)(2,1)}), s16[32,16,384]{2,1,0:T(8,128)(2,1)S(1)}, u32[]{:S(2)}, u32[]{:S(2)}) async-start(s16[32,16,384]{2,1,0:T(8,128)(2,1)} %get-tuple-element.32), calls=%async_computation | async-start | bytes 786432 | tf_op jit(solution)/shard_map/all_to_all | solution.py:526
  30.2 7.2 %local_input.1 = (bf16[2048,512]{1,0:T(8,128)(2,1)}, bf16[2048,512]{1,0:T(8,128)(2,1)}) custom-call(f32[2048,512]{1,0:T(8,128)} %get-tuple-element.33.slope_hbm, bf16[2048,512]{1,0:T(8,128)(2,1)} %grad_hbm.9, bf16[2048,128]{1,0:T(8,128)(2,1)} %inject_hbm.7, bf16[2048,128]{1,0:T(8,128)(2,1)} %read_hbm.5, f32[8,128,512]{2,1,0:T(8,128)} %get-tuple-element.34.after_hbm, ...), custom_call_target="tpu_custom_call" | custom-call | flops 2147483648 | bytes 13631488 | tf_op jit(solution)/shard_map/local_input/pallas_call | solution.py:528
  37.4 5.3 %all-to-all-done.own_ref = s16[32,16,384]{2,1,0:T(8,128)(2,1)S(1)} async-done(((s16[32,16,384]{2,1,0:T(8,128)(2,1)}), s16[32,16,384]{2,1,0:T(8,128)(2,1)S(1)}, u32[]{:S(2)}, u32[]{:S(2)}) %all-to-all-start) | async-done | bytes 393248 | tf_op jit(solution)/shard_map/all_to_all | solution.py:526
  42.7 1.1 %carry.1 = s16[32,16,384]{2,1,0:T(8,128)(2,1)} custom-call(s16[32,16,384]{2,1,0:T(8,128)(2,1)S(1)} %all-to-all-done.own_ref), custom_call_target="tpu_custom_call" | custom-call | flops 262144 | bytes 1048576 | tf_op jit(solution)/shard_map/carry/pallas_call | solution.py:553
  43.8 6.3 %all-to-all-start.1 = ((s16[32,16,384]{2,1,0:T(8,128)(2,1)}), s16[32,16,384]{2,1,0:T(8,128)(2,1)S(1)}, u32[]{:S(2)}, u32[]{:S(2)}) async-start(s16[32,16,384]{2,1,0:T(8,128)(2,1)} %carry.1), calls=%async_computation.1 | async-start | bytes 786432 | tf_op jit(solution)/shard_map/all_to_all | solution.py:561
  50.1 9.7 %local_shared.1 = (f32[2048,128]{1,0:T(8,128)}, f32[2048,128]{1,0:T(8,128)}) custom-call(bf16[2048,512]{1,0:T(8,128)(2,1)} %grad_hbm.9, bf16[2048,512]{1,0:T(8,128)(2,1)} %get-tuple-element.41.act_hbm, bf16[2048,128]{1,0:T(8,128)(2,1)} %inject_hbm.7, bf16[2048,128]{1,0:T(8,128)(2,1)} %read_hbm.5, f32[8,128,512]{2,1,0:T(8,128)} %get-tuple-element.34.after_hbm, ...), custom_call_target="tpu_custom_call" | custom-call | flops 3221225472 | bytes 9437184 | tf_op jit(solution)/shard_map/local_shared/pallas_call | solution.py:541
  59.8 2.3 %all-to-all-done.1.back_ref = s16[32,16,384]{2,1,0:T(8,128)(2,1)S(1)} async-done(((s16[32,16,384]{2,1,0:T(8,128)(2,1)}), s16[32,16,384]{2,1,0:T(8,128)(2,1)S(1)}, u32[]{:S(2)}, u32[]{:S(2)}) %all-to-all-start.1) | async-done | bytes 393248 | tf_op jit(solution)/shard_map/all_to_all | solution.py:561
  62.2 4.6 %shared_terms_0.1 = f32[2048,128]{1,0:T(8,128)} custom-call(s32[1]{0:T(128)} %bitcast.core_ref, s16[32,16,384]{2,1,0:T(8,128)(2,1)S(1)} %all-to-all-done.1.back_ref, bf16[2048,512]{1,0:T(8,128)(2,1)} %grad_hbm.9, bf16[2048,512]{1,0:T(8,128)(2,1)} %get-tuple-element.41.act_hbm, f32[2048,128]{1,0:T(8,128)} %get-tuple-element.43.gr_hbm, ...), custom_call_target="tpu_custom_call" | custom-call | flops 805306368 | bytes 4194304 | tf_op jit(solution)/shard_map/shared_terms_0/pallas_call | solution.py:567
  66.8 3.3 %collective-permute-start.1 = (f32[2048,128]{1,0:T(8,128)}, f32[2048,128]{1,0:T(8,128)S(1)}, u32[]{:S(2)}, u32[]{:S(2)}) collective-permute-start(f32[2048,128]{1,0:T(8,128)} %shared_terms_0.1), channel_id=1, source_target_pairs={{0,1},{1,0},{2,3},{3,2},{4,5},{5,4},{6,7},{7,6},{8,9},{9,8},{10,11... | collective-permute-start | bytes 3145736 | tf_op jit(solution)/shard_map/ppermute | solution.py:580
  70.1 4.6 %shared_terms_1.1 = f32[2048,128]{1,0:T(8,128)} custom-call(s32[1]{0:T(128)} %bitcast.core_ref, s16[32,16,384]{2,1,0:T(8,128)(2,1)S(1)} %all-to-all-done.1.back_ref, bf16[2048,512]{1,0:T(8,128)(2,1)} %grad_hbm.9, bf16[2048,512]{1,0:T(8,128)(2,1)} %get-tuple-element.41.act_hbm, f32[2048,128]{1,0:T(8,128)} %get-tuple-element.43.gr_hbm, ...), custom_call_target="tpu_custom_call" | custom-call | flops 805306368 | bytes 4194304 | tf_op jit(solution)/shard_map/shared_terms_1/pallas_call | solution.py:567
  74.7 1.4 %add.69 = f32[2048,128]{1,0:T(8,128)S(1)} add(f32[2048,128]{1,0:T(8,128)} %shared_terms_1.1, f32[2048,128]{1,0:T(8,128)S(1)} %collective-permute-done.1) | non-fusion elementwise | flops 262144 | bytes 3145728 | tf_op jit(solution)/shard_map/add | solution.py:581
  76.1 0.1 dynamic-slice_convert_fusion
  76.2 1.4 %collective-permute-start.2 = (bf16[512,128]{1,0:T(8,128)(2,1)S(1)}, bf16[512,128]{1,0:T(8,128)(2,1)S(1)}, u32[]{:S(2)}, u32[]{:S(2)}) collective-permute-start(bf16[512,128]{1,0:T(8,128)(2,1)S(1)} %get-tuple-element.61), channel_id=1, source_target_pairs={{0,2},{2,4},{4,6},{6,0},{1,3},{3,5},{5,7},{7,1},{8,10},{10,12},{12... | collective-permute-start | bytes 393224 | tf_op jit(solution)/shard_map/ppermute | solution.py:586
  77.6 2.6 %collective-permute-start.3 = (bf16[512,128]{1,0:T(8,128)(2,1)S(1)}, bf16[512,128]{1,0:T(8,128)(2,1)S(1)}, u32[]{:S(2)}, u32[]{:S(2)}) collective-permute-start(bf16[512,128]{1,0:T(8,128)(2,1)S(1)} %get-tuple-element.60), channel_id=1, source_target_pairs={{0,4},{2,6},{4,0},{6,2},{1,5},{3,7},{5,1},{7,3},{8,12},{10,14},{12... | collective-permute-start | bytes 393224 | tf_op jit(solution)/shard_map/ppermute | solution.py:586
  80.2 1.1 %collective-permute-start.4 = (bf16[512,128]{1,0:T(8,128)(2,1)S(1)}, bf16[512,128]{1,0:T(8,128)(2,1)S(1)}, u32[]{:S(2)}, u32[]{:S(2)}) collective-permute-start(bf16[512,128]{1,0:T(8,128)(2,1)S(1)} %get-tuple-element.59), channel_id=1, source_target_pairs={{0,6},{2,0},{4,2},{6,4},{1,7},{3,1},{5,3},{7,5},{8,14},{10,8},{12,... | collective-permute-start | bytes 393224 | tf_op jit(solution)/shard_map/ppermute | solution.py:586
  81.3 6.0 %input_grads.1 = (f32[2048,512]{1,0:T(8,128)}, f32[8,512]{1,0:T(8,128)S(1)}) custom-call(s16[32,16,384]{2,1,0:T(8,128)(2,1)S(1)} %all-to-all-done.1.back_ref, bf16[2048,512]{1,0:T(8,128)(2,1)} %get-tuple-element.38.pre_hbm, bf16[2048,512]{1,0:T(8,128)(2,1)} %get-tuple-element.39.factor_hbm, bf16[2048,128]{1,0:T(8,128)(2,1)S(1)} %copy-done, ...), custom_call_target="tpu_custom_call" | custom-call | flops 536870912 | bytes 13631488 | tf_op jit(solution)/shard_map/input_grads/pallas_call | solution.py:593
  87.3 0.1 broadcast_in_dim.7
  87.4 0.1 constant_dynamic-update-slice_fusion.3
  87.5 0.5 collective-permute-start.5
  88.0 2.0 %collective-permute-start.6 = (bf16[512,128]{1,0:T(8,128)(2,1)S(1)}, bf16[512,128]{1,0:T(8,128)(2,1)S(1)}, u32[]{:S(2)}, u32[]{:S(2)}) collective-permute-start(bf16[512,128]{1,0:T(8,128)(2,1)S(1)} %get-tuple-element.56), channel_id=1, source_target_pairs={{0,4},{2,6},{4,0},{6,2},{1,5},{3,7},{5,1},{7,3},{8,12},{10,14},{12... | collective-permute-start | bytes 393224 | tf_op jit(solution)/shard_map/ppermute | solution.py:586
  90.0 0.9 collective-permute-start.7
  90.9 2.5 %collective-permute-start.8 = (f32[8,512]{1,0:T(8,128)S(1)}, f32[8,512]{1,0:T(8,128)S(1)}, u32[]{:S(2)}, u32[]{:S(2)}) collective-permute-start(f32[8,512]{1,0:T(8,128)S(1)} %get-tuple-element.50), channel_id=1, source_target_pairs={{8,0},{16,8},{24,16},{32,24},{40,32},{48,40},{56,48},{64,56},{72,6... | collective-permute-start | bytes 49160 | tf_op jit(solution)/shard_map/ppermute | solution.py:613
  93.4 4.1 %collective-permute-done.8 = f32[8,512]{1,0:T(8,128)S(1)} collective-permute-done((f32[8,512]{1,0:T(8,128)S(1)}, f32[8,512]{1,0:T(8,128)S(1)}, u32[]{:S(2)}, u32[]{:S(2)}) %collective-permute-start.8) | collective-permute-done | bytes 16416 | tf_op jit(solution)/shard_map/ppermute | solution.py:613
  97.6 3.2 %collective-permute-start.9 = (bf16[2048,128]{1,0:T(8,128)(2,1)S(1)}, bf16[2048,128]{1,0:T(8,128)(2,1)S(1)}, u32[]{:S(2)}, u32[]{:S(2)}) collective-permute-start(bf16[2048,128]{1,0:T(8,128)(2,1)S(1)} %constant_dynamic-update-slice_fusion), channel_id=1, source_target_pairs={{0,1},{1,0},{2,3},{3,2},{4,5},{5,4},{6,7},{7,6},{8,9},{9,8},{10,11... | collective-permute-start | bytes 1572872 | tf_op jit(solution)/shard_map/ppermute | solution.py:620
  100.9 1.4 %fusion = f32[2048,512]{1,0:T(8,128)} fusion(f32[2048,512]{1,0:T(8,128)} %get-tuple-element.40, f32[1,512]{1,0:T(1,128)S(1)} %get-tuple-element.63, f32[1,512]{1,0:T(1,128)S(1)} %get-tuple-element.64, f32[1,512]{1,0:T(1,128)S(1)} %get-tuple-element.62, f32[8]{0:T(128)S(1)} %pad.clone), kind=kLoop, calls=%fused_computation.7 | loop fusion | flops 16384 | bytes 38944 | tf_op jit(solution)/shard_map/dynamic_update_slice | solution.py:631
  102.3 0.1 collective-permute-done.9
  102.4 1.5 %select_convert_fusion = (f32[2048,128]{1,0:T(8,128)}, f32[2048,128]{1,0:T(8,128)}) fusion(bf16[2048,128]{1,0:T(8,128)(2,1)S(1)} %collective-permute-done.9, bf16[2048,128]{1,0:T(8,128)(2,1)S(1)} %constant_dynamic-update-slice_fusion, pred[]{:T(512)S(6)} %eq.3), kind=kLoop, calls=%fused_computation | loop fusion | flops 1048576 | bytes 3145729 | tf_op jit(solution)/shard_map/convert_element_type | solution.py:623
  (26 shorter events, 0.1 us)
Async XLA Ops:
  1.4 9.1 %collective-permute-start = (bf16[16,512]{1,0:T(8,128)(2,1)S(1)}, bf16[16,512]{1,0:T(8,128)(2,1)S(1)}, u32[]{:S(2)}, u32[]{:S(2)}) collective-permute-start(bf16[16,512]{1,0:T(8,128)(2,1)S(1)} %slice.30), channel_id=1, source_target_pairs={{0,8},{8,16},{16,24},{24,32},{32,40},{40,48},{48,56},{56,64},{64,7... | collective-permute-start | bytes 49160 | tf_op jit(solution)/shard_map/ppermute | solution.py:485
  10.4 0.6 copy-start.5
  19.8 22.9 %all-to-all-start = ((s16[32,16,384]{2,1,0:T(8,128)(2,1)}), s16[32,16,384]{2,1,0:T(8,128)(2,1)S(1)}, u32[]{:S(2)}, u32[]{:S(2)}) async-start(s16[32,16,384]{2,1,0:T(8,128)(2,1)} %get-tuple-element.32), calls=%async_computation | async-start | bytes 786432 | tf_op jit(solution)/shard_map/all_to_all | solution.py:526
  43.8 18.3 %all-to-all-start.1 = ((s16[32,16,384]{2,1,0:T(8,128)(2,1)}), s16[32,16,384]{2,1,0:T(8,128)(2,1)S(1)}, u32[]{:S(2)}, u32[]{:S(2)}) async-start(s16[32,16,384]{2,1,0:T(8,128)(2,1)} %carry.1), calls=%async_computation.1 | async-start | bytes 786432 | tf_op jit(solution)/shard_map/all_to_all | solution.py:561
  50.1 12.1 %copy-start.1 = (f32[8,512]{1,0:T(8,128)S(1)}, f32[8,512]{1,0:T(8,128)}, u32[]{:S(2)}) copy-start(f32[8,512]{1,0:T(8,128)} %get-tuple-element.29.rate_hbm) | copy-start | bytes 49156
  50.1 12.0 %copy-start.2 = (f32[8,512]{1,0:T(8,128)S(1)}, f32[8,512]{1,0:T(8,128)}, u32[]{:S(2)}) copy-start(f32[8,512]{1,0:T(8,128)} %get-tuple-element.35.later_hbm) | copy-start | bytes 49156
  50.1 12.0 %copy-start.3 = (f32[8,512]{1,0:T(8,128)S(1)}, f32[8,512]{1,0:T(8,128)}, u32[]{:S(2)}) copy-start(f32[8,512]{1,0:T(8,128)} %get-tuple-element.45.prior_hbm) | copy-start | bytes 49156
  66.8 7.9 %collective-permute-start.1 = (f32[2048,128]{1,0:T(8,128)}, f32[2048,128]{1,0:T(8,128)S(1)}, u32[]{:S(2)}, u32[]{:S(2)}) collective-permute-start(f32[2048,128]{1,0:T(8,128)} %shared_terms_0.1), channel_id=1, source_target_pairs={{0,1},{1,0},{2,3},{3,2},{4,5},{5,4},{6,7},{7,6},{8,9},{9,8},{10,11... | collective-permute-start | bytes 3145736 | tf_op jit(solution)/shard_map/ppermute | solution.py:580
  74.7 6.6 %copy-start = (bf16[2048,128]{1,0:T(8,128)(2,1)S(1)}, bf16[2048,128]{1,0:T(8,128)(2,1)}, u32[]{:S(2)}) copy-start(bf16[2048,128]{1,0:T(8,128)(2,1)} %inject_hbm.7) | copy-start | bytes 1572868
  74.7 6.6 %copy-start.4 = (bf16[4,512]{1,0:T(4,128)(2,1)S(1)}, bf16[4,512]{1,0:T(4,128)(2,1)}, u32[]{:S(2)}) copy-start(bf16[4,512]{1,0:T(4,128)(2,1)} %weight_ref.1) | copy-start | bytes 12292
  76.2 11.1 %collective-permute-start.2 = (bf16[512,128]{1,0:T(8,128)(2,1)S(1)}, bf16[512,128]{1,0:T(8,128)(2,1)S(1)}, u32[]{:S(2)}, u32[]{:S(2)}) collective-permute-start(bf16[512,128]{1,0:T(8,128)(2,1)S(1)} %get-tuple-element.61), channel_id=1, source_target_pairs={{0,2},{2,4},{4,6},{6,0},{1,3},{3,5},{5,7},{7,1},{8,10},{10,12},{12... | collective-permute-start | bytes 393224 | tf_op jit(solution)/shard_map/ppermute | solution.py:586
  77.6 9.7 %collective-permute-start.3 = (bf16[512,128]{1,0:T(8,128)(2,1)S(1)}, bf16[512,128]{1,0:T(8,128)(2,1)S(1)}, u32[]{:S(2)}, u32[]{:S(2)}) collective-permute-start(bf16[512,128]{1,0:T(8,128)(2,1)S(1)} %get-tuple-element.60), channel_id=1, source_target_pairs={{0,4},{2,6},{4,0},{6,2},{1,5},{3,7},{5,1},{7,3},{8,12},{10,14},{12... | collective-permute-start | bytes 393224 | tf_op jit(solution)/shard_map/ppermute | solution.py:586
  80.2 7.1 %collective-permute-start.4 = (bf16[512,128]{1,0:T(8,128)(2,1)S(1)}, bf16[512,128]{1,0:T(8,128)(2,1)S(1)}, u32[]{:S(2)}, u32[]{:S(2)}) collective-permute-start(bf16[512,128]{1,0:T(8,128)(2,1)S(1)} %get-tuple-element.59), channel_id=1, source_target_pairs={{0,6},{2,0},{4,2},{6,4},{1,7},{3,1},{5,3},{7,5},{8,14},{10,8},{12,... | collective-permute-start | bytes 393224 | tf_op jit(solution)/shard_map/ppermute | solution.py:586
  87.5 10.0 %collective-permute-start.5 = (bf16[512,128]{1,0:T(8,128)(2,1)S(1)}, bf16[512,128]{1,0:T(8,128)(2,1)S(1)}, u32[]{:S(2)}, u32[]{:S(2)}) collective-permute-start(bf16[512,128]{1,0:T(8,128)(2,1)S(1)} %get-tuple-element.56), channel_id=1, source_target_pairs={{0,2},{2,4},{4,6},{6,0},{1,3},{3,5},{5,7},{7,1},{8,10},{10,12},{12... | collective-permute-start | bytes 393224 | tf_op jit(solution)/shard_map/ppermute | solution.py:586
  88.0 9.5 %collective-permute-start.6 = (bf16[512,128]{1,0:T(8,128)(2,1)S(1)}, bf16[512,128]{1,0:T(8,128)(2,1)S(1)}, u32[]{:S(2)}, u32[]{:S(2)}) collective-permute-start(bf16[512,128]{1,0:T(8,128)(2,1)S(1)} %get-tuple-element.56), channel_id=1, source_target_pairs={{0,4},{2,6},{4,0},{6,2},{1,5},{3,7},{5,1},{7,3},{8,12},{10,14},{12... | collective-permute-start | bytes 393224 | tf_op jit(solution)/shard_map/ppermute | solution.py:586
  90.0 7.5 %collective-permute-start.7 = (bf16[512,128]{1,0:T(8,128)(2,1)S(1)}, bf16[512,128]{1,0:T(8,128)(2,1)S(1)}, u32[]{:S(2)}, u32[]{:S(2)}) collective-permute-start(bf16[512,128]{1,0:T(8,128)(2,1)S(1)} %get-tuple-element.56), channel_id=1, source_target_pairs={{0,6},{2,0},{4,2},{6,4},{1,7},{3,1},{5,3},{7,5},{8,14},{10,8},{12,... | collective-permute-start | bytes 393224 | tf_op jit(solution)/shard_map/ppermute | solution.py:586
  90.9 6.6 %collective-permute-start.8 = (f32[8,512]{1,0:T(8,128)S(1)}, f32[8,512]{1,0:T(8,128)S(1)}, u32[]{:S(2)}, u32[]{:S(2)}) collective-permute-start(f32[8,512]{1,0:T(8,128)S(1)} %get-tuple-element.50), channel_id=1, source_target_pairs={{8,0},{16,8},{24,16},{32,24},{40,32},{48,40},{56,48},{64,56},{72,6... | collective-permute-start | bytes 49160 | tf_op jit(solution)/shard_map/ppermute | solution.py:613
  97.6 4.8 %collective-permute-start.9 = (bf16[2048,128]{1,0:T(8,128)(2,1)S(1)}, bf16[2048,128]{1,0:T(8,128)(2,1)S(1)}, u32[]{:S(2)}, u32[]{:S(2)}) collective-permute-start(bf16[2048,128]{1,0:T(8,128)(2,1)S(1)} %constant_dynamic-update-slice_fusion), channel_id=1, source_target_pairs={{0,1},{1,0},{2,3},{3,2},{4,5},{5,4},{6,7},{7,6},{8,9},{9,8},{10,11... | collective-permute-start | bytes 1572872 | tf_op jit(solution)/shard_map/ppermute | solution.py:620

commit v6 on v5

--- a/solution.py
+++ b/solution.py
@@ -178,16 +178,13 @@
 
 def states_kernel(
     x_hbm, halo_hbm, inject_hbm, rate_hbm, weight_hbm, own_grad_hbm, log_hbm,
-    pay_ref, act_hbm, slope_hbm, before_hbm,
+    pay_ref, before_hbm,
     x_ref, halo_ref, inject_ref, rate_ref, weight_ref, own_grad_ref, log_ref, carry, prev,
-    act_ref, slope_ref, before_ref, xsem, isem, sems, osems,
+    before_ref, xsem, isem, sems, osem,
 ):
     spans = rate_ref.shape[0]
     pieces = [by_span(x_hbm, x_ref, xsem), by_span(inject_hbm, inject_ref, isem)]
-    outs = [
-        by_span(act_ref, act_hbm, osems.at[0]), by_span(slope_ref, slope_hbm, osems.at[1]),
-        by_span(before_ref, before_hbm, osems.at[2]),
-    ]
+    sending = by_span(before_ref, before_hbm, osem)
     start = starting(pieces)
     late = pltpu.make_async_copy(own_grad_hbm, own_grad_ref, sems.at[4])
     fetch(
@@ -209,16 +206,12 @@
         x = x_ref[span_at(span), :].astype(f32)
         preact = convolved(x, prev[...], weights)
         prev[...] = x[SPAN - 8 :]
-        squashed = jax.nn.sigmoid(preact)
-        act = (preact * squashed).astype(bf16)
-        act_ref[span_at(span), :] = act
-        slope_ref[span_at(span), :] = squashed * (1.0 + preact * (1.0 - squashed))
+        act = (preact * jax.nn.sigmoid(preact)).astype(bf16)
         rate = rate_ref[pl.ds(span, 1), :]
         tail = jnp.exp((SPAN - 1.0 - places()) * rate)
         before = carry[...]
         before_ref[span] = before
-        for out in outs:
-            out(span).start()
+        sending(span).start()
         fresh = dot2(inject_ref[span_at(span), :], act.astype(f32) * tail, TN)
         carry[...] = jnp.exp(SPAN * rate) * before + fresh
 
@@ -233,7 +226,7 @@
         pay_ref[d, :, 0:LANES] = state_codes[rows, lanes]
         pay_ref[d, :, LANES : 2 * LANES] = grad_codes[rows, lanes]
         pay_ref[d, :, 2 * LANES :] = side[:, lanes]
-    drain(spans, outs)
+    drain(spans, [sending])
 
 
 def chunk_place(d, height):
@@ -269,25 +262,32 @@
 
 
 def local_input_kernel(
-    slope_hbm, grad_hbm, inject_hbm, read_hbm, after_hbm, rate_hbm, later_hbm,
-    pre_hbm, factor_hbm,
-    slope_ref, grad_ref, inject_ref, read_ref, after_ref, rate_ref, later_ref,
-    pre_ref, factor_ref, isems, sems, osems,
+    x_hbm, grad_hbm, inject_hbm, read_hbm, after_hbm, rate_hbm, later_hbm, halo_hbm, weight_hbm,
+    act_hbm, pre_hbm, factor_hbm,
+    x_ref, grad_ref, inject_ref, read_ref, after_ref, rate_ref, later_ref, halo_ref, weight_ref,
+    act_ref, pre_ref, factor_ref, prev, isems, sems, osems,
 ):
     spans = rate_ref.shape[0]
-    sources = [slope_hbm, grad_hbm, inject_hbm, read_hbm, after_hbm]
-    targets = [slope_ref, grad_ref, inject_ref, read_ref, after_ref]
+    sources = [x_hbm, grad_hbm, inject_hbm, read_hbm, after_hbm]
+    targets = [x_ref, grad_ref, inject_ref, read_ref, after_ref]
     pieces = [by_span(a, b, isems.at[k]) for k, (a, b) in enumerate(zip(sources, targets))]
     start = starting(pieces)
-    outs = [by_span(pre_ref, pre_hbm, osems.at[0]), by_span(factor_ref, factor_hbm, osems.at[1])]
+    outs = [
+        by_span(act_ref, act_hbm, osems.at[0]), by_span(pre_ref, pre_hbm, osems.at[1]),
+        by_span(factor_ref, factor_hbm, osems.at[2]),
+    ]
     fetch(
         spans,
         [
             pltpu.make_async_copy(rate_hbm, rate_ref, sems.at[0]),
             pltpu.make_async_copy(later_hbm, later_ref, sems.at[1]),
+            pltpu.make_async_copy(halo_hbm, halo_ref, sems.at[2]),
+            pltpu.make_async_copy(weight_hbm, weight_ref, sems.at[3]),
         ],
         start,
     )
+    prev[...] = halo_ref[...].astype(f32)[PREV - 8 :]
+    weights = weight_ref[...].astype(f32)
 
     def step(span):
         rows = span_at(span)
@@ -295,7 +295,13 @@
         later = jnp.exp(later_ref[pl.ds(span, 1), :])
         inject, read = inject_ref[rows, :], read_ref[rows, :]
         here = places()
-        steep = slope_ref[rows, :] * jnp.exp(-here * rate)
+        x = x_ref[rows, :].astype(f32)
+        preact = convolved(x, prev[...], weights)
+        prev[...] = x[SPAN - 8 :]
+        squashed = jax.nn.sigmoid(preact)
+        act_ref[rows, :] = (preact * squashed).astype(bf16)
+        slope = squashed * (1.0 + preact * (1.0 - squashed))
+        steep = slope * jnp.exp(-here * rate)
         end = jnp.exp((SPAN - 1.0) * rate)
         up = (grad_ref[rows, :].astype(f32) * jnp.exp(here * rate)).astype(bf16)
         mixing = jnp.where(causal(), dot(read, inject, NT), 0.0).astype(bf16)
@@ -446,10 +452,10 @@
         carried = dot(jnp.concatenate([inject, inject], axis=1), grads[...], NN)
         now = pre_ref[rows, :].astype(f32) + factor_ref[rows, :].astype(f32) * carried
         joined = jnp.concatenate([now, after[...]], axis=0)
-        summed = weights[3:4] * now
-        for k in range(3):
-            ahead = pltpu.roll(joined, SPAN + 8 - (3 - k), axis=0)[:SPAN]
-            summed = summed + weights[k : k + 1] * ahead
+        one = pltpu.roll(joined, SPAN + 8 - 1, axis=0)
+        further = weights[1:2] * joined + weights[0:1] * one
+        summed = weights[3:4] * now + weights[2:3] * one[:SPAN]
+        summed = summed + pltpu.roll(further, SPAN + 8 - 2, axis=0)[:SPAN]
         after[...] = now[0:8]
         made[rows, :] = summed
         out(span).start()
@@ -508,15 +514,15 @@
         name="own_grads",
     )(decay_codes, grad_output, readout)
 
-    payload, act, slope, before = pl.pallas_call(
+    payload, before = pl.pallas_call(
         states_kernel,
         in_specs=[hbm, anywhere, hbm, anywhere, hbm, anywhere, anywhere],
-        out_specs=[plain] + [hbm] * 3,
-        out_shape=[shape(chunk, jnp.int16), wide16, wide, local],
+        out_specs=[plain, hbm],
+        out_shape=[shape(chunk, jnp.int16), local],
         scratch_shapes=[
             wide16_v, halo_v, narrow16_v, row_v, weight_v, state_v, pltpu.VMEM((1, channels), f32),
-            state_v, pltpu.VMEM((8, channels), f32), wide16_v, wide_v, local_v,
-            dma((spans,)), dma((spans,)), dma((5,)), dma((3, spans)),
+            state_v, pltpu.VMEM((8, channels), f32), local_v,
+            dma((spans,)), dma((spans,)), dma((5,)), dma((spans,)),
         ],
         compiler_params=params(),
         cost_estimate=cost(4 * tokens * channels * states, 4 << 20),
@@ -525,18 +531,19 @@
 
     arrived = lax.all_to_all(payload, SEQ, 0, 0, tiled=True)
 
-    pre, factor = pl.pallas_call(
+    act, pre, factor = pl.pallas_call(
         local_input_kernel,
-        in_specs=[hbm] * 5 + [anywhere] * 2,
-        out_specs=[hbm] * 2,
-        out_shape=[wide16] * 2,
-        scratch_shapes=[wide_v, wide16_v, narrow16_v, narrow16_v, local_v, row_v, row_v]
-        + [wide16_v] * 2 + [dma((5, spans)), dma((2,)), dma((2, spans))],
+        in_specs=[hbm] * 5 + [anywhere] * 3 + [hbm],
+        out_specs=[hbm] * 3,
+        out_shape=[wide16] * 3,
+        scratch_shapes=[wide16_v, wide16_v, narrow16_v, narrow16_v, local_v, row_v, row_v]
+        + [halo_v, weight_v] + [wide16_v] * 3 + [pltpu.VMEM((8, channels), f32)]
+        + [dma((5, spans)), dma((4,)), dma((3, spans))],
         compiler_params=params(),
         cost_estimate=cost(8 * tokens * channels * SPAN, 13 << 20),
         name="local_input",
-    )(slope, grad_output, inject, readout, after, rates, later)
-    arrived, pre = lax.optimization_barrier((arrived, pre))
+    )(conv_input, grad_output, inject, readout, after, rates, later, halo, conv_weight)
+    arrived, act = lax.optimization_barrier((arrived, act))
 
     gi, gr = pl.pallas_call(
         local_shared_kernel,
@@ -578,17 +585,18 @@
 
     swap = [(i, i ^ 1) for i in range(nc)]
     swapped = lax.ppermute(shared(0), "c", swap)
-    chip = shared(1) + swapped
+    kept = shared(1)
     here = lax.axis_index("y")
     part = tokens // ny
 
     def turn(array, by):
         return lax.ppermute(array, "y", [(i, (i + by) % ny) for i in range(ny)])
 
-    def cut(array, which):
-        return lax.dynamic_slice_in_dim(array, lax.rem(here + which, ny) * part, part)
-
-    sent = [turn(cut(chip, by).astype(bf16), by) for by in range(1, ny)]
+    def cut(which):
+        at = lax.rem(here + which, ny) * part
+        return lax.dynamic_slice_in_dim(kept, at, part) + lax.dynamic_slice_in_dim(swapped, at, part)
+
+    sent = [turn(cut(by).astype(bf16), by) for by in range(1, ny)]
 
     grad_input, first = pl.pallas_call(
         input_kernel,
@@ -605,7 +613,7 @@
     )(returned, pre, factor, inject, conv_weight)
 
     *sent, first = lax.optimization_barrier((*sent, first))
-    quarter = cut(chip, 0)
+    quarter = cut(0)
     for piece in sent:
         quarter = quarter + piece.astype(f32)
     quarter = quarter.astype(bf16)

time: 104 us -> 104 us (level)
  waiting for transfers between devices: 11.8 us -> 9.5 us
  Pallas kernels: 47.7 us -> 48.8 us
    pallas_call x1, Pallas kernels: 7.23 us -> 9.47 us  [body(): pl.pallas_call(local_input_kernel, in_specs=[hbm] * 5 + [anywhere] * 3 +...]
    all_to_all x1, waiting for transfers between devices: 5.27 us -> 3.03 us  [body(): arrived = lax.all_to_all(payload, SEQ, 0, 0, tiled=True)]
    add x1 -> x0, other arithmetic: 1.39 us -> none  [body(): chip = shared(1) + swapped]
    convert_element_type x0 -> x1, other arithmetic: none -> 1.25 us  [body(): sent = [turn(cut(by).astype(bf16), by) for by in range(1, ny)]]
  transfers between devices with their start and end apart: 12 -> 12, of which waited for: 4 -> 4; matrix products, arithmetic and copies ran while one was open for 1% -> 1% of each run, Pallas kernels for 32% -> 34%
where the time goes in v6:
time: 104 us
  Pallas kernels  48.8 us (47%)
  starting transfers between devices  37.9 us (36%)
  waiting for transfers between devices  9.5 us (9%)
  other arithmetic  5.19 us (5%)
  local copies, waits for them, and re-layouts  1.49 us (1%)
    all_to_all x1, starting transfers between devices, body(): arrived = lax.all_to_all(payload, SEQ, 0, 0, tiled=True)  10.4 us
    pallas_call x1, Pallas kernels, body(): pl.pallas_call(local_shared_kernel, in_specs=[hbm] * 6 + [anywhere], out_...  9.77 us
    pallas_call x1, Pallas kernels, body(): pl.pallas_call(local_input_kernel, in_specs=[hbm] * 5 + [anywhere] * 3 +...  9.47 us
    pallas_call x2, Pallas kernels, shared(): pl.pallas_call(functools.partial(shared_kernel, turn), in_specs=[smem, pl...  9.23 us
    ppermute x6, starting transfers between devices, turn(): return lax.ppermute(array, 'y', [(i, (i + by) % ny) for i in range(ny)])  8.77 us
    pallas_call x1, Pallas kernels, body(): pl.pallas_call(states_kernel, in_specs=[hbm, anywhere, hbm, anywhere, hbm...  7.86 us
    all_to_all x1, starting transfers between devices, body(): returned = lax.all_to_all(scanned, SEQ, 0, 0, tiled=True)  6.28 us
    pallas_call x1, Pallas kernels, body(): pl.pallas_call(input_kernel, in_specs=[plain] + [hbm] * 3 + [plain], out_...  5.68 us
  transfers between devices with their start and end apart: 12, of which 4 were waited for; matrix products, arithmetic and copies ran while one was open for 1% of the time, Pallas kernels for 34%

profile of v6, /device:TPU:7, one launch (start us, length us, event | category | flops | bytes accessed | tf_op | source)
XLA Modules:
  0.0 103.7 jit_solution(11355399242286312833)
XLA Ops:
  0.6 0.7 slice.30
  1.4 3.4 %collective-permute-start = (bf16[16,512]{1,0:T(8,128)(2,1)S(1)}, bf16[16,512]{1,0:T(8,128)(2,1)S(1)}, u32[]{:S(2)}, u32[]{:S(2)}) collective-permute-start(bf16[16,512]{1,0:T(8,128)(2,1)S(1)} %slice.30), channel_id=1, source_target_pairs={{0,8},{8,16},{16,24},{24,32},{32,40},{40,48},{48,56},{56,64},{64,7... | collective-permute-start | bytes 49160 | tf_op jit(solution)/shard_map/ppermute | solution.py:491
  4.8 5.6 %own_grads.1 = (f32[8,512]{1,0:T(8,128)}, f32[8,512]{1,0:T(8,128)}, f32[8,512]{1,0:T(8,128)}, f32[1,512]{1,0:T(1,128)}, f32[128,512]{1,0:T(8,128)}, /*index=5*/f32[8,128,512]{2,1,0:T(8,128)}) custom-call(s32[8,8]{1,0:T(8,128)} %code_hbm.1, bf16[2048,512]{1,0:T(8,128)(2,1)} %grad_hbm.9, bf16[2048,128]{1,0:T(8,128)(2,1)} %read_hbm.5), custom_call_target="tpu_custom_call" | custom-call | flops 536870912 | bytes 3145728 | tf_op jit(solution)/shard_map/own_grads/pallas_call | solution.py:503
  10.4 0.6 copy-done.5
  11.0 7.9 %own_states.1 = (s16[32,16,384]{2,1,0:T(8,128)(2,1)}, f32[8,128,512]{2,1,0:T(8,128)}) custom-call(bf16[2048,512]{1,0:T(8,128)(2,1)} %x_hbm.3, bf16[16,512]{1,0:T(8,128)(2,1)} %copy-done.5, bf16[2048,128]{1,0:T(8,128)(2,1)} %inject_hbm.7, f32[8,512]{1,0:T(8,128)} %get-tuple-element.28.rate_hbm, bf16[4,512]{1,0:T(4,128)(2,1)} %weight_ref.1, ...), custom_call_target="tpu_custom_call" | custom-call | flops 536870912 | bytes 4194304 | tf_op jit(solution)/shard_map/own_states/pallas_call | solution.py:517
  18.9 10.4 %all-to-all-start = ((s16[32,16,384]{2,1,0:T(8,128)(2,1)}), s16[32,16,384]{2,1,0:T(8,128)(2,1)S(1)}, u32[]{:S(2)}, u32[]{:S(2)}) async-start(s16[32,16,384]{2,1,0:T(8,128)(2,1)} %get-tuple-element.31), calls=%async_computation | async-start | bytes 786432 | tf_op jit(solution)/shard_map/all_to_all | solution.py:532
  29.3 9.5 %local_input.1 = (bf16[2048,512]{1,0:T(8,128)(2,1)}, bf16[2048,512]{1,0:T(8,128)(2,1)}, bf16[2048,512]{1,0:T(8,128)(2,1)}) custom-call(bf16[2048,512]{1,0:T(8,128)(2,1)} %x_hbm.3, bf16[2048,512]{1,0:T(8,128)(2,1)} %grad_hbm.9, bf16[2048,128]{1,0:T(8,128)(2,1)} %inject_hbm.7, bf16[2048,128]{1,0:T(8,128)(2,1)} %read_hbm.5, ...), custom_call_target="tpu_custom_call" | custom-call | flops 2147483648 | bytes 13631488 | tf_op jit(solution)/shard_map/local_input/pallas_call | solution.py:534
  38.8 3.0 %all-to-all-done.own_ref = s16[32,16,384]{2,1,0:T(8,128)(2,1)S(1)} async-done(((s16[32,16,384]{2,1,0:T(8,128)(2,1)}), s16[32,16,384]{2,1,0:T(8,128)(2,1)S(1)}, u32[]{:S(2)}, u32[]{:S(2)}) %all-to-all-start) | async-done | bytes 393248 | tf_op jit(solution)/shard_map/all_to_all | solution.py:532
  41.8 1.2 %carry.1 = s16[32,16,384]{2,1,0:T(8,128)(2,1)} custom-call(s16[32,16,384]{2,1,0:T(8,128)(2,1)S(1)} %all-to-all-done.own_ref), custom_call_target="tpu_custom_call" | custom-call | flops 262144 | bytes 1048576 | tf_op jit(solution)/shard_map/carry/pallas_call | solution.py:560
  42.9 6.3 %all-to-all-start.1 = ((s16[32,16,384]{2,1,0:T(8,128)(2,1)}), s16[32,16,384]{2,1,0:T(8,128)(2,1)S(1)}, u32[]{:S(2)}, u32[]{:S(2)}) async-start(s16[32,16,384]{2,1,0:T(8,128)(2,1)} %carry.1), calls=%async_computation.1 | async-start | bytes 786432 | tf_op jit(solution)/shard_map/all_to_all | solution.py:568
  49.3 9.8 %local_shared.1 = (f32[2048,128]{1,0:T(8,128)}, f32[2048,128]{1,0:T(8,128)}) custom-call(bf16[2048,512]{1,0:T(8,128)(2,1)} %grad_hbm.9, bf16[2048,512]{1,0:T(8,128)(2,1)} %get-tuple-element.39.act_hbm, bf16[2048,128]{1,0:T(8,128)(2,1)} %inject_hbm.7, bf16[2048,128]{1,0:T(8,128)(2,1)} %read_hbm.5, f32[8,128,512]{2,1,0:T(8,128)} %get-tuple-element.32.after_hbm, ...), custom_call_target="tpu_custom_call" | custom-call | flops 3221225472 | bytes 9437184 | tf_op jit(solution)/shard_map/local_shared/pallas_call | solution.py:548
  59.0 2.2 %all-to-all-done.1.back_ref = s16[32,16,384]{2,1,0:T(8,128)(2,1)S(1)} async-done(((s16[32,16,384]{2,1,0:T(8,128)(2,1)}), s16[32,16,384]{2,1,0:T(8,128)(2,1)S(1)}, u32[]{:S(2)}, u32[]{:S(2)}) %all-to-all-start.1) | async-done | bytes 393248 | tf_op jit(solution)/shard_map/all_to_all | solution.py:568
  61.3 4.6 %shared_terms_0.1 = f32[2048,128]{1,0:T(8,128)} custom-call(s32[1]{0:T(128)} %bitcast.core_ref, s16[32,16,384]{2,1,0:T(8,128)(2,1)S(1)} %all-to-all-done.1.back_ref, bf16[2048,512]{1,0:T(8,128)(2,1)} %grad_hbm.9, bf16[2048,512]{1,0:T(8,128)(2,1)} %get-tuple-element.39.act_hbm, f32[2048,128]{1,0:T(8,128)} %get-tuple-element.41.gr_hbm, ...), custom_call_target="tpu_custom_call" | custom-call | flops 805306368 | bytes 4194304 | tf_op jit(solution)/shard_map/shared_terms_0/pallas_call | solution.py:574
  65.9 3.3 %collective-permute-start.1 = (f32[2048,128]{1,0:T(8,128)}, f32[2048,128]{1,0:T(8,128)S(1)}, u32[]{:S(2)}, u32[]{:S(2)}) collective-permute-start(f32[2048,128]{1,0:T(8,128)} %shared_terms_0.1), channel_id=1, source_target_pairs={{0,1},{1,0},{2,3},{3,2},{4,5},{5,4},{6,7},{7,6},{8,9},{9,8},{10,11... | collective-permute-start | bytes 3145736 | tf_op jit(solution)/shard_map/ppermute | solution.py:587
  69.2 4.6 %shared_terms_1.1 = f32[2048,128]{1,0:T(8,128)} custom-call(s32[1]{0:T(128)} %bitcast.core_ref, s16[32,16,384]{2,1,0:T(8,128)(2,1)S(1)} %all-to-all-done.1.back_ref, bf16[2048,512]{1,0:T(8,128)(2,1)} %grad_hbm.9, bf16[2048,512]{1,0:T(8,128)(2,1)} %get-tuple-element.39.act_hbm, f32[2048,128]{1,0:T(8,128)} %get-tuple-element.41.gr_hbm, ...), custom_call_target="tpu_custom_call" | custom-call | flops 805306368 | bytes 4194304 | tf_op jit(solution)/shard_map/shared_terms_1/pallas_call | solution.py:574
  73.8 0.0 copy-start
  73.9 1.3 %add_convert_fusion.1 = (bf16[512,128]{1,0:T(8,128)(2,1)S(1)}, bf16[512,128]{1,0:T(8,128)(2,1)S(1)}, bf16[512,128]{1,0:T(8,128)(2,1)S(1)}) fusion(f32[2048,128]{1,0:T(8,128)S(1)} %collective-permute-done.1, s32[]{:T(128)S(6)} %select_n.37, f32[2048,128]{1,0:T(8,128)} %shared_terms_1.1, s32[]{:T(128)S(6)} %select_n.36, s32[]{:T(128)S(6)} %select_n.35), kind=kLoop, calls=%fused_computation.3 | loop fusion | flops 393216 | bytes 1966092 | tf_op jit(solution)/shard_map/convert_element_type | solution.py:599
  75.1 1.4 %collective-permute-start.2 = (bf16[512,128]{1,0:T(8,128)(2,1)S(1)}, bf16[512,128]{1,0:T(8,128)(2,1)S(1)}, u32[]{:S(2)}, u32[]{:S(2)}) collective-permute-start(bf16[512,128]{1,0:T(8,128)(2,1)S(1)} %get-tuple-element.57), channel_id=1, source_target_pairs={{0,2},{2,4},{4,6},{6,0},{1,3},{3,5},{5,7},{7,1},{8,10},{10,12},{12... | collective-permute-start | bytes 393224 | tf_op jit(solution)/shard_map/ppermute | solution.py:593
  76.5 2.6 %collective-permute-start.3 = (bf16[512,128]{1,0:T(8,128)(2,1)S(1)}, bf16[512,128]{1,0:T(8,128)(2,1)S(1)}, u32[]{:S(2)}, u32[]{:S(2)}) collective-permute-start(bf16[512,128]{1,0:T(8,128)(2,1)S(1)} %get-tuple-element.56), channel_id=1, source_target_pairs={{0,4},{2,6},{4,0},{6,2},{1,5},{3,7},{5,1},{7,3},{8,12},{10,14},{12... | collective-permute-start | bytes 393224 | tf_op jit(solution)/shard_map/ppermute | solution.py:593
  79.1 1.1 %collective-permute-start.4 = (bf16[512,128]{1,0:T(8,128)(2,1)S(1)}, bf16[512,128]{1,0:T(8,128)(2,1)S(1)}, u32[]{:S(2)}, u32[]{:S(2)}) collective-permute-start(bf16[512,128]{1,0:T(8,128)(2,1)S(1)} %get-tuple-element.55), channel_id=1, source_target_pairs={{0,6},{2,0},{4,2},{6,4},{1,7},{3,1},{5,3},{7,5},{8,14},{10,8},{12,... | collective-permute-start | bytes 393224 | tf_op jit(solution)/shard_map/ppermute | solution.py:593
  80.2 5.7 %input_grads.1 = (f32[2048,512]{1,0:T(8,128)}, f32[8,512]{1,0:T(8,128)S(1)}) custom-call(s16[32,16,384]{2,1,0:T(8,128)(2,1)S(1)} %all-to-all-done.1.back_ref, bf16[2048,512]{1,0:T(8,128)(2,1)} %get-tuple-element.36.pre_hbm, bf16[2048,512]{1,0:T(8,128)(2,1)} %get-tuple-element.37.factor_hbm, bf16[2048,128]{1,0:T(8,128)(2,1)S(1)} %copy-done, ...), custom_call_target="tpu_custom_call" | custom-call | flops 536870912 | bytes 13631488 | tf_op jit(solution)/shard_map/input_grads/pallas_call | solution.py:601
  85.9 0.1 broadcast_in_dim.7
  86.0 1.1 %constant_dynamic-update-slice_fusion.3 = (bf16[2048,128]{1,0:T(8,128)(2,1)S(1)}, bf16[512,128]{1,0:T(8,128)(2,1)S(1)}) fusion(bf16[2048,128]{1,0:T(8,128)(2,1)S(1)} %broadcast_in_dim.7, s32[]{:T(128)S(6)} %select_n.39, bf16[512,128]{1,0:T(8,128)(2,1)S(1)} %collective-permute-done.4, bf16[512,128]{1,0:T(8,128)(2,1)S(1)} %collective-permute-done.3, ...), kind=kLoop, calls=%fused_computation.11 | loop fusion | flops 524288 | bytes 1179656 | tf_op jit(solution)/shard_map/dynamic_update_slice | solution.py:625
  87.0 0.5 collective-permute-start.5
  87.5 2.3 %collective-permute-start.6 = (bf16[512,128]{1,0:T(8,128)(2,1)S(1)}, bf16[512,128]{1,0:T(8,128)(2,1)S(1)}, u32[]{:S(2)}, u32[]{:S(2)}) collective-permute-start(bf16[512,128]{1,0:T(8,128)(2,1)S(1)} %get-tuple-element.54), channel_id=1, source_target_pairs={{0,4},{2,6},{4,0},{6,2},{1,5},{3,7},{5,1},{7,3},{8,12},{10,14},{12... | collective-permute-start | bytes 393224 | tf_op jit(solution)/shard_map/ppermute | solution.py:593
  89.8 0.9 collective-permute-start.7
  90.7 2.5 %collective-permute-start.8 = (f32[8,512]{1,0:T(8,128)S(1)}, f32[8,512]{1,0:T(8,128)S(1)}, u32[]{:S(2)}, u32[]{:S(2)}) collective-permute-start(f32[8,512]{1,0:T(8,128)S(1)} %get-tuple-element.48), channel_id=1, source_target_pairs={{8,0},{16,8},{24,16},{32,24},{40,32},{48,40},{56,48},{64,56},{72,6... | collective-permute-start | bytes 49160 | tf_op jit(solution)/shard_map/ppermute | solution.py:621
  93.2 4.1 %collective-permute-done.8 = f32[8,512]{1,0:T(8,128)S(1)} collective-permute-done((f32[8,512]{1,0:T(8,128)S(1)}, f32[8,512]{1,0:T(8,128)S(1)}, u32[]{:S(2)}, u32[]{:S(2)}) %collective-permute-start.8) | collective-permute-done | bytes 16416 | tf_op jit(solution)/shard_map/ppermute | solution.py:621
  97.4 3.3 %collective-permute-start.9 = (bf16[2048,128]{1,0:T(8,128)(2,1)S(1)}, bf16[2048,128]{1,0:T(8,128)(2,1)S(1)}, u32[]{:S(2)}, u32[]{:S(2)}) collective-permute-start(bf16[2048,128]{1,0:T(8,128)(2,1)S(1)} %constant_dynamic-update-slice_fusion), channel_id=1, source_target_pairs={{0,1},{1,0},{2,3},{3,2},{4,5},{5,4},{6,7},{7,6},{8,9},{9,8},{10,11... | collective-permute-start | bytes 1572872 | tf_op jit(solution)/shard_map/ppermute | solution.py:628
  100.7 1.4 %fusion = f32[2048,512]{1,0:T(8,128)} fusion(f32[2048,512]{1,0:T(8,128)} %get-tuple-element.38, f32[1,512]{1,0:T(1,128)S(1)} %get-tuple-element.61, f32[1,512]{1,0:T(1,128)S(1)} %get-tuple-element.62, f32[1,512]{1,0:T(1,128)S(1)} %get-tuple-element.60, f32[8]{0:T(128)S(1)} %pad.clone), kind=kLoop, calls=%fused_computation.7 | loop fusion | flops 16384 | bytes 38944 | tf_op jit(solution)/shard_map/dynamic_update_slice | solution.py:639
  102.1 0.1 collective-permute-done.9
  102.2 1.5 %select_convert_fusion = (f32[2048,128]{1,0:T(8,128)}, f32[2048,128]{1,0:T(8,128)}) fusion(bf16[2048,128]{1,0:T(8,128)(2,1)S(1)} %collective-permute-done.9, bf16[2048,128]{1,0:T(8,128)(2,1)S(1)} %constant_dynamic-update-slice_fusion, pred[]{:T(512)S(6)} %eq.3), kind=kLoop, calls=%fused_computation | loop fusion | flops 1048576 | bytes 3145729 | tf_op jit(solution)/shard_map/convert_element_type | solution.py:631
  (25 shorter events, 0.1 us)
Async XLA Ops:
  1.4 9.1 %collective-permute-start = (bf16[16,512]{1,0:T(8,128)(2,1)S(1)}, bf16[16,512]{1,0:T(8,128)(2,1)S(1)}, u32[]{:S(2)}, u32[]{:S(2)}) collective-permute-start(bf16[16,512]{1,0:T(8,128)(2,1)S(1)} %slice.30), channel_id=1, source_target_pairs={{0,8},{8,16},{16,24},{24,32},{32,40},{40,48},{48,56},{56,64},{64,7... | collective-permute-start | bytes 49160 | tf_op jit(solution)/shard_map/ppermute | solution.py:491
  10.4 0.6 copy-start.5
  18.9 22.9 %all-to-all-start = ((s16[32,16,384]{2,1,0:T(8,128)(2,1)}), s16[32,16,384]{2,1,0:T(8,128)(2,1)S(1)}, u32[]{:S(2)}, u32[]{:S(2)}) async-start(s16[32,16,384]{2,1,0:T(8,128)(2,1)} %get-tuple-element.31), calls=%async_computation | async-start | bytes 786432 | tf_op jit(solution)/shard_map/all_to_all | solution.py:532
  42.9 18.3 %all-to-all-start.1 = ((s16[32,16,384]{2,1,0:T(8,128)(2,1)}), s16[32,16,384]{2,1,0:T(8,128)(2,1)S(1)}, u32[]{:S(2)}, u32[]{:S(2)}) async-start(s16[32,16,384]{2,1,0:T(8,128)(2,1)} %carry.1), calls=%async_computation.1 | async-start | bytes 786432 | tf_op jit(solution)/shard_map/all_to_all | solution.py:568
  49.2 12.1 %copy-start.1 = (f32[8,512]{1,0:T(8,128)S(1)}, f32[8,512]{1,0:T(8,128)}, u32[]{:S(2)}) copy-start(f32[8,512]{1,0:T(8,128)} %get-tuple-element.28.rate_hbm) | copy-start | bytes 49156
  49.2 12.0 %copy-start.2 = (f32[8,512]{1,0:T(8,128)S(1)}, f32[8,512]{1,0:T(8,128)}, u32[]{:S(2)}) copy-start(f32[8,512]{1,0:T(8,128)} %get-tuple-element.43.prior_hbm) | copy-start | bytes 49156
  49.3 12.0 %copy-start.3 = (f32[8,512]{1,0:T(8,128)S(1)}, f32[8,512]{1,0:T(8,128)}, u32[]{:S(2)}) copy-start(f32[8,512]{1,0:T(8,128)} %get-tuple-element.33.later_hbm) | copy-start | bytes 49156
  65.9 7.9 %collective-permute-start.1 = (f32[2048,128]{1,0:T(8,128)}, f32[2048,128]{1,0:T(8,128)S(1)}, u32[]{:S(2)}, u32[]{:S(2)}) collective-permute-start(f32[2048,128]{1,0:T(8,128)} %shared_terms_0.1), channel_id=1, source_target_pairs={{0,1},{1,0},{2,3},{3,2},{4,5},{5,4},{6,7},{7,6},{8,9},{9,8},{10,11... | collective-permute-start | bytes 3145736 | tf_op jit(solution)/shard_map/ppermute | solution.py:587
  69.2 10.9 %copy-start.4 = (bf16[4,512]{1,0:T(4,128)(2,1)S(1)}, bf16[4,512]{1,0:T(4,128)(2,1)}, u32[]{:S(2)}) copy-start(bf16[4,512]{1,0:T(4,128)(2,1)} %weight_ref.1) | copy-start | bytes 12292
  73.8 6.3 %copy-start = (bf16[2048,128]{1,0:T(8,128)(2,1)S(1)}, bf16[2048,128]{1,0:T(8,128)(2,1)}, u32[]{:S(2)}) copy-start(bf16[2048,128]{1,0:T(8,128)(2,1)} %inject_hbm.7) | copy-start | bytes 1572868
  75.1 10.7 %collective-permute-start.2 = (bf16[512,128]{1,0:T(8,128)(2,1)S(1)}, bf16[512,128]{1,0:T(8,128)(2,1)S(1)}, u32[]{:S(2)}, u32[]{:S(2)}) collective-permute-start(bf16[512,128]{1,0:T(8,128)(2,1)S(1)} %get-tuple-element.57), channel_id=1, source_target_pairs={{0,2},{2,4},{4,6},{6,0},{1,3},{3,5},{5,7},{7,1},{8,10},{10,12},{12... | collective-permute-start | bytes 393224 | tf_op jit(solution)/shard_map/ppermute | solution.py:593
  76.5 9.4 %collective-permute-start.3 = (bf16[512,128]{1,0:T(8,128)(2,1)S(1)}, bf16[512,128]{1,0:T(8,128)(2,1)S(1)}, u32[]{:S(2)}, u32[]{:S(2)}) collective-permute-start(bf16[512,128]{1,0:T(8,128)(2,1)S(1)} %get-tuple-element.56), channel_id=1, source_target_pairs={{0,4},{2,6},{4,0},{6,2},{1,5},{3,7},{5,1},{7,3},{8,12},{10,14},{12... | collective-permute-start | bytes 393224 | tf_op jit(solution)/shard_map/ppermute | solution.py:593
  79.1 6.8 %collective-permute-start.4 = (bf16[512,128]{1,0:T(8,128)(2,1)S(1)}, bf16[512,128]{1,0:T(8,128)(2,1)S(1)}, u32[]{:S(2)}, u32[]{:S(2)}) collective-permute-start(bf16[512,128]{1,0:T(8,128)(2,1)S(1)} %get-tuple-element.55), channel_id=1, source_target_pairs={{0,6},{2,0},{4,2},{6,4},{1,7},{3,1},{5,3},{7,5},{8,14},{10,8},{12,... | collective-permute-start | bytes 393224 | tf_op jit(solution)/shard_map/ppermute | solution.py:593
  87.0 10.3 %collective-permute-start.5 = (bf16[512,128]{1,0:T(8,128)(2,1)S(1)}, bf16[512,128]{1,0:T(8,128)(2,1)S(1)}, u32[]{:S(2)}, u32[]{:S(2)}) collective-permute-start(bf16[512,128]{1,0:T(8,128)(2,1)S(1)} %get-tuple-element.54), channel_id=1, source_target_pairs={{0,2},{2,4},{4,6},{6,0},{1,3},{3,5},{5,7},{7,1},{8,10},{10,12},{12... | collective-permute-start | bytes 393224 | tf_op jit(solution)/shard_map/ppermute | solution.py:593
  87.5 9.8 %collective-permute-start.6 = (bf16[512,128]{1,0:T(8,128)(2,1)S(1)}, bf16[512,128]{1,0:T(8,128)(2,1)S(1)}, u32[]{:S(2)}, u32[]{:S(2)}) collective-permute-start(bf16[512,128]{1,0:T(8,128)(2,1)S(1)} %get-tuple-element.54), channel_id=1, source_target_pairs={{0,4},{2,6},{4,0},{6,2},{1,5},{3,7},{5,1},{7,3},{8,12},{10,14},{12... | collective-permute-start | bytes 393224 | tf_op jit(solution)/shard_map/ppermute | solution.py:593
  89.8 7.5 %collective-permute-start.7 = (bf16[512,128]{1,0:T(8,128)(2,1)S(1)}, bf16[512,128]{1,0:T(8,128)(2,1)S(1)}, u32[]{:S(2)}, u32[]{:S(2)}) collective-permute-start(bf16[512,128]{1,0:T(8,128)(2,1)S(1)} %get-tuple-element.54), channel_id=1, source_target_pairs={{0,6},{2,0},{4,2},{6,4},{1,7},{3,1},{5,3},{7,5},{8,14},{10,8},{12,... | collective-permute-start | bytes 393224 | tf_op jit(solution)/shard_map/ppermute | solution.py:593
  90.7 6.6 %collective-permute-start.8 = (f32[8,512]{1,0:T(8,128)S(1)}, f32[8,512]{1,0:T(8,128)S(1)}, u32[]{:S(2)}, u32[]{:S(2)}) collective-permute-start(f32[8,512]{1,0:T(8,128)S(1)} %get-tuple-element.48), channel_id=1, source_target_pairs={{8,0},{16,8},{24,16},{32,24},{40,32},{48,40},{56,48},{64,56},{72,6... | collective-permute-start | bytes 49160 | tf_op jit(solution)/shard_map/ppermute | solution.py:621
  97.4 4.8 %collective-permute-start.9 = (bf16[2048,128]{1,0:T(8,128)(2,1)S(1)}, bf16[2048,128]{1,0:T(8,128)(2,1)S(1)}, u32[]{:S(2)}, u32[]{:S(2)}) collective-permute-start(bf16[2048,128]{1,0:T(8,128)(2,1)S(1)} %constant_dynamic-update-slice_fusion), channel_id=1, source_target_pairs={{0,1},{1,0},{2,3},{3,2},{4,5},{5,4},{6,7},{7,6},{8,9},{9,8},{10,11... | collective-permute-start | bytes 1572872 | tf_op jit(solution)/shard_map/ppermute | solution.py:628

commit v7 on v6

--- a/solution.py
+++ b/solution.py
@@ -48,7 +48,7 @@
 AHEAD = 3
 
 
-def each_span(spans, step, start, pieces, backwards=False, ahead=AHEAD):
+def each_span(spans, step, start, pieces, backwards=False, ahead=AHEAD, unroll=1):
     def visit(i, _):
         span = spans - 1 - i if backwards else i
         for piece in pieces:
@@ -61,7 +61,7 @@
         step(span)
         return 0
 
-    lax.fori_loop(0, spans, visit, 0)
+    lax.fori_loop(0, spans, visit, 0, unroll=unroll)
 
 
 def starting(pieces):
@@ -215,7 +215,7 @@
         fresh = dot2(inject_ref[span_at(span), :], act.astype(f32) * tail, TN)
         carry[...] = jnp.exp(SPAN * rate) * before + fresh
 
-    each_span(spans, step, start, pieces)
+    each_span(spans, step, start, pieces, unroll=True)
     late.wait()
     chunks, height, _ = pay_ref.shape
     state_codes, state_power = coded(carry[...], 0)
@@ -356,7 +356,7 @@
         for out in outs:
             out(span).start()
 
-    each_span(spans, step, start, pieces)
+    each_span(spans, step, start, pieces, unroll=True)
     drain(spans, outs)
 
 

time: 104 us -> 104 us (level)
  no operation moved by 1% of the time
where the time goes in v7:
time: 104 us; the launch traced here: 103 us
  Pallas kernels  48.1 us (46%)
  starting transfers between devices  37.9 us (36%)
  waiting for transfers between devices  9.67 us (9%)
  other arithmetic  5.19 us (5%)
  local copies, waits for them, and re-layouts  1.49 us (1%)
    all_to_all x1, starting transfers between devices, body(): arrived = lax.all_to_all(payload, SEQ, 0, 0, tiled=True)  10.4 us
    pallas_call x1, Pallas kernels, body(): pl.pallas_call(local_shared_kernel, in_specs=[hbm] * 6 + [anywhere], out_...  9.61 us
    pallas_call x1, Pallas kernels, body(): pl.pallas_call(local_input_kernel, in_specs=[hbm] * 5 + [anywhere] * 3 +...  9.47 us
    pallas_call x2, Pallas kernels, shared(): pl.pallas_call(functools.partial(shared_kernel, turn), in_specs=[smem, pl...  9.23 us
    ppermute x6, starting transfers between devices, turn(): return lax.ppermute(array, 'y', [(i, (i + by) % ny) for i in range(ny)])  8.79 us
    pallas_call x1, Pallas kernels, body(): pl.pallas_call(states_kernel, in_specs=[hbm, anywhere, hbm, anywhere, hbm...  7.38 us
    all_to_all x1, starting transfers between devices, body(): returned = lax.all_to_all(scanned, SEQ, 0, 0, tiled=True)  6.27 us
    pallas_call x1, Pallas kernels, body(): pl.pallas_call(input_kernel, in_specs=[plain] + [hbm] * 3 + [plain], out_...  5.68 us
  transfers between devices with their start and end apart: 12, of which 4 were waited for; matrix products, arithmetic and copies ran while one was open for 1% of the time, Pallas kernels for 34%

profile of v7, /device:TPU:7, one launch (start us, length us, event | category | flops | bytes accessed | tf_op | source)
XLA Modules:
  0.0 103.2 jit_solution(1603540714681681933)
XLA Ops:
  0.6 0.7 slice.30
  1.4 3.4 %collective-permute-start = (bf16[16,512]{1,0:T(8,128)(2,1)S(1)}, bf16[16,512]{1,0:T(8,128)(2,1)S(1)}, u32[]{:S(2)}, u32[]{:S(2)}) collective-permute-start(bf16[16,512]{1,0:T(8,128)(2,1)S(1)} %slice.30), channel_id=1, source_target_pairs={{0,8},{8,16},{16,24},{24,32},{32,40},{40,48},{48,56},{56,64},{64,7... | collective-permute-start | bytes 49160 | tf_op jit(solution)/shard_map/ppermute | solution.py:491
  4.8 5.6 %own_grads.1 = (f32[8,512]{1,0:T(8,128)}, f32[8,512]{1,0:T(8,128)}, f32[8,512]{1,0:T(8,128)}, f32[1,512]{1,0:T(1,128)}, f32[128,512]{1,0:T(8,128)}, /*index=5*/f32[8,128,512]{2,1,0:T(8,128)}) custom-call(s32[8,8]{1,0:T(8,128)} %code_hbm.1, bf16[2048,512]{1,0:T(8,128)(2,1)} %grad_hbm.9, bf16[2048,128]{1,0:T(8,128)(2,1)} %read_hbm.5), custom_call_target="tpu_custom_call" | custom-call | flops 536870912 | bytes 3145728 | tf_op jit(solution)/shard_map/own_grads/pallas_call | solution.py:503
  10.4 0.6 copy-done.5
  11.0 7.4 %own_states.1 = (s16[32,16,384]{2,1,0:T(8,128)(2,1)}, f32[8,128,512]{2,1,0:T(8,128)}) custom-call(bf16[2048,512]{1,0:T(8,128)(2,1)} %x_hbm.3, bf16[16,512]{1,0:T(8,128)(2,1)} %copy-done.5, bf16[2048,128]{1,0:T(8,128)(2,1)} %inject_hbm.7, f32[8,512]{1,0:T(8,128)} %get-tuple-element.28.rate_hbm, bf16[4,512]{1,0:T(4,128)(2,1)} %weight_ref.1, ...), custom_call_target="tpu_custom_call" | custom-call | flops 536870912 | bytes 4194304 | tf_op jit(solution)/shard_map/own_states/pallas_call | solution.py:517
  18.4 10.4 %all-to-all-start = ((s16[32,16,384]{2,1,0:T(8,128)(2,1)}), s16[32,16,384]{2,1,0:T(8,128)(2,1)S(1)}, u32[]{:S(2)}, u32[]{:S(2)}) async-start(s16[32,16,384]{2,1,0:T(8,128)(2,1)} %get-tuple-element.31), calls=%async_computation | async-start | bytes 786432 | tf_op jit(solution)/shard_map/all_to_all | solution.py:532
  28.8 9.5 %local_input.1 = (bf16[2048,512]{1,0:T(8,128)(2,1)}, bf16[2048,512]{1,0:T(8,128)(2,1)}, bf16[2048,512]{1,0:T(8,128)(2,1)}) custom-call(bf16[2048,512]{1,0:T(8,128)(2,1)} %x_hbm.3, bf16[2048,512]{1,0:T(8,128)(2,1)} %grad_hbm.9, bf16[2048,128]{1,0:T(8,128)(2,1)} %inject_hbm.7, bf16[2048,128]{1,0:T(8,128)(2,1)} %read_hbm.5, ...), custom_call_target="tpu_custom_call" | custom-call | flops 2147483648 | bytes 13631488 | tf_op jit(solution)/shard_map/local_input/pallas_call | solution.py:534
  38.3 3.0 %all-to-all-done.own_ref = s16[32,16,384]{2,1,0:T(8,128)(2,1)S(1)} async-done(((s16[32,16,384]{2,1,0:T(8,128)(2,1)}), s16[32,16,384]{2,1,0:T(8,128)(2,1)S(1)}, u32[]{:S(2)}, u32[]{:S(2)}) %all-to-all-start) | async-done | bytes 393248 | tf_op jit(solution)/shard_map/all_to_all | solution.py:532
  41.3 1.2 %carry.1 = s16[32,16,384]{2,1,0:T(8,128)(2,1)} custom-call(s16[32,16,384]{2,1,0:T(8,128)(2,1)S(1)} %all-to-all-done.own_ref), custom_call_target="tpu_custom_call" | custom-call | flops 262144 | bytes 1048576 | tf_op jit(solution)/shard_map/carry/pallas_call | solution.py:560
  42.5 6.3 %all-to-all-start.1 = ((s16[32,16,384]{2,1,0:T(8,128)(2,1)}), s16[32,16,384]{2,1,0:T(8,128)(2,1)S(1)}, u32[]{:S(2)}, u32[]{:S(2)}) async-start(s16[32,16,384]{2,1,0:T(8,128)(2,1)} %carry.1), calls=%async_computation.1 | async-start | bytes 786432 | tf_op jit(solution)/shard_map/all_to_all | solution.py:568
  48.8 9.6 %local_shared.1 = (f32[2048,128]{1,0:T(8,128)}, f32[2048,128]{1,0:T(8,128)}) custom-call(bf16[2048,512]{1,0:T(8,128)(2,1)} %grad_hbm.9, bf16[2048,512]{1,0:T(8,128)(2,1)} %get-tuple-element.39.act_hbm, bf16[2048,128]{1,0:T(8,128)(2,1)} %inject_hbm.7, bf16[2048,128]{1,0:T(8,128)(2,1)} %read_hbm.5, f32[8,128,512]{2,1,0:T(8,128)} %get-tuple-element.32.after_hbm, ...), custom_call_target="tpu_custom_call" | custom-call | flops 3221225472 | bytes 9437184 | tf_op jit(solution)/shard_map/local_shared/pallas_call | solution.py:548
  58.4 2.4 %all-to-all-done.1.back_ref = s16[32,16,384]{2,1,0:T(8,128)(2,1)S(1)} async-done(((s16[32,16,384]{2,1,0:T(8,128)(2,1)}), s16[32,16,384]{2,1,0:T(8,128)(2,1)S(1)}, u32[]{:S(2)}, u32[]{:S(2)}) %all-to-all-start.1) | async-done | bytes 393248 | tf_op jit(solution)/shard_map/all_to_all | solution.py:568
  60.8 4.6 %shared_terms_0.1 = f32[2048,128]{1,0:T(8,128)} custom-call(s32[1]{0:T(128)} %bitcast.core_ref, s16[32,16,384]{2,1,0:T(8,128)(2,1)S(1)} %all-to-all-done.1.back_ref, bf16[2048,512]{1,0:T(8,128)(2,1)} %grad_hbm.9, bf16[2048,512]{1,0:T(8,128)(2,1)} %get-tuple-element.39.act_hbm, f32[2048,128]{1,0:T(8,128)} %get-tuple-element.41.gr_hbm, ...), custom_call_target="tpu_custom_call" | custom-call | flops 805306368 | bytes 4194304 | tf_op jit(solution)/shard_map/shared_terms_0/pallas_call | solution.py:574
  65.5 3.3 %collective-permute-start.1 = (f32[2048,128]{1,0:T(8,128)}, f32[2048,128]{1,0:T(8,128)S(1)}, u32[]{:S(2)}, u32[]{:S(2)}) collective-permute-start(f32[2048,128]{1,0:T(8,128)} %shared_terms_0.1), channel_id=1, source_target_pairs={{0,1},{1,0},{2,3},{3,2},{4,5},{5,4},{6,7},{7,6},{8,9},{9,8},{10,11... | collective-permute-start | bytes 3145736 | tf_op jit(solution)/shard_map/ppermute | solution.py:587
  68.8 4.6 %shared_terms_1.1 = f32[2048,128]{1,0:T(8,128)} custom-call(s32[1]{0:T(128)} %bitcast.core_ref, s16[32,16,384]{2,1,0:T(8,128)(2,1)S(1)} %all-to-all-done.1.back_ref, bf16[2048,512]{1,0:T(8,128)(2,1)} %grad_hbm.9, bf16[2048,512]{1,0:T(8,128)(2,1)} %get-tuple-element.39.act_hbm, f32[2048,128]{1,0:T(8,128)} %get-tuple-element.41.gr_hbm, ...), custom_call_target="tpu_custom_call" | custom-call | flops 805306368 | bytes 4194304 | tf_op jit(solution)/shard_map/shared_terms_1/pallas_call | solution.py:574
  73.4 0.0 copy-start
  73.4 1.3 %add_convert_fusion.1 = (bf16[512,128]{1,0:T(8,128)(2,1)S(1)}, bf16[512,128]{1,0:T(8,128)(2,1)S(1)}, bf16[512,128]{1,0:T(8,128)(2,1)S(1)}) fusion(f32[2048,128]{1,0:T(8,128)S(1)} %collective-permute-done.1, s32[]{:T(128)S(6)} %select_n.37, f32[2048,128]{1,0:T(8,128)} %shared_terms_1.1, s32[]{:T(128)S(6)} %select_n.36, s32[]{:T(128)S(6)} %select_n.35), kind=kLoop, calls=%fused_computation.3 | loop fusion | flops 393216 | bytes 1966092 | tf_op jit(solution)/shard_map/convert_element_type | solution.py:599
  74.6 1.4 %collective-permute-start.2 = (bf16[512,128]{1,0:T(8,128)(2,1)S(1)}, bf16[512,128]{1,0:T(8,128)(2,1)S(1)}, u32[]{:S(2)}, u32[]{:S(2)}) collective-permute-start(bf16[512,128]{1,0:T(8,128)(2,1)S(1)} %get-tuple-element.57), channel_id=1, source_target_pairs={{0,2},{2,4},{4,6},{6,0},{1,3},{3,5},{5,7},{7,1},{8,10},{10,12},{12... | collective-permute-start | bytes 393224 | tf_op jit(solution)/shard_map/ppermute | solution.py:593
  76.0 2.6 %collective-permute-start.3 = (bf16[512,128]{1,0:T(8,128)(2,1)S(1)}, bf16[512,128]{1,0:T(8,128)(2,1)S(1)}, u32[]{:S(2)}, u32[]{:S(2)}) collective-permute-start(bf16[512,128]{1,0:T(8,128)(2,1)S(1)} %get-tuple-element.56), channel_id=1, source_target_pairs={{0,4},{2,6},{4,0},{6,2},{1,5},{3,7},{5,1},{7,3},{8,12},{10,14},{12... | collective-permute-start | bytes 393224 | tf_op jit(solution)/shard_map/ppermute | solution.py:593
  78.6 1.1 %collective-permute-start.4 = (bf16[512,128]{1,0:T(8,128)(2,1)S(1)}, bf16[512,128]{1,0:T(8,128)(2,1)S(1)}, u32[]{:S(2)}, u32[]{:S(2)}) collective-permute-start(bf16[512,128]{1,0:T(8,128)(2,1)S(1)} %get-tuple-element.55), channel_id=1, source_target_pairs={{0,6},{2,0},{4,2},{6,4},{1,7},{3,1},{5,3},{7,5},{8,14},{10,8},{12,... | collective-permute-start | bytes 393224 | tf_op jit(solution)/shard_map/ppermute | solution.py:593
  79.7 5.7 %input_grads.1 = (f32[2048,512]{1,0:T(8,128)}, f32[8,512]{1,0:T(8,128)S(1)}) custom-call(s16[32,16,384]{2,1,0:T(8,128)(2,1)S(1)} %all-to-all-done.1.back_ref, bf16[2048,512]{1,0:T(8,128)(2,1)} %get-tuple-element.36.pre_hbm, bf16[2048,512]{1,0:T(8,128)(2,1)} %get-tuple-element.37.factor_hbm, bf16[2048,128]{1,0:T(8,128)(2,1)S(1)} %copy-done, ...), custom_call_target="tpu_custom_call" | custom-call | flops 536870912 | bytes 13631488 | tf_op jit(solution)/shard_map/input_grads/pallas_call | solution.py:601
  85.4 0.1 broadcast_in_dim.7
  85.5 1.1 %constant_dynamic-update-slice_fusion.3 = (bf16[2048,128]{1,0:T(8,128)(2,1)S(1)}, bf16[512,128]{1,0:T(8,128)(2,1)S(1)}) fusion(bf16[2048,128]{1,0:T(8,128)(2,1)S(1)} %broadcast_in_dim.7, s32[]{:T(128)S(6)} %select_n.39, bf16[512,128]{1,0:T(8,128)(2,1)S(1)} %collective-permute-done.4, bf16[512,128]{1,0:T(8,128)(2,1)S(1)} %collective-permute-done.3, ...), kind=kLoop, calls=%fused_computation.11 | loop fusion | flops 524288 | bytes 1179656 | tf_op jit(solution)/shard_map/dynamic_update_slice | solution.py:625
  86.6 0.5 collective-permute-start.5
  87.0 2.3 %collective-permute-start.6 = (bf16[512,128]{1,0:T(8,128)(2,1)S(1)}, bf16[512,128]{1,0:T(8,128)(2,1)S(1)}, u32[]{:S(2)}, u32[]{:S(2)}) collective-permute-start(bf16[512,128]{1,0:T(8,128)(2,1)S(1)} %get-tuple-element.54), channel_id=1, source_target_pairs={{0,4},{2,6},{4,0},{6,2},{1,5},{3,7},{5,1},{7,3},{8,12},{10,14},{12... | collective-permute-start | bytes 393224 | tf_op jit(solution)/shard_map/ppermute | solution.py:593
  89.4 0.9 collective-permute-start.7
  90.3 2.5 %collective-permute-start.8 = (f32[8,512]{1,0:T(8,128)S(1)}, f32[8,512]{1,0:T(8,128)S(1)}, u32[]{:S(2)}, u32[]{:S(2)}) collective-permute-start(f32[8,512]{1,0:T(8,128)S(1)} %get-tuple-element.48), channel_id=1, source_target_pairs={{8,0},{16,8},{24,16},{32,24},{40,32},{48,40},{56,48},{64,56},{72,6... | collective-permute-start | bytes 49160 | tf_op jit(solution)/shard_map/ppermute | solution.py:621
  92.8 4.1 %collective-permute-done.8 = f32[8,512]{1,0:T(8,128)S(1)} collective-permute-done((f32[8,512]{1,0:T(8,128)S(1)}, f32[8,512]{1,0:T(8,128)S(1)}, u32[]{:S(2)}, u32[]{:S(2)}) %collective-permute-start.8) | collective-permute-done | bytes 16416 | tf_op jit(solution)/shard_map/ppermute | solution.py:621
  97.0 3.2 %collective-permute-start.9 = (bf16[2048,128]{1,0:T(8,128)(2,1)S(1)}, bf16[2048,128]{1,0:T(8,128)(2,1)S(1)}, u32[]{:S(2)}, u32[]{:S(2)}) collective-permute-start(bf16[2048,128]{1,0:T(8,128)(2,1)S(1)} %constant_dynamic-update-slice_fusion), channel_id=1, source_target_pairs={{0,1},{1,0},{2,3},{3,2},{4,5},{5,4},{6,7},{7,6},{8,9},{9,8},{10,11... | collective-permute-start | bytes 1572872 | tf_op jit(solution)/shard_map/ppermute | solution.py:628
  100.3 1.4 %fusion = f32[2048,512]{1,0:T(8,128)} fusion(f32[2048,512]{1,0:T(8,128)} %get-tuple-element.38, f32[1,512]{1,0:T(1,128)S(1)} %get-tuple-element.61, f32[1,512]{1,0:T(1,128)S(1)} %get-tuple-element.62, f32[1,512]{1,0:T(1,128)S(1)} %get-tuple-element.60, f32[8]{0:T(128)S(1)} %pad.clone), kind=kLoop, calls=%fused_computation.7 | loop fusion | flops 16384 | bytes 38944 | tf_op jit(solution)/shard_map/dynamic_update_slice | solution.py:639
  101.7 0.1 collective-permute-done.9
  101.8 1.5 %select_convert_fusion = (f32[2048,128]{1,0:T(8,128)}, f32[2048,128]{1,0:T(8,128)}) fusion(bf16[2048,128]{1,0:T(8,128)(2,1)S(1)} %collective-permute-done.9, bf16[2048,128]{1,0:T(8,128)(2,1)S(1)} %constant_dynamic-update-slice_fusion, pred[]{:T(512)S(6)} %eq.3), kind=kLoop, calls=%fused_computation | loop fusion | flops 1048576 | bytes 3145729 | tf_op jit(solution)/shard_map/convert_element_type | solution.py:631
  (25 shorter events, 0.1 us)
Async XLA Ops:
  1.4 9.1 %collective-permute-start = (bf16[16,512]{1,0:T(8,128)(2,1)S(1)}, bf16[16,512]{1,0:T(8,128)(2,1)S(1)}, u32[]{:S(2)}, u32[]{:S(2)}) collective-permute-start(bf16[16,512]{1,0:T(8,128)(2,1)S(1)} %slice.30), channel_id=1, source_target_pairs={{0,8},{8,16},{16,24},{24,32},{32,40},{40,48},{48,56},{56,64},{64,7... | collective-permute-start | bytes 49160 | tf_op jit(solution)/shard_map/ppermute | solution.py:491
  10.4 0.6 copy-start.5
  18.4 22.9 %all-to-all-start = ((s16[32,16,384]{2,1,0:T(8,128)(2,1)}), s16[32,16,384]{2,1,0:T(8,128)(2,1)S(1)}, u32[]{:S(2)}, u32[]{:S(2)}) async-start(s16[32,16,384]{2,1,0:T(8,128)(2,1)} %get-tuple-element.31), calls=%async_computation | async-start | bytes 786432 | tf_op jit(solution)/shard_map/all_to_all | solution.py:532
  42.5 18.3 %all-to-all-start.1 = ((s16[32,16,384]{2,1,0:T(8,128)(2,1)}), s16[32,16,384]{2,1,0:T(8,128)(2,1)S(1)}, u32[]{:S(2)}, u32[]{:S(2)}) async-start(s16[32,16,384]{2,1,0:T(8,128)(2,1)} %carry.1), calls=%async_computation.1 | async-start | bytes 786432 | tf_op jit(solution)/shard_map/all_to_all | solution.py:568
  48.8 12.0 %copy-start.1 = (f32[8,512]{1,0:T(8,128)S(1)}, f32[8,512]{1,0:T(8,128)}, u32[]{:S(2)}) copy-start(f32[8,512]{1,0:T(8,128)} %get-tuple-element.28.rate_hbm) | copy-start | bytes 49156
  48.8 12.0 %copy-start.2 = (f32[8,512]{1,0:T(8,128)S(1)}, f32[8,512]{1,0:T(8,128)}, u32[]{:S(2)}) copy-start(f32[8,512]{1,0:T(8,128)} %get-tuple-element.43.prior_hbm) | copy-start | bytes 49156
  48.8 12.0 %copy-start.3 = (f32[8,512]{1,0:T(8,128)S(1)}, f32[8,512]{1,0:T(8,128)}, u32[]{:S(2)}) copy-start(f32[8,512]{1,0:T(8,128)} %get-tuple-element.33.later_hbm) | copy-start | bytes 49156
  65.5 7.9 %collective-permute-start.1 = (f32[2048,128]{1,0:T(8,128)}, f32[2048,128]{1,0:T(8,128)S(1)}, u32[]{:S(2)}, u32[]{:S(2)}) collective-permute-start(f32[2048,128]{1,0:T(8,128)} %shared_terms_0.1), channel_id=1, source_target_pairs={{0,1},{1,0},{2,3},{3,2},{4,5},{5,4},{6,7},{7,6},{8,9},{9,8},{10,11... | collective-permute-start | bytes 3145736 | tf_op jit(solution)/shard_map/ppermute | solution.py:587
  68.8 10.9 %copy-start.4 = (bf16[4,512]{1,0:T(4,128)(2,1)S(1)}, bf16[4,512]{1,0:T(4,128)(2,1)}, u32[]{:S(2)}) copy-start(bf16[4,512]{1,0:T(4,128)(2,1)} %weight_ref.1) | copy-start | bytes 12292
  73.4 6.3 %copy-start = (bf16[2048,128]{1,0:T(8,128)(2,1)S(1)}, bf16[2048,128]{1,0:T(8,128)(2,1)}, u32[]{:S(2)}) copy-start(bf16[2048,128]{1,0:T(8,128)(2,1)} %inject_hbm.7) | copy-start | bytes 1572868
  74.6 10.8 %collective-permute-start.2 = (bf16[512,128]{1,0:T(8,128)(2,1)S(1)}, bf16[512,128]{1,0:T(8,128)(2,1)S(1)}, u32[]{:S(2)}, u32[]{:S(2)}) collective-permute-start(bf16[512,128]{1,0:T(8,128)(2,1)S(1)} %get-tuple-element.57), channel_id=1, source_target_pairs={{0,2},{2,4},{4,6},{6,0},{1,3},{3,5},{5,7},{7,1},{8,10},{10,12},{12... | collective-permute-start | bytes 393224 | tf_op jit(solution)/shard_map/ppermute | solution.py:593
  76.0 9.4 %collective-permute-start.3 = (bf16[512,128]{1,0:T(8,128)(2,1)S(1)}, bf16[512,128]{1,0:T(8,128)(2,1)S(1)}, u32[]{:S(2)}, u32[]{:S(2)}) collective-permute-start(bf16[512,128]{1,0:T(8,128)(2,1)S(1)} %get-tuple-element.56), channel_id=1, source_target_pairs={{0,4},{2,6},{4,0},{6,2},{1,5},{3,7},{5,1},{7,3},{8,12},{10,14},{12... | collective-permute-start | bytes 393224 | tf_op jit(solution)/shard_map/ppermute | solution.py:593
  78.6 6.8 %collective-permute-start.4 = (bf16[512,128]{1,0:T(8,128)(2,1)S(1)}, bf16[512,128]{1,0:T(8,128)(2,1)S(1)}, u32[]{:S(2)}, u32[]{:S(2)}) collective-permute-start(bf16[512,128]{1,0:T(8,128)(2,1)S(1)} %get-tuple-element.55), channel_id=1, source_target_pairs={{0,6},{2,0},{4,2},{6,4},{1,7},{3,1},{5,3},{7,5},{8,14},{10,8},{12,... | collective-permute-start | bytes 393224 | tf_op jit(solution)/shard_map/ppermute | solution.py:593
  86.6 10.3 %collective-permute-start.5 = (bf16[512,128]{1,0:T(8,128)(2,1)S(1)}, bf16[512,128]{1,0:T(8,128)(2,1)S(1)}, u32[]{:S(2)}, u32[]{:S(2)}) collective-permute-start(bf16[512,128]{1,0:T(8,128)(2,1)S(1)} %get-tuple-element.54), channel_id=1, source_target_pairs={{0,2},{2,4},{4,6},{6,0},{1,3},{3,5},{5,7},{7,1},{8,10},{10,12},{12... | collective-permute-start | bytes 393224 | tf_op jit(solution)/shard_map/ppermute | solution.py:593
  87.0 9.8 %collective-permute-start.6 = (bf16[512,128]{1,0:T(8,128)(2,1)S(1)}, bf16[512,128]{1,0:T(8,128)(2,1)S(1)}, u32[]{:S(2)}, u32[]{:S(2)}) collective-permute-start(bf16[512,128]{1,0:T(8,128)(2,1)S(1)} %get-tuple-element.54), channel_id=1, source_target_pairs={{0,4},{2,6},{4,0},{6,2},{1,5},{3,7},{5,1},{7,3},{8,12},{10,14},{12... | collective-permute-start | bytes 393224 | tf_op jit(solution)/shard_map/ppermute | solution.py:593
  89.4 7.5 %collective-permute-start.7 = (bf16[512,128]{1,0:T(8,128)(2,1)S(1)}, bf16[512,128]{1,0:T(8,128)(2,1)S(1)}, u32[]{:S(2)}, u32[]{:S(2)}) collective-permute-start(bf16[512,128]{1,0:T(8,128)(2,1)S(1)} %get-tuple-element.54), channel_id=1, source_target_pairs={{0,6},{2,0},{4,2},{6,4},{1,7},{3,1},{5,3},{7,5},{8,14},{10,8},{12,... | collective-permute-start | bytes 393224 | tf_op jit(solution)/shard_map/ppermute | solution.py:593
  90.3 6.6 %collective-permute-start.8 = (f32[8,512]{1,0:T(8,128)S(1)}, f32[8,512]{1,0:T(8,128)S(1)}, u32[]{:S(2)}, u32[]{:S(2)}) collective-permute-start(f32[8,512]{1,0:T(8,128)S(1)} %get-tuple-element.48), channel_id=1, source_target_pairs={{8,0},{16,8},{24,16},{32,24},{40,32},{48,40},{56,48},{64,56},{72,6... | collective-permute-start | bytes 49160 | tf_op jit(solution)/shard_map/ppermute | solution.py:621
  97.0 4.8 %collective-permute-start.9 = (bf16[2048,128]{1,0:T(8,128)(2,1)S(1)}, bf16[2048,128]{1,0:T(8,128)(2,1)S(1)}, u32[]{:S(2)}, u32[]{:S(2)}) collective-permute-start(bf16[2048,128]{1,0:T(8,128)(2,1)S(1)} %constant_dynamic-update-slice_fusion), channel_id=1, source_target_pairs={{0,1},{1,0},{2,3},{3,2},{4,5},{5,4},{6,7},{7,6},{8,9},{9,8},{10,11... | collective-permute-start | bytes 1572872 | tf_op jit(solution)/shard_map/ppermute | solution.py:628

commit v8 on v7

--- a/solution.py
+++ b/solution.py
@@ -616,7 +616,7 @@
     quarter = cut(0)
     for piece in sent:
         quarter = quarter + piece.astype(f32)
-    quarter = quarter.astype(bf16)
+    quarter = lax.optimization_barrier(quarter.astype(bf16))
     turned = [turn(quarter, by) for by in range(1, ny)]
     next_rows = lax.ppermute(first, SEQ, down)
     *turned, next_rows = lax.optimization_barrier((*turned, next_rows))

time: 104 us -> 104 us (level)
    dynamic_update_slice x1 -> x0, other arithmetic: 1.06 us -> none  [body(): lax.dynamic_update_slice_in_dim(done, piece, lax.rem(here - by + ny, ny)...]
    convert_element_type x0 -> x1, other arithmetic: none -> 1.04 us  [body(): quarter = lax.optimization_barrier(quarter.astype(bf16))]
where the time goes in v8:
time: 104 us; the launch traced here: 103 us
  Pallas kernels  48.1 us (46%)
  starting transfers between devices  37.9 us (36%)
  waiting for transfers between devices  9.56 us (9%)
  other arithmetic  5.17 us (5%)
  local copies, waits for them, and re-layouts  1.51 us (1%)
    all_to_all x1, starting transfers between devices, body(): arrived = lax.all_to_all(payload, SEQ, 0, 0, tiled=True)  10.4 us
    pallas_call x1, Pallas kernels, body(): pl.pallas_call(local_shared_kernel, in_specs=[hbm] * 6 + [anywhere], out_...  9.61 us
    pallas_call x1, Pallas kernels, body(): pl.pallas_call(local_input_kernel, in_specs=[hbm] * 5 + [anywhere] * 3 +...  9.47 us
    pallas_call x2, Pallas kernels, shared(): pl.pallas_call(functools.partial(shared_kernel, turn), in_specs=[smem, pl...  9.25 us
    ppermute x6, starting transfers between devices, turn(): return lax.ppermute(array, 'y', [(i, (i + by) % ny) for i in range(ny)])  8.78 us
    pallas_call x1, Pallas kernels, body(): pl.pallas_call(states_kernel, in_specs=[hbm, anywhere, hbm, anywhere, hbm...  7.38 us
    all_to_all x1, starting transfers between devices, body(): returned = lax.all_to_all(scanned, SEQ, 0, 0, tiled=True)  6.27 us
    pallas_call x1, Pallas kernels, body(): pl.pallas_call(input_kernel, in_specs=[plain] + [hbm] * 3 + [plain], out_...  5.68 us
  transfers between devices with their start and end apart: 12, of which 4 were waited for; matrix products, arithmetic and copies ran while one was open for 1% of the time, Pallas kernels for 34%

profile of v8, /device:TPU:7, one launch (start us, length us, event | category | flops | bytes accessed | tf_op | source)
XLA Modules:
  0.0 103.1 jit_solution(1388474944926121455)
XLA Ops:
  0.6 0.7 slice.30
  1.4 3.4 %collective-permute-start = (bf16[16,512]{1,0:T(8,128)(2,1)S(1)}, bf16[16,512]{1,0:T(8,128)(2,1)S(1)}, u32[]{:S(2)}, u32[]{:S(2)}) collective-permute-start(bf16[16,512]{1,0:T(8,128)(2,1)S(1)} %slice.30), channel_id=1, source_target_pairs={{0,8},{8,16},{16,24},{24,32},{32,40},{40,48},{48,56},{56,64},{64,7... | collective-permute-start | bytes 49160 | tf_op jit(solution)/shard_map/ppermute | solution.py:491
  4.8 5.6 %own_grads.1 = (f32[8,512]{1,0:T(8,128)}, f32[8,512]{1,0:T(8,128)}, f32[8,512]{1,0:T(8,128)}, f32[1,512]{1,0:T(1,128)}, f32[128,512]{1,0:T(8,128)}, /*index=5*/f32[8,128,512]{2,1,0:T(8,128)}) custom-call(s32[8,8]{1,0:T(8,128)} %code_hbm.1, bf16[2048,512]{1,0:T(8,128)(2,1)} %grad_hbm.9, bf16[2048,128]{1,0:T(8,128)(2,1)} %read_hbm.5), custom_call_target="tpu_custom_call" | custom-call | flops 536870912 | bytes 3145728 | tf_op jit(solution)/shard_map/own_grads/pallas_call | solution.py:503
  10.4 0.6 copy-done.5
  11.0 7.4 %own_states.1 = (s16[32,16,384]{2,1,0:T(8,128)(2,1)}, f32[8,128,512]{2,1,0:T(8,128)}) custom-call(bf16[2048,512]{1,0:T(8,128)(2,1)} %x_hbm.3, bf16[16,512]{1,0:T(8,128)(2,1)} %copy-done.5, bf16[2048,128]{1,0:T(8,128)(2,1)} %inject_hbm.7, f32[8,512]{1,0:T(8,128)} %get-tuple-element.28.rate_hbm, bf16[4,512]{1,0:T(4,128)(2,1)} %weight_ref.1, ...), custom_call_target="tpu_custom_call" | custom-call | flops 536870912 | bytes 4194304 | tf_op jit(solution)/shard_map/own_states/pallas_call | solution.py:517
  18.4 10.4 %all-to-all-start = ((s16[32,16,384]{2,1,0:T(8,128)(2,1)}), s16[32,16,384]{2,1,0:T(8,128)(2,1)S(1)}, u32[]{:S(2)}, u32[]{:S(2)}) async-start(s16[32,16,384]{2,1,0:T(8,128)(2,1)} %get-tuple-element.31), calls=%async_computation | async-start | bytes 786432 | tf_op jit(solution)/shard_map/all_to_all | solution.py:532
  28.8 9.5 %local_input.1 = (bf16[2048,512]{1,0:T(8,128)(2,1)}, bf16[2048,512]{1,0:T(8,128)(2,1)}, bf16[2048,512]{1,0:T(8,128)(2,1)}) custom-call(bf16[2048,512]{1,0:T(8,128)(2,1)} %x_hbm.3, bf16[2048,512]{1,0:T(8,128)(2,1)} %grad_hbm.9, bf16[2048,128]{1,0:T(8,128)(2,1)} %inject_hbm.7, bf16[2048,128]{1,0:T(8,128)(2,1)} %read_hbm.5, ...), custom_call_target="tpu_custom_call" | custom-call | flops 2147483648 | bytes 13631488 | tf_op jit(solution)/shard_map/local_input/pallas_call | solution.py:534
  38.3 3.1 %all-to-all-done.own_ref = s16[32,16,384]{2,1,0:T(8,128)(2,1)S(1)} async-done(((s16[32,16,384]{2,1,0:T(8,128)(2,1)}), s16[32,16,384]{2,1,0:T(8,128)(2,1)S(1)}, u32[]{:S(2)}, u32[]{:S(2)}) %all-to-all-start) | async-done | bytes 393248 | tf_op jit(solution)/shard_map/all_to_all | solution.py:532
  41.3 1.1 %carry.1 = s16[32,16,384]{2,1,0:T(8,128)(2,1)} custom-call(s16[32,16,384]{2,1,0:T(8,128)(2,1)S(1)} %all-to-all-done.own_ref), custom_call_target="tpu_custom_call" | custom-call | flops 262144 | bytes 1048576 | tf_op jit(solution)/shard_map/carry/pallas_call | solution.py:560
  42.5 6.3 %all-to-all-start.1 = ((s16[32,16,384]{2,1,0:T(8,128)(2,1)}), s16[32,16,384]{2,1,0:T(8,128)(2,1)S(1)}, u32[]{:S(2)}, u32[]{:S(2)}) async-start(s16[32,16,384]{2,1,0:T(8,128)(2,1)} %carry.1), calls=%async_computation.1 | async-start | bytes 786432 | tf_op jit(solution)/shard_map/all_to_all | solution.py:568
  48.8 9.6 %local_shared.1 = (f32[2048,128]{1,0:T(8,128)}, f32[2048,128]{1,0:T(8,128)}) custom-call(bf16[2048,512]{1,0:T(8,128)(2,1)} %grad_hbm.9, bf16[2048,512]{1,0:T(8,128)(2,1)} %get-tuple-element.39.act_hbm, bf16[2048,128]{1,0:T(8,128)(2,1)} %inject_hbm.7, bf16[2048,128]{1,0:T(8,128)(2,1)} %read_hbm.5, f32[8,128,512]{2,1,0:T(8,128)} %get-tuple-element.32.after_hbm, ...), custom_call_target="tpu_custom_call" | custom-call | flops 3221225472 | bytes 9437184 | tf_op jit(solution)/shard_map/local_shared/pallas_call | solution.py:548
  58.4 2.4 %all-to-all-done.1.back_ref = s16[32,16,384]{2,1,0:T(8,128)(2,1)S(1)} async-done(((s16[32,16,384]{2,1,0:T(8,128)(2,1)}), s16[32,16,384]{2,1,0:T(8,128)(2,1)S(1)}, u32[]{:S(2)}, u32[]{:S(2)}) %all-to-all-start.1) | async-done | bytes 393248 | tf_op jit(solution)/shard_map/all_to_all | solution.py:568
  60.8 4.6 %shared_terms_0.1 = f32[2048,128]{1,0:T(8,128)} custom-call(s32[1]{0:T(128)} %bitcast.core_ref, s16[32,16,384]{2,1,0:T(8,128)(2,1)S(1)} %all-to-all-done.1.back_ref, bf16[2048,512]{1,0:T(8,128)(2,1)} %grad_hbm.9, bf16[2048,512]{1,0:T(8,128)(2,1)} %get-tuple-element.39.act_hbm, f32[2048,128]{1,0:T(8,128)} %get-tuple-element.41.gr_hbm, ...), custom_call_target="tpu_custom_call" | custom-call | flops 805306368 | bytes 4194304 | tf_op jit(solution)/shard_map/shared_terms_0/pallas_call | solution.py:574
  65.5 3.3 %collective-permute-start.1 = (f32[2048,128]{1,0:T(8,128)}, f32[2048,128]{1,0:T(8,128)S(1)}, u32[]{:S(2)}, u32[]{:S(2)}) collective-permute-start(f32[2048,128]{1,0:T(8,128)} %shared_terms_0.1), channel_id=1, source_target_pairs={{0,1},{1,0},{2,3},{3,2},{4,5},{5,4},{6,7},{7,6},{8,9},{9,8},{10,11... | collective-permute-start | bytes 3145736 | tf_op jit(solution)/shard_map/ppermute | solution.py:587
  68.8 4.6 %shared_terms_1.1 = f32[2048,128]{1,0:T(8,128)} custom-call(s32[1]{0:T(128)} %bitcast.core_ref, s16[32,16,384]{2,1,0:T(8,128)(2,1)S(1)} %all-to-all-done.1.back_ref, bf16[2048,512]{1,0:T(8,128)(2,1)} %grad_hbm.9, bf16[2048,512]{1,0:T(8,128)(2,1)} %get-tuple-element.39.act_hbm, f32[2048,128]{1,0:T(8,128)} %get-tuple-element.41.gr_hbm, ...), custom_call_target="tpu_custom_call" | custom-call | flops 805306368 | bytes 4194304 | tf_op jit(solution)/shard_map/shared_terms_1/pallas_call | solution.py:574
  73.4 0.0 copy-start
  73.4 1.3 %add_convert_fusion.1 = (bf16[512,128]{1,0:T(8,128)(2,1)S(1)}, bf16[512,128]{1,0:T(8,128)(2,1)S(1)}, bf16[512,128]{1,0:T(8,128)(2,1)S(1)}) fusion(f32[2048,128]{1,0:T(8,128)S(1)} %collective-permute-done.1, s32[]{:T(128)S(6)} %select_n.37, f32[2048,128]{1,0:T(8,128)} %shared_terms_1.1, s32[]{:T(128)S(6)} %select_n.36, s32[]{:T(128)S(6)} %select_n.35), kind=kLoop, calls=%fused_computation.3 | loop fusion | flops 393216 | bytes 1966092 | tf_op jit(solution)/shard_map/convert_element_type | solution.py:599
  74.6 1.4 %collective-permute-start.2 = (bf16[512,128]{1,0:T(8,128)(2,1)S(1)}, bf16[512,128]{1,0:T(8,128)(2,1)S(1)}, u32[]{:S(2)}, u32[]{:S(2)}) collective-permute-start(bf16[512,128]{1,0:T(8,128)(2,1)S(1)} %get-tuple-element.55), channel_id=1, source_target_pairs={{0,2},{2,4},{4,6},{6,0},{1,3},{3,5},{5,7},{7,1},{8,10},{10,12},{12... | collective-permute-start | bytes 393224 | tf_op jit(solution)/shard_map/ppermute | solution.py:593
  76.0 2.6 %collective-permute-start.3 = (bf16[512,128]{1,0:T(8,128)(2,1)S(1)}, bf16[512,128]{1,0:T(8,128)(2,1)S(1)}, u32[]{:S(2)}, u32[]{:S(2)}) collective-permute-start(bf16[512,128]{1,0:T(8,128)(2,1)S(1)} %get-tuple-element.54), channel_id=1, source_target_pairs={{0,4},{2,6},{4,0},{6,2},{1,5},{3,7},{5,1},{7,3},{8,12},{10,14},{12... | collective-permute-start | bytes 393224 | tf_op jit(solution)/shard_map/ppermute | solution.py:593
  78.6 1.1 %collective-permute-start.4 = (bf16[512,128]{1,0:T(8,128)(2,1)S(1)}, bf16[512,128]{1,0:T(8,128)(2,1)S(1)}, u32[]{:S(2)}, u32[]{:S(2)}) collective-permute-start(bf16[512,128]{1,0:T(8,128)(2,1)S(1)} %get-tuple-element.53), channel_id=1, source_target_pairs={{0,6},{2,0},{4,2},{6,4},{1,7},{3,1},{5,3},{7,5},{8,14},{10,8},{12,... | collective-permute-start | bytes 393224 | tf_op jit(solution)/shard_map/ppermute | solution.py:593
  79.7 5.7 %input_grads.1 = (f32[2048,512]{1,0:T(8,128)}, f32[8,512]{1,0:T(8,128)S(1)}) custom-call(s16[32,16,384]{2,1,0:T(8,128)(2,1)S(1)} %all-to-all-done.1.back_ref, bf16[2048,512]{1,0:T(8,128)(2,1)} %get-tuple-element.36.pre_hbm, bf16[2048,512]{1,0:T(8,128)(2,1)} %get-tuple-element.37.factor_hbm, bf16[2048,128]{1,0:T(8,128)(2,1)S(1)} %copy-done, ...), custom_call_target="tpu_custom_call" | custom-call | flops 536870912 | bytes 13631488 | tf_op jit(solution)/shard_map/input_grads/pallas_call | solution.py:601
  85.4 1.0 %add_convert_fusion = bf16[512,128]{1,0:T(8,128)(2,1)S(1)} fusion(bf16[512,128]{1,0:T(8,128)(2,1)S(1)} %collective-permute-done.4, bf16[512,128]{1,0:T(8,128)(2,1)S(1)} %collective-permute-done.3, bf16[512,128]{1,0:T(8,128)(2,1)S(1)} %collective-permute-done.2, f32[2048,128]{1,0:T(8,128)S(1)} %collective-permute-done.1, s32[]{:T(128)S(6)} %select_n.34, ...), kind=kLoop, calls=%fused_computation.2 | loop fusion | flops 524288 | bytes 1048580 | tf_op jit(solution)/shard_map/convert_element_type | solution.py:619
  86.5 0.5 collective-permute-start.5
  86.9 2.3 %collective-permute-start.6 = (bf16[512,128]{1,0:T(8,128)(2,1)S(1)}, bf16[512,128]{1,0:T(8,128)(2,1)S(1)}, u32[]{:S(2)}, u32[]{:S(2)}) collective-permute-start(bf16[512,128]{1,0:T(8,128)(2,1)S(1)} %add_convert_fusion), channel_id=1, source_target_pairs={{0,4},{2,6},{4,0},{6,2},{1,5},{3,7},{5,1},{7,3},{8,12},{10,14},{12... | collective-permute-start | bytes 393224 | tf_op jit(solution)/shard_map/ppermute | solution.py:593
  89.3 0.9 collective-permute-start.7
  90.2 2.5 %collective-permute-start.8 = (f32[8,512]{1,0:T(8,128)S(1)}, f32[8,512]{1,0:T(8,128)S(1)}, u32[]{:S(2)}, u32[]{:S(2)}) collective-permute-start(f32[8,512]{1,0:T(8,128)S(1)} %get-tuple-element.48), channel_id=1, source_target_pairs={{8,0},{16,8},{24,16},{32,24},{40,32},{48,40},{56,48},{64,56},{72,6... | collective-permute-start | bytes 49160 | tf_op jit(solution)/shard_map/ppermute | solution.py:621
  92.7 0.1 broadcast_in_dim.7
  92.8 4.0 %collective-permute-done.8 = f32[8,512]{1,0:T(8,128)S(1)} collective-permute-done((f32[8,512]{1,0:T(8,128)S(1)}, f32[8,512]{1,0:T(8,128)S(1)}, u32[]{:S(2)}, u32[]{:S(2)}) %collective-permute-start.8) | collective-permute-done | bytes 16416 | tf_op jit(solution)/shard_map/ppermute | solution.py:621
  96.9 3.2 %collective-permute-start.9 = (bf16[2048,128]{1,0:T(8,128)(2,1)S(1)}, bf16[2048,128]{1,0:T(8,128)(2,1)S(1)}, u32[]{:S(2)}, u32[]{:S(2)}) collective-permute-start(bf16[2048,128]{1,0:T(8,128)(2,1)S(1)} %constant_dynamic-update-slice_fusion), channel_id=1, source_target_pairs={{0,1},{1,0},{2,3},{3,2},{4,5},{5,4},{6,7},{7,6},{8,9},{9,8},{10,11... | collective-permute-start | bytes 1572872 | tf_op jit(solution)/shard_map/ppermute | solution.py:628
  100.2 1.4 %fusion = f32[2048,512]{1,0:T(8,128)} fusion(f32[2048,512]{1,0:T(8,128)} %get-tuple-element.38, f32[1,512]{1,0:T(1,128)S(1)} %get-tuple-element.59, f32[1,512]{1,0:T(1,128)S(1)} %get-tuple-element.60, f32[1,512]{1,0:T(1,128)S(1)} %get-tuple-element.58, f32[8]{0:T(128)S(1)} %pad.clone), kind=kLoop, calls=%fused_computation.7 | loop fusion | flops 16384 | bytes 38944 | tf_op jit(solution)/shard_map/dynamic_update_slice | solution.py:639
  101.6 0.1 collective-permute-done.9
  101.7 1.5 %select_convert_fusion = (f32[2048,128]{1,0:T(8,128)}, f32[2048,128]{1,0:T(8,128)}) fusion(bf16[2048,128]{1,0:T(8,128)(2,1)S(1)} %collective-permute-done.9, bf16[2048,128]{1,0:T(8,128)(2,1)S(1)} %constant_dynamic-update-slice_fusion, pred[]{:T(512)S(6)} %eq.3), kind=kLoop, calls=%fused_computation | loop fusion | flops 1048576 | bytes 3145729 | tf_op jit(solution)/shard_map/convert_element_type | solution.py:631
  (26 shorter events, 0.2 us)
Async XLA Ops:
  1.4 9.1 %collective-permute-start = (bf16[16,512]{1,0:T(8,128)(2,1)S(1)}, bf16[16,512]{1,0:T(8,128)(2,1)S(1)}, u32[]{:S(2)}, u32[]{:S(2)}) collective-permute-start(bf16[16,512]{1,0:T(8,128)(2,1)S(1)} %slice.30), channel_id=1, source_target_pairs={{0,8},{8,16},{16,24},{24,32},{32,40},{40,48},{48,56},{56,64},{64,7... | collective-permute-start | bytes 49160 | tf_op jit(solution)/shard_map/ppermute | solution.py:491
  10.4 0.6 copy-start.5
  18.4 22.9 %all-to-all-start = ((s16[32,16,384]{2,1,0:T(8,128)(2,1)}), s16[32,16,384]{2,1,0:T(8,128)(2,1)S(1)}, u32[]{:S(2)}, u32[]{:S(2)}) async-start(s16[32,16,384]{2,1,0:T(8,128)(2,1)} %get-tuple-element.31), calls=%async_computation | async-start | bytes 786432 | tf_op jit(solution)/shard_map/all_to_all | solution.py:532
  42.5 18.3 %all-to-all-start.1 = ((s16[32,16,384]{2,1,0:T(8,128)(2,1)}), s16[32,16,384]{2,1,0:T(8,128)(2,1)S(1)}, u32[]{:S(2)}, u32[]{:S(2)}) async-start(s16[32,16,384]{2,1,0:T(8,128)(2,1)} %carry.1), calls=%async_computation.1 | async-start | bytes 786432 | tf_op jit(solution)/shard_map/all_to_all | solution.py:568
  48.8 12.0 %copy-start.1 = (f32[8,512]{1,0:T(8,128)S(1)}, f32[8,512]{1,0:T(8,128)}, u32[]{:S(2)}) copy-start(f32[8,512]{1,0:T(8,128)} %get-tuple-element.28.rate_hbm) | copy-start | bytes 49156
  48.8 12.0 %copy-start.2 = (f32[8,512]{1,0:T(8,128)S(1)}, f32[8,512]{1,0:T(8,128)}, u32[]{:S(2)}) copy-start(f32[8,512]{1,0:T(8,128)} %get-tuple-element.43.prior_hbm) | copy-start | bytes 49156
  48.8 12.0 %copy-start.3 = (f32[8,512]{1,0:T(8,128)S(1)}, f32[8,512]{1,0:T(8,128)}, u32[]{:S(2)}) copy-start(f32[8,512]{1,0:T(8,128)} %get-tuple-element.33.later_hbm) | copy-start | bytes 49156
  65.5 7.9 %collective-permute-start.1 = (f32[2048,128]{1,0:T(8,128)}, f32[2048,128]{1,0:T(8,128)S(1)}, u32[]{:S(2)}, u32[]{:S(2)}) collective-permute-start(f32[2048,128]{1,0:T(8,128)} %shared_terms_0.1), channel_id=1, source_target_pairs={{0,1},{1,0},{2,3},{3,2},{4,5},{5,4},{6,7},{7,6},{8,9},{9,8},{10,11... | collective-permute-start | bytes 3145736 | tf_op jit(solution)/shard_map/ppermute | solution.py:587
  68.7 11.0 %copy-start.4 = (bf16[4,512]{1,0:T(4,128)(2,1)S(1)}, bf16[4,512]{1,0:T(4,128)(2,1)}, u32[]{:S(2)}) copy-start(bf16[4,512]{1,0:T(4,128)(2,1)} %weight_ref.1) | copy-start | bytes 12292
  73.4 6.3 %copy-start = (bf16[2048,128]{1,0:T(8,128)(2,1)S(1)}, bf16[2048,128]{1,0:T(8,128)(2,1)}, u32[]{:S(2)}) copy-start(bf16[2048,128]{1,0:T(8,128)(2,1)} %inject_hbm.7) | copy-start | bytes 1572868
  74.6 10.8 %collective-permute-start.2 = (bf16[512,128]{1,0:T(8,128)(2,1)S(1)}, bf16[512,128]{1,0:T(8,128)(2,1)S(1)}, u32[]{:S(2)}, u32[]{:S(2)}) collective-permute-start(bf16[512,128]{1,0:T(8,128)(2,1)S(1)} %get-tuple-element.55), channel_id=1, source_target_pairs={{0,2},{2,4},{4,6},{6,0},{1,3},{3,5},{5,7},{7,1},{8,10},{10,12},{12... | collective-permute-start | bytes 393224 | tf_op jit(solution)/shard_map/ppermute | solution.py:593
  76.0 9.4 %collective-permute-start.3 = (bf16[512,128]{1,0:T(8,128)(2,1)S(1)}, bf16[512,128]{1,0:T(8,128)(2,1)S(1)}, u32[]{:S(2)}, u32[]{:S(2)}) collective-permute-start(bf16[512,128]{1,0:T(8,128)(2,1)S(1)} %get-tuple-element.54), channel_id=1, source_target_pairs={{0,4},{2,6},{4,0},{6,2},{1,5},{3,7},{5,1},{7,3},{8,12},{10,14},{12... | collective-permute-start | bytes 393224 | tf_op jit(solution)/shard_map/ppermute | solution.py:593
  78.6 6.8 %collective-permute-start.4 = (bf16[512,128]{1,0:T(8,128)(2,1)S(1)}, bf16[512,128]{1,0:T(8,128)(2,1)S(1)}, u32[]{:S(2)}, u32[]{:S(2)}) collective-permute-start(bf16[512,128]{1,0:T(8,128)(2,1)S(1)} %get-tuple-element.53), channel_id=1, source_target_pairs={{0,6},{2,0},{4,2},{6,4},{1,7},{3,1},{5,3},{7,5},{8,14},{10,8},{12,... | collective-permute-start | bytes 393224 | tf_op jit(solution)/shard_map/ppermute | solution.py:593
  86.5 10.3 %collective-permute-start.5 = (bf16[512,128]{1,0:T(8,128)(2,1)S(1)}, bf16[512,128]{1,0:T(8,128)(2,1)S(1)}, u32[]{:S(2)}, u32[]{:S(2)}) collective-permute-start(bf16[512,128]{1,0:T(8,128)(2,1)S(1)} %add_convert_fusion), channel_id=1, source_target_pairs={{0,2},{2,4},{4,6},{6,0},{1,3},{3,5},{5,7},{7,1},{8,10},{10,12},{12... | collective-permute-start | bytes 393224 | tf_op jit(solution)/shard_map/ppermute | solution.py:593
  86.9 9.8 %collective-permute-start.6 = (bf16[512,128]{1,0:T(8,128)(2,1)S(1)}, bf16[512,128]{1,0:T(8,128)(2,1)S(1)}, u32[]{:S(2)}, u32[]{:S(2)}) collective-permute-start(bf16[512,128]{1,0:T(8,128)(2,1)S(1)} %add_convert_fusion), channel_id=1, source_target_pairs={{0,4},{2,6},{4,0},{6,2},{1,5},{3,7},{5,1},{7,3},{8,12},{10,14},{12... | collective-permute-start | bytes 393224 | tf_op jit(solution)/shard_map/ppermute | solution.py:593
  89.3 7.5 %collective-permute-start.7 = (bf16[512,128]{1,0:T(8,128)(2,1)S(1)}, bf16[512,128]{1,0:T(8,128)(2,1)S(1)}, u32[]{:S(2)}, u32[]{:S(2)}) collective-permute-start(bf16[512,128]{1,0:T(8,128)(2,1)S(1)} %add_convert_fusion), channel_id=1, source_target_pairs={{0,6},{2,0},{4,2},{6,4},{1,7},{3,1},{5,3},{7,5},{8,14},{10,8},{12,... | collective-permute-start | bytes 393224 | tf_op jit(solution)/shard_map/ppermute | solution.py:593
  90.2 6.6 %collective-permute-start.8 = (f32[8,512]{1,0:T(8,128)S(1)}, f32[8,512]{1,0:T(8,128)S(1)}, u32[]{:S(2)}, u32[]{:S(2)}) collective-permute-start(f32[8,512]{1,0:T(8,128)S(1)} %get-tuple-element.48), channel_id=1, source_target_pairs={{8,0},{16,8},{24,16},{32,24},{40,32},{48,40},{56,48},{64,56},{72,6... | collective-permute-start | bytes 49160 | tf_op jit(solution)/shard_map/ppermute | solution.py:621
  96.9 4.8 %collective-permute-start.9 = (bf16[2048,128]{1,0:T(8,128)(2,1)S(1)}, bf16[2048,128]{1,0:T(8,128)(2,1)S(1)}, u32[]{:S(2)}, u32[]{:S(2)}) collective-permute-start(bf16[2048,128]{1,0:T(8,128)(2,1)S(1)} %constant_dynamic-update-slice_fusion), channel_id=1, source_target_pairs={{0,1},{1,0},{2,3},{3,2},{4,5},{5,4},{6,7},{7,6},{8,9},{9,8},{10,11... | collective-permute-start | bytes 1572872 | tf_op jit(solution)/shard_map/ppermute | solution.py:628
